TPU v7x, 128 devices: a whole 4x4x4 slice. The times are simulated.
128 devices in a mesh: replica: 32 (over z, y, core), shard: 4 (over x).
Axes of the slice: x: 4, y: 4, z: 4, core: 2. Of those that a mesh axis runs over, the one named last changes fastest.
Arguments:
- acts: bfloat16 [2, 65536, 1280], P(None, 'replica', 'shard'), may hold values from -6 to 6
- cots: bfloat16 [2, 65536, 1280], P(None, 'replica'), may hold values from -6 to 6
- errors: float32 [32, 2, 1280, 1280], P('replica', None, 'shard'), may hold values from -4 to 4
- weights: float32 [2, 1280, 1280], P(None, 'shard'), may hold values from -0.3 to 0.3
- momentum: float32 [2, 1280, 1280], P(None, 'shard'), may hold values from -3 to 3
- start_q: float32 [2, 1280, 32], replicated, may hold values from -6 to 6
- vec_grads: float32 [32, 4, 1280], P('replica', None, 'shard'), may hold values from -6 to 6
- vec_weights: float32 [4, 1280], P(None, 'shard'), may hold values from 0.5 to 1.5
- vec_momentum: float32 [4, 1280], P(None, 'shard'), may hold values from -6 to 6
Outputs:
- new_errors: float32 [32, 2, 1280, 1280], P('replica', None, 'shard')
- new_weights: float32 [2, 1280, 1280], P(None, 'shard')
- new_momentum: float32 [2, 1280, 1280], P(None, 'shard')
- new_vec_weights: float32 [4, 1280], P(None, 'shard')
- new_vec_momentum: float32 [4, 1280], P(None, 'shard')
All inputs are finite; a program needn't handle non-finite values.
Results may differ from a plain program's by a relative error of at most 0.0003.
Values sent between devices are 32-bit elements; how exact they have to be, the bound alone decides.
No kernel may reach another device: no remote copies, remote signals or barrier semaphores. Data moves between devices by JAX's collectives and lax.ppermute only.
A program may use at most 128 MiB of HBM per device.

v0:
```python
import math

import jax
import jax.numpy as jnp
from jax import lax
from jax.sharding import PartitionSpec as P

HIGH = lax.Precision.HIGHEST


def finish(block, gram):
    lower = jnp.linalg.cholesky(gram)
    return lax.linalg.triangular_solve(lower, block, left_side=False, lower=True, transpose_a=True)


def orth_local(block):
    gram = jnp.einsum("mdk,mdl->mkl", block, block, precision=HIGH)
    return finish(block, gram)


def orth_rows(block):
    gram = jnp.einsum("mdk,mdl->mkl", block, block, precision=HIGH)
    gram = lax.psum(gram, "shard")
    return finish(block, gram)


def project_rows(full, right):
    return jnp.einsum("mde,mek->mdk", full, right, precision=HIGH)


def reduce_right(full, left):
    terms = jnp.einsum("mde,mdk->mek", full, left, precision=HIGH)
    return lax.psum(terms, ("replica", "shard"))


def body(acts, cots, errors, weights, momentum, start_q, vec_grads, vec_weights, vec_momentum):
    tok_rows = acts.shape[1]
    replicas = float(lax.axis_size("replica"))
    grads = jnp.einsum("mtd,mte->mde", acts, cots, preferred_element_type=jnp.float32)
    full = grads * (1.0 / math.sqrt(tok_rows)) + errors[0]
    local_left = project_rows(full, start_q)
    vec_total = lax.psum(vec_grads[0], "replica")
    left_sum = lax.psum(local_left, "replica")
    left = orth_rows(left_sum)
    right = reduce_right(full, left)
    right_hat = orth_local(right)
    left_sum = lax.psum(project_rows(full, right_hat), "replica")
    left = orth_rows(left_sum)
    right = reduce_right(full, left)
    approx = jnp.einsum("mdk,mek->mde", left, right, precision=HIGH) / replicas
    new_errors = (full - approx)[None]
    new_momentum = 0.9 * momentum + approx
    new_weights = weights - 0.1 * new_momentum
    vec_moved = 0.9 * vec_momentum + vec_total / replicas
    return (new_errors, new_weights, new_momentum, vec_weights - 0.1 * vec_moved, vec_moved)


def solution(mesh):
    placed = (
        P(None, "replica", "shard"),
        P(None, "replica", None),
        P("replica", None, "shard", None),
        P(None, "shard", None),
        P(None, "shard", None),
        P(),
        P("replica", None, "shard"),
        P(None, "shard"),
        P(None, "shard"),
    )
    return jax.shard_map(
        body,
        mesh=mesh,
        in_specs=placed,
        out_specs=(
            P("replica", None, "shard", None),
            P(None, "shard", None),
            P(None, "shard", None),
            P(None, "shard"),
            P(None, "shard"),
        ),
        check_vma=False,
    )
```

profile of v0, /device:TPU:1, one launch (start us, length us, event | category | flops | bytes accessed | tf_op | source)
XLA Modules:
  0.0 609.8 jit_solution(3013208280082749145)
XLA Ops:
  7.2 1.7 copy-done
  8.9 8.5 %fusion = f32[2,320,1280]{2,1,0:T(8,128)S(1)} fusion(bf16[2,2048,320]{1,2,0:T(8,128)(2,1)S(1)} %copy-done, bf16[2,2048,1280]{2,1,0:T(8,128)(2,1)} %param.13, f32[1,2,320,1280]{3,2,1,0:T(8,128)} %param.14), kind=kOutput, calls=%fused_computation.2 | convolution fusion | flops 3357081600 | bytes 19660800 | tf_op jit(solution)/shard_map/mtd,mte->mde/dot_general | solution.py:39
  17.4 1.7 copy-done.1
  19.1 3.5 fusion.9
  22.7 101.0 %all-reduce.5.cloned.1.call-done = f32[2,320,32]{1,2,0:T(8,128)} async-done(((f32[2,320,32]{1,2,0:T(8,128)}), f32[2,320,32]{1,2,0:T(8,128)}) %all-reduce.5.cloned.1.call-update) | async-done | bytes 81936 | tf_op jit(solution)/shard_map/psum | solution.py:43
  124.9 13.2 %psum.50 = f32[2,32,32]{1,2,0:T(8,128)S(1)} all-reduce(f32[2,32,32]{1,2,0:T(8,128)S(1)} %fusion.10), channel_id=1, replica_groups=mesh['replica'=32,'shard'=4] {'shard'}, use_global_device_ids=true, to_apply=%region_1.0 | all-reduce | flops 2048 | bytes 16384 | tf_op jit(solution)/shard_map/psum | solution.py:23
  138.2 5.9 custom-call.13
  144.3 4.9 custom-call.14
  150.5 4.6 fusion.11
  155.4 144.9 %all-reduce.7.cloned.1.call-done = f32[2,1280,32]{1,2,0:T(8,128)} async-done(((f32[2,1280,32]{1,2,0:T(8,128)}), f32[2,1280,32]{1,2,0:T(8,128)}) %all-reduce.7.cloned.1.call-update) | async-done | bytes 327696 | tf_op jit(solution)/shard_map/psum | solution.py:33
  300.3 1.5 fusion.12
  301.9 5.9 custom-call.15
  308.0 4.9 custom-call.9
  312.9 1.5 fusion.3
  314.4 5.4 fusion.13
  319.9 62.7 %psum.55 = f32[4,320]{1,0:T(4,128)S(1)} all-reduce(f32[4,320]{1,0:T(4,128)S(1)} %bitcast.57), channel_id=1, replica_groups=mesh['replica'=32,'shard'=4] {'replica'}, use_global_device_ids=true, to_apply=%region_8.11 | all-reduce | flops 1280 | bytes 10240 | tf_op jit(solution)/shard_map/psum | solution.py:42
  382.6 32.9 %all-reduce.9.cloned.1.call-done = f32[2,320,32]{1,2,0:T(8,128)} async-done(((f32[2,320,32]{1,2,0:T(8,128)}), f32[2,320,32]{1,2,0:T(8,128)}) %all-reduce.9.cloned.1.call-update) | async-done | bytes 81936 | tf_op jit(solution)/shard_map/psum | solution.py:47
  416.7 13.2 %psum.53 = f32[2,32,32]{1,2,0:T(8,128)S(1)} all-reduce(f32[2,32,32]{1,2,0:T(8,128)S(1)} %fusion.14), channel_id=1, replica_groups=mesh['replica'=32,'shard'=4] {'shard'}, use_global_device_ids=true, to_apply=%region_6.9 | all-reduce | flops 2048 | bytes 16384 | tf_op jit(solution)/shard_map/psum | solution.py:23
  430.1 5.9 custom-call.16
  436.2 4.9 custom-call.17
  441.1 1.2 convolution_bitcast_fusion
  442.3 4.6 fusion.15
  447.6 144.5 %all-reduce.11.cloned.1.call-done = f32[2,1280,32]{1,2,0:T(8,128)} async-done(((f32[2,1280,32]{1,2,0:T(8,128)}), f32[2,1280,32]{1,2,0:T(8,128)}) %all-reduce.11.cloned.1.call-update) | async-done | bytes 327696 | tf_op jit(solution)/shard_map/psum | solution.py:33
  592.0 11.3 %multiply_subtract_fusion = (f32[2,320,1280]{2,1,0:T(8,128)}, f32[2,320,1280]{2,1,0:T(8,128)}, f32[1,2,320,1280]{3,2,1,0:T(8,128)}) fusion(f32[2,320,1280]{2,1,0:T(8,128)} %param.15, f32[2,320,1280]{2,1,0:T(8,128)} %param.16, f32[2,320,1280]{2,1,0:T(8,128)} %copy-done.1, f32[2,320,32]{1,2,0:T(8,128)S(1)} %convolution_bitcast_fusion, ...), kind=kOutput, calls=%fused_computation.3 | convolution fusion | flops 319488000 | bytes 20070400 | tf_op jit(solution)/shard_map/mdk,mek->mde/dot_general | solution.py:50
  (39 shorter events, 5.6 us)
Async XLA Ops:
  7.2 1.7 copy-start
  7.2 11.9 %copy-start.2 = (f32[2,1280,32]{1,2,0:T(8,128)S(1)}, f32[2,1280,32]{1,2,0:T(8,128)}, u32[]{:S(2)}) copy-start(f32[2,1280,32]{1,2,0:T(8,128)} %param.17) | copy-start | bytes 983044
  7.2 116.5 %all-reduce.5.cloned.1.call-start = ((), (), s32[]{:S(2)}) async-start(), calls=%async_computation | async-start | bytes 196608 | tf_op jit(solution)/shard_map/psum | solution.py:43
  17.4 1.7 copy-start.1
  22.7 277.6 %all-reduce.7.cloned.1.call-start = ((), (), s32[]{:S(2)}) async-start(), calls=%async_computation.1 | async-start | bytes 655360 | tf_op jit(solution)/shard_map/psum | solution.py:33
  155.1 164.8 %copy-start.3 = (f32[1,4,320]{2,1,0:T(4,128)S(1)}, f32[1,4,320]{2,1,0:T(4,128)}, u32[]{:S(2)}) copy-start(f32[1,4,320]{2,1,0:T(4,128)} %param.18) | copy-start | bytes 15364
  155.1 260.4 %all-reduce.9.cloned.1.call-start = ((), (), s32[]{:S(2)}) async-start(), calls=%async_computation.2 | async-start | bytes 196608 | tf_op jit(solution)/shard_map/psum | solution.py:47
  319.8 127.1 %copy-start.4 = (f32[4,320]{1,0:T(4,128)S(1)}, f32[4,320]{1,0:T(4,128)}, u32[]{:S(2)}) copy-start(f32[4,320]{1,0:T(4,128)} %param.19) | copy-start | bytes 15364
  319.8 127.2 %copy-start.5 = (f32[4,320]{1,0:T(4,128)S(1)}, f32[4,320]{1,0:T(4,128)}, u32[]{:S(2)}) copy-start(f32[4,320]{1,0:T(4,128)} %param.20) | copy-start | bytes 15364
  319.8 272.2 %all-reduce.11.cloned.1.call-start = ((), (), s32[]{:S(2)}) async-start(), calls=%async_computation.3 | async-start | bytes 655360 | tf_op jit(solution)/shard_map/psum | solution.py:33
Sparse Core Ops, SparseCore 0:
  22.8 100.8 all-reduce.4
  155.2 144.9 all-reduce.6
  319.9 95.5 all-reduce.8
  447.1 144.9 all-reduce.10
where the time goes:
time: 610 us
  waiting for transfers between devices  423 us (69%)
  blocking collectives  89.2 us (15%)
  matrix products  45.7 us (7%)
  other arithmetic  33.7 us (6%)
  between operations  13.9 us (2%)
    psum x2, waiting for transfers between devices, reduce_right(): return lax.psum(terms, ('replica', 'shard'))  289 us
    psum x1, waiting for transfers between devices, body(): left_sum = lax.psum(local_left, 'replica')  101 us
    psum x1, blocking collectives, body(): vec_total = lax.psum(vec_grads[0], 'replica')  62.7 us
    psum x1, waiting for transfers between devices, body(): left_sum = lax.psum(project_rows(full, right_hat), 'replica')  32.9 us
    psum x2, blocking collectives, orth_rows(): gram = lax.psum(gram, 'shard')  26.5 us
    another operation x10, other arithmetic, finish(): lower = jnp.linalg.cholesky(gram)  18.1 us
    another operation x7, other arithmetic, finish(): lax.linalg.triangular_solve(lower, block, left_side=False, lower=True, tr...  15 us
  transfers between devices with their start and end apart: 4, of which 4 were waited for; matrix products, arithmetic and copies ran while one was open for 0% of the time, Pallas kernels for 0%

commit v1 on v0

v1 whole, which is shorter than its diff:
```python
import math

import jax
import jax.numpy as jnp
from jax import lax
from jax.sharding import PartitionSpec as P

HIGH = lax.Precision.HIGHEST

CORE = [(r, r ^ 1) for r in range(32)]


def y_pairs(k):
    return [(r, r ^ (k << 1)) for r in range(32)]


def z_pairs(k):
    return [(r, r ^ (k << 3)) for r in range(32)]


X_PAIRS = [None] + [[(s, s ^ k) for s in range(4)] for k in (1, 2, 3)]


def swap_y(value, k):
    return lax.ppermute(value, "replica", y_pairs(k))


def swap_z(value, k):
    return lax.ppermute(value, "replica", z_pairs(k))


def swap_x(value, k):
    return lax.ppermute(value, "shard", X_PAIRS[k])


def sum4(value, swap):
    one, two, three = (swap(value, k) for k in (1, 2, 3))
    return (value + one) + (two + three)


def inv_lower(gram):
    lower = jnp.linalg.cholesky(gram)
    eye = jnp.eye(gram.shape[0], dtype=gram.dtype)
    return lax.linalg.triangular_solve(lower, eye, left_side=True, lower=True)


def mm(spec, a, b):
    return jnp.einsum(spec, a, b, precision=HIGH)


def body(acts, cots, errors, weights, momentum, start_q, vec_grads, vec_weights, vec_momentum):
    tok_rows = acts.shape[1]
    rows = acts.shape[2]
    replicas = float(lax.axis_size("replica"))
    index = lax.axis_index("replica")
    core = index & 1
    y = (index >> 1) & 3
    grads = jnp.einsum("mtd,mte->mde", acts, cots, preferred_element_type=jnp.float32)
    full = grads * (1.0 / math.sqrt(tok_rows)) + errors[0]
    own = lax.dynamic_index_in_dim(full, core, 0, False)
    other = lax.dynamic_index_in_dim(full, 1 - core, 0, False)
    both = own + lax.ppermute(other, "replica", CORE)
    parts = both.reshape(rows, 4, -1).transpose(1, 2, 0)
    take = lambda k: lax.dynamic_index_in_dim(parts, y ^ k, 0, False)
    mine = (take(0) + swap_y(take(1), 1)) + (swap_y(take(2), 2) + swap_y(take(3), 3))
    wide = sum4(mine, swap_z)

    q0 = lax.dynamic_index_in_dim(start_q, core, 0, False)
    p1 = sum4(sum4(mm("de,ek->kd", both, q0), swap_y), swap_z)
    vec = sum4(vec_grads[0] + lax.ppermute(vec_grads[0], "replica", CORE), swap_y)
    vec_total = sum4(vec, swap_z)

    packed = jnp.concatenate([mm("ed,kd->ke", wide, p1), mm("kd,ld->kl", p1, p1)], axis=1)
    packed = sum4(packed, swap_x)
    cols = wide.shape[0]
    q1 = mm("lk,ke->le", inv_lower(packed[:, cols:]), packed[:, :cols])

    packed = jnp.concatenate([mm("ke,ed->kd", q1, wide), mm("ke,le->kl", q1, q1)], axis=1)
    packed = sum4(packed, swap_y)
    p2 = mm("lk,kd->ld", inv_lower(packed[:, rows:]), packed[:, :rows])

    packed = jnp.concatenate([mm("ed,kd->ke", wide, p2), mm("kd,ld->kl", p2, p2)], axis=1)
    packed = sum4(packed, swap_x)
    inv = inv_lower(packed[:, cols:])
    left = mm("lk,kd->ld", inv, p2)
    q2 = mm("lk,ke->le", inv, packed[:, :cols])
    quarters = jnp.stack([q2] + [swap_y(q2, k) for k in (1, 2, 3)])
    right = jnp.concatenate([lax.dynamic_index_in_dim(quarters, y ^ k, 0, False) for k in range(4)], axis=1)
    mine = jnp.concatenate([left, right], axis=1)
    theirs = lax.ppermute(mine, "replica", CORE)
    low = jnp.where(core == 0, mine, theirs)
    high = jnp.where(core == 0, theirs, mine)
    pair = jnp.stack([low, high])
    approx = mm("mkd,mke->mde", pair[:, :, :rows], pair[:, :, rows:]) / replicas
    new_errors = (full - approx)[None]
    new_momentum = 0.9 * momentum + approx
    new_weights = weights - 0.1 * new_momentum
    vec_moved = 0.9 * vec_momentum + vec_total / replicas
    return (new_errors, new_weights, new_momentum, vec_weights - 0.1 * vec_moved, vec_moved)


def solution(mesh):
    placed = (
        P(None, "replica", "shard"),
        P(None, "replica", None),
        P("replica", None, "shard", None),
        P(None, "shard", None),
        P(None, "shard", None),
        P(),
        P("replica", None, "shard"),
        P(None, "shard"),
        P(None, "shard"),
    )
    return jax.shard_map(
        body,
        mesh=mesh,
        in_specs=placed,
        out_specs=(
            P("replica", None, "shard", None),
            P(None, "shard", None),
            P(None, "shard", None),
            P(None, "shard"),
            P(None, "shard"),
        ),
        check_vma=False,
    )
```

time: 610 us -> 172 us (0.28)
  waiting for transfers between devices: 423 us -> 48.5 us
  blocking collectives: 89.2 us -> 0 us
  starting transfers between devices: 0.34 us -> 57.8 us
  matrix products: 45.7 us -> 21.6 us
  between operations: 13.9 us -> 1.07 us
  local copies, waits for them, and re-layouts: 3.63 us -> 15.2 us
  other arithmetic: 33.7 us -> 27.1 us
    psum x4 -> x0, waiting for transfers between devices: 423 us -> none  [the longest x2 289 us: reduce_right(): return lax.psum(terms, ('replica', 'shard'))]
    psum x3 -> x0, blocking collectives: 89.2 us -> none  [the longest x1 62.7 us: body(): vec_total = lax.psum(vec_grads[0], 'replica')]
    ppermute x0 -> x33, starting transfers between devices: none -> 57.8 us  [the longest x15 22.7 us: swap_y(): return lax.ppermute(value, 'replica', y_pairs(k))]
    ppermute x0 -> x33, waiting for transfers between devices: none -> 48.5 us  [the longest x15 20.9 us: swap_y(): return lax.ppermute(value, 'replica', y_pairs(k))]
    dot_general x8 -> x12, matrix products: 33.4 us -> 12.4 us  [mm(): return jnp.einsum(spec, a, b, precision=HIGH)]
    another operation x17, other arithmetic: 33 us -> 20.1 us  [the longest x9 10.8 us: inv_lower(): lower = jnp.linalg.cholesky(gram)]
    add x0 -> x10, other arithmetic: none -> 6.13 us  [the longest x1 3.26 us: body(): both = own + lax.ppermute(other, 'replica', CORE)]
  transfers between devices with their start and end apart: 4 -> 33, of which waited for: 4 -> 13; matrix products, arithmetic and copies ran while one was open for 0% -> 17% of each run, Pallas kernels for 0% -> 0%
where the time goes in v1:
time: 172 us; the launch traced here: 171 us
  starting transfers between devices  57.8 us (34%)
  waiting for transfers between devices  48.5 us (28%)
  other arithmetic  27.1 us (16%)
  matrix products  21.6 us (13%)
  local copies, waits for them, and re-layouts  15.2 us (9%)
    ppermute x15, starting transfers between devices, swap_y(): return lax.ppermute(value, 'replica', y_pairs(k))  22.7 us
    ppermute x15, waiting for transfers between devices, swap_y(): return lax.ppermute(value, 'replica', y_pairs(k))  20.9 us
    ppermute x9, waiting for transfers between devices, swap_z(): return lax.ppermute(value, 'replica', z_pairs(k))  18.9 us
    dot_general x12, matrix products, mm(): return jnp.einsum(spec, a, b, precision=HIGH)  12.4 us
    another operation x9, other arithmetic, inv_lower(): lower = jnp.linalg.cholesky(gram)  10.8 us
    ppermute x9, starting transfers between devices, swap_z(): return lax.ppermute(value, 'replica', z_pairs(k))  10.1 us
    another operation x6, other arithmetic, inv_lower(): return lax.linalg.triangular_solve(lower, eye, left_side=True, lower=True)  9.26 us
    ppermute x1, starting transfers between devices, body(): theirs = lax.ppermute(mine, 'replica', CORE)  8.64 us
  transfers between devices with their start and end apart: 33, of which 13 were waited for; matrix products, arithmetic and copies ran while one was open for 17% of the time, Pallas kernels for 0%

profile of v1, /device:TPU:1, one launch (start us, length us, event | category | flops | bytes accessed | tf_op | source)
XLA Modules:
  0.0 171.2 jit_solution(2265916065543590072)
XLA Ops:
  2.4 8.5 %fusion = f32[2,320,1280]{2,1,0:T(8,128)S(1)} fusion(bf16[2,2048,320]{1,2,0:T(8,128)(2,1)S(1)} %copy-done, bf16[2,2048,1280]{2,1,0:T(8,128)(2,1)} %param.13, f32[1,2,320,1280]{3,2,1,0:T(8,128)} %param.14), kind=kOutput, calls=%fused_computation.2 | convolution fusion | flops 3357081600 | bytes 19660800 | tf_op jit(solution)/shard_map/mtd,mte->mde/dot_general | solution.py:58
  15.3 3.5 %collective-permute-done = f32[320,1280]{1,0:T(8,128)} collective-permute-done((f32[320,1280]{1,0:T(8,128)}, f32[320,1280]{1,0:T(8,128)}, u32[]{:S(2)}, u32[]{:S(2)}) %collective-permute-start) | collective-permute-done | bytes 1638432 | tf_op jit(solution)/shard_map/ppermute | solution.py:62
  18.7 3.3 %bitcast_add_fusion = f32[320,1280]{1,0:T(8,128)} fusion(f32[320,1280]{1,0:T(8,128)} %collective-permute-done, f32[2,320,1280]{2,1,0:T(8,128)} %copy-done.1, s32[]{:T(128)S(6)} %select_n.43), kind=kLoop, calls=%fused_computation.6 | loop fusion | flops 409600 | bytes 4915204 | tf_op jit(solution)/shard_map/add | solution.py:62
  22.0 3.5 %reshape.24 = f32[320,4,320]{2,1,0:T(4,128)} reshape(f32[320,1280]{1,0:T(8,128)} %bitcast_add_fusion) | data formatting | bytes 3276800 | tf_op jit(solution)/shard_map/reshape | solution.py:63
  25.5 5.5 %dynamic-slice_bitcast_fusion.1 = (f32[1,320,320]{1,0,2:T(1,128)S(1)}, f32[320,1,320]{2,1,0:T(1,128)S(1)}, f32[320,1,320]{2,1,0:T(1,128)S(1)}, f32[320,1,320]{2,1,0:T(1,128)S(1)}) fusion(f32[320,4,320]{2,1,0:T(4,128)} %reshape.24, s32[]{:T(128)S(6)} %select_n.48, s32[]{:T(128)S(6)} %select_n.46, s32[]{:T(128)S(6)} %select_n.45, s32[]{:T(128)S(6)} %select_n.47), kind=kLoop, calls=%fused_computation.15 | loop fusion | bytes 3276816 | tf_op jit(solution)/shard_map/jit(dynamic_index_in_dim)/dynamic_slice | solution.py:64
  32.6 2.7 %collective-permute-start.8 = (f32[320,320]{0,1:T(8,128)S(1)}, f32[320,320]{0,1:T(8,128)S(1)}, u32[]{:S(2)}, u32[]{:S(2)}) collective-permute-start(f32[320,320]{0,1:T(8,128)S(1)} %bitcast.99), channel_id=1, source_target_pairs={{0,16},{4,20},{8,24},{12,28},{16,0},{20,4},{24,8},{28,12},{32,48},... | collective-permute-start | bytes 1228808 | tf_op jit(solution)/shard_map/ppermute | solution.py:25
  37.0 3.8 %collective-permute-start.2 = (f32[32,320]{1,0:T(8,128)S(1)}, f32[32,320]{1,0:T(8,128)S(1)}, u32[]{:S(2)}, u32[]{:S(2)}) collective-permute-start(f32[32,320]{1,0:T(8,128)S(1)} %fusion.10), channel_id=1, source_target_pairs={{0,16},{4,20},{8,24},{12,28},{16,0},{20,4},{24,8},{28,12},{32,48},... | collective-permute-start | bytes 122888 | tf_op jit(solution)/shard_map/ppermute | solution.py:25
  40.8 14.4 %collective-permute-done.1 = f32[32,320]{1,0:T(8,128)S(1)} collective-permute-done((f32[32,320]{1,0:T(8,128)S(1)}, f32[32,320]{1,0:T(8,128)S(1)}, u32[]{:S(2)}, u32[]{:S(2)}) %collective-permute-start.1) | collective-permute-done | bytes 40992 | tf_op jit(solution)/shard_map/ppermute | solution.py:25
  55.2 2.8 %collective-permute-start.3 = (f32[32,320]{1,0:T(8,128)S(1)}, f32[32,320]{1,0:T(8,128)S(1)}, u32[]{:S(2)}, u32[]{:S(2)}) collective-permute-start(f32[32,320]{1,0:T(8,128)S(1)} %fusion.10), channel_id=1, source_target_pairs={{0,24},{4,28},{8,16},{12,20},{16,8},{20,12},{24,0},{28,4},{32,56},... | collective-permute-start | bytes 122888 | tf_op jit(solution)/shard_map/ppermute | solution.py:25
  58.5 2.5 %collective-permute-done.3 = f32[32,320]{1,0:T(8,128)S(1)} collective-permute-done((f32[32,320]{1,0:T(8,128)S(1)}, f32[32,320]{1,0:T(8,128)S(1)}, u32[]{:S(2)}, u32[]{:S(2)}) %collective-permute-start.3) | collective-permute-done | bytes 40992 | tf_op jit(solution)/shard_map/ppermute | solution.py:25
  62.7 3.3 %collective-permute-start.5 = (f32[32,320]{1,0:T(8,128)S(1)}, f32[32,320]{1,0:T(8,128)S(1)}, u32[]{:S(2)}, u32[]{:S(2)}) collective-permute-start(f32[32,320]{1,0:T(8,128)S(1)} %add_add_fusion.5), channel_id=1, source_target_pairs={{0,64},{4,68},{8,72},{12,76},{16,80},{20,84},{24,88},{28,92},{32,9... | collective-permute-start | bytes 122888 | tf_op jit(solution)/shard_map/ppermute | solution.py:29
  66.3 3.8 %collective-permute-start.11 = (f32[320,320]{0,1:T(8,128)S(1)}, f32[320,320]{0,1:T(8,128)S(1)}, u32[]{:S(2)}, u32[]{:S(2)}) collective-permute-start(f32[320,320]{0,1:T(8,128)S(1)} %fusion.2), channel_id=1, source_target_pairs={{0,64},{4,68},{8,72},{12,76},{16,80},{20,84},{24,88},{28,92},{32,9... | collective-permute-start | bytes 1228808 | tf_op jit(solution)/shard_map/ppermute | solution.py:29
  70.9 6.7 %collective-permute-done.10 = f32[320,320]{0,1:T(8,128)S(1)} collective-permute-done((f32[320,320]{0,1:T(8,128)S(1)}, f32[320,320]{0,1:T(8,128)S(1)}, u32[]{:S(2)}, u32[]{:S(2)}) %collective-permute-start.10) | collective-permute-done | bytes 409632 | tf_op jit(solution)/shard_map/ppermute | solution.py:29
  77.6 11.6 %collective-permute-done.11 = f32[320,320]{0,1:T(8,128)S(1)} collective-permute-done((f32[320,320]{0,1:T(8,128)S(1)}, f32[320,320]{0,1:T(8,128)S(1)}, u32[]{:S(2)}, u32[]{:S(2)}) %collective-permute-start.11) | collective-permute-done | bytes 409632 | tf_op jit(solution)/shard_map/ppermute | solution.py:29
  93.9 7.1 %collective-permute-start.26 = (f32[4,320]{1,0:T(4,128)S(1)}, f32[4,320]{1,0:T(4,128)}, u32[]{:S(2)}, u32[]{:S(2)}) collective-permute-start(f32[4,320]{1,0:T(4,128)S(1)} %bitcast.106), channel_id=1, source_target_pairs={{0,4},{4,0},{8,12},{12,8},{16,20},{20,16},{24,28},{28,24},{32,36},... | collective-permute-start | bytes 15368 | tf_op jit(solution)/shard_map/ppermute | solution.py:70
  102.9 2.9 %cholesky.59 = f32[32,32]{1,0:T(8,128)S(1)} custom-call(f32[32,32]{1,0:T(8,128)S(1)} %fusion.30), custom_call_target="Cholesky" | custom-call | tf_op jit(solution)/shard_map/jit(cholesky)/cholesky | solution.py:42
  111.1 2.7 %collective-permute-start.17 = (f32[32,352]{0,1:T(8,128)S(1)}, f32[32,352]{0,1:T(8,128)S(1)}, u32[]{:S(2)}, u32[]{:S(2)}) collective-permute-start(f32[32,352]{0,1:T(8,128)S(1)} %copy.45), channel_id=1, source_target_pairs={{0,16},{4,20},{8,24},{12,28},{16,0},{20,4},{24,8},{28,12},{32,48},... | collective-permute-start | bytes 135176 | tf_op jit(solution)/shard_map/ppermute | solution.py:25
  115.7 2.7 %collective-permute-start.28 = (f32[4,320]{1,0:T(4,128)S(1)}, f32[4,320]{1,0:T(4,128)}, u32[]{:S(2)}, u32[]{:S(2)}) collective-permute-start(f32[4,320]{1,0:T(4,128)S(1)} %bitcast_add_fusion.4), channel_id=1, source_target_pairs={{0,16},{4,20},{8,24},{12,28},{16,0},{20,4},{24,8},{28,12},{32,48},... | collective-permute-start | bytes 15368 | tf_op jit(solution)/shard_map/ppermute | solution.py:25
  120.8 2.9 %cholesky.70 = f32[32,32]{1,0:T(8,128)S(1)} custom-call(f32[32,32]{1,0:T(8,128)S(1)} %fusion.28), custom_call_target="Cholesky" | custom-call | tf_op jit(solution)/shard_map/jit(cholesky)/cholesky | solution.py:42
  128.8 3.6 %collective-permute-start.20 = (f32[32,352]{0,1:T(8,128)S(1)}, f32[32,352]{0,1:T(8,128)S(1)}, u32[]{:S(2)}, u32[]{:S(2)}) collective-permute-start(f32[32,352]{0,1:T(8,128)S(1)} %copy.50), channel_id=1, source_target_pairs={{0,2},{1,3},{2,0},{3,1},{4,6},{5,7},{6,4},{7,5},{8,10},{9,11},{10,... | collective-permute-start | bytes 135176 | tf_op jit(solution)/shard_map/ppermute | solution.py:33
  134.5 2.9 %collective-permute-done.20 = f32[32,352]{0,1:T(8,128)S(1)} collective-permute-done((f32[32,352]{0,1:T(8,128)S(1)}, f32[32,352]{0,1:T(8,128)S(1)}, u32[]{:S(2)}, u32[]{:S(2)}) %collective-permute-start.20) | collective-permute-done | bytes 45088 | tf_op jit(solution)/shard_map/ppermute | solution.py:33
  139.4 2.9 %cholesky.81 = f32[32,32]{1,0:T(8,128)S(1)} custom-call(f32[32,32]{1,0:T(8,128)S(1)} %fusion.26), custom_call_target="Cholesky" | custom-call | tf_op jit(solution)/shard_map/jit(cholesky)/cholesky | solution.py:42
  153.3 8.6 %collective-permute-start.25 = (f32[32,1600]{1,0:T(8,128)S(1)}, f32[32,1600]{1,0:T(8,128)S(1)}, u32[]{:S(2)}, u32[]{:S(2)}) collective-permute-start(f32[32,1600]{1,0:T(8,128)S(1)} %concatenate.15), channel_id=1, source_target_pairs={{0,4},{4,0},{8,12},{12,8},{16,20},{20,16},{24,28},{28,24},{32,36},... | collective-permute-start | bytes 614408 | tf_op jit(solution)/shard_map/ppermute | solution.py:90
  163.1 8.1 %multiply_subtract_fusion = (f32[2,320,1280]{2,1,0:T(8,128)}, f32[2,320,1280]{2,1,0:T(8,128)}, f32[1,2,320,1280]{3,2,1,0:T(8,128)}) fusion(f32[2,320,1280]{2,1,0:T(8,128)} %param.15, f32[2,320,1280]{2,1,0:T(8,128)} %param.16, f32[2,320,1280]{2,1,0:T(8,128)} %copy-done.1, f32[1,32,1600]{2,1,0:T(8,128)S(1)} %get-tuple-element.17, ...), kind=kOutput, calls=%fused_computation.3 | convolution fusion | flops 319590400 | bytes 20070400 | tf_op jit(solution)/shard_map/mkd,mke->mde/dot_general | solution.py:48
  (125 shorter events, 49.7 us)
Async XLA Ops:
  31.1 35.0 %collective-permute-start.7 = (f32[320,320]{0,1:T(8,128)S(1)}, f32[320,320]{0,1:T(8,128)S(1)}, u32[]{:S(2)}, u32[]{:S(2)}) collective-permute-start(f32[320,320]{0,1:T(8,128)S(1)} %bitcast.100), channel_id=1, source_target_pairs={{0,8},{4,12},{8,0},{12,4},{16,24},{20,28},{24,16},{28,20},{32,40},... | collective-permute-start | bytes 1228808 | tf_op jit(solution)/shard_map/ppermute | solution.py:25
  32.6 33.5 %collective-permute-start.8 = (f32[320,320]{0,1:T(8,128)S(1)}, f32[320,320]{0,1:T(8,128)S(1)}, u32[]{:S(2)}, u32[]{:S(2)}) collective-permute-start(f32[320,320]{0,1:T(8,128)S(1)} %bitcast.99), channel_id=1, source_target_pairs={{0,16},{4,20},{8,24},{12,28},{16,0},{20,4},{24,8},{28,12},{32,48},... | collective-permute-start | bytes 1228808 | tf_op jit(solution)/shard_map/ppermute | solution.py:25
  35.3 30.8 %collective-permute-start.9 = (f32[320,320]{0,1:T(8,128)S(1)}, f32[320,320]{0,1:T(8,128)S(1)}, u32[]{:S(2)}, u32[]{:S(2)}) collective-permute-start(f32[320,320]{0,1:T(8,128)S(1)} %bitcast.101), channel_id=1, source_target_pairs={{0,24},{4,28},{8,16},{12,20},{16,8},{20,12},{24,0},{28,4},{32,56},... | collective-permute-start | bytes 1228808 | tf_op jit(solution)/shard_map/ppermute | solution.py:25
  36.9 18.3 %collective-permute-start.1 = (f32[32,320]{1,0:T(8,128)S(1)}, f32[32,320]{1,0:T(8,128)S(1)}, u32[]{:S(2)}, u32[]{:S(2)}) collective-permute-start(f32[32,320]{1,0:T(8,128)S(1)} %fusion.10), channel_id=1, source_target_pairs={{0,8},{4,12},{8,0},{12,4},{16,24},{20,28},{24,16},{28,20},{32,40},... | collective-permute-start | bytes 122888 | tf_op jit(solution)/shard_map/ppermute | solution.py:25
  37.0 21.5 %collective-permute-start.2 = (f32[32,320]{1,0:T(8,128)S(1)}, f32[32,320]{1,0:T(8,128)S(1)}, u32[]{:S(2)}, u32[]{:S(2)}) collective-permute-start(f32[32,320]{1,0:T(8,128)S(1)} %fusion.10), channel_id=1, source_target_pairs={{0,16},{4,20},{8,24},{12,28},{16,0},{20,4},{24,8},{28,12},{32,48},... | collective-permute-start | bytes 122888 | tf_op jit(solution)/shard_map/ppermute | solution.py:25
  61.0 9.1 %collective-permute-start.4 = (f32[32,320]{1,0:T(8,128)S(1)}, f32[32,320]{1,0:T(8,128)S(1)}, u32[]{:S(2)}, u32[]{:S(2)}) collective-permute-start(f32[32,320]{1,0:T(8,128)S(1)} %add_add_fusion.5), channel_id=1, source_target_pairs={{0,32},{4,36},{8,40},{12,44},{16,48},{20,52},{24,56},{28,60},{32,0... | collective-permute-start | bytes 122888 | tf_op jit(solution)/shard_map/ppermute | solution.py:29
  62.7 7.4 %collective-permute-start.5 = (f32[32,320]{1,0:T(8,128)S(1)}, f32[32,320]{1,0:T(8,128)S(1)}, u32[]{:S(2)}, u32[]{:S(2)}) collective-permute-start(f32[32,320]{1,0:T(8,128)S(1)} %add_add_fusion.5), channel_id=1, source_target_pairs={{0,64},{4,68},{8,72},{12,76},{16,80},{20,84},{24,88},{28,92},{32,9... | collective-permute-start | bytes 122888 | tf_op jit(solution)/shard_map/ppermute | solution.py:29
  66.2 11.4 %collective-permute-start.10 = (f32[320,320]{0,1:T(8,128)S(1)}, f32[320,320]{0,1:T(8,128)S(1)}, u32[]{:S(2)}, u32[]{:S(2)}) collective-permute-start(f32[320,320]{0,1:T(8,128)S(1)} %fusion.2), channel_id=1, source_target_pairs={{0,32},{4,36},{8,40},{12,44},{16,48},{20,52},{24,56},{28,60},{32,0... | collective-permute-start | bytes 1228808 | tf_op jit(solution)/shard_map/ppermute | solution.py:29
  66.3 23.0 %collective-permute-start.11 = (f32[320,320]{0,1:T(8,128)S(1)}, f32[320,320]{0,1:T(8,128)S(1)}, u32[]{:S(2)}, u32[]{:S(2)}) collective-permute-start(f32[320,320]{0,1:T(8,128)S(1)} %fusion.2), channel_id=1, source_target_pairs={{0,64},{4,68},{8,72},{12,76},{16,80},{20,84},{24,88},{28,92},{32,9... | collective-permute-start | bytes 1228808 | tf_op jit(solution)/shard_map/ppermute | solution.py:29
  70.1 19.1 %collective-permute-start.12 = (f32[320,320]{0,1:T(8,128)S(1)}, f32[320,320]{0,1:T(8,128)S(1)}, u32[]{:S(2)}, u32[]{:S(2)}) collective-permute-start(f32[320,320]{0,1:T(8,128)S(1)} %fusion.2), channel_id=1, source_target_pairs={{0,96},{4,100},{8,104},{12,108},{16,112},{20,116},{24,120},{28,124... | collective-permute-start | bytes 1228808 | tf_op jit(solution)/shard_map/ppermute | solution.py:29
  89.9 11.0 %collective-permute-start.13 = (f32[32,352]{0,1:T(8,128)S(1)}, f32[32,352]{0,1:T(8,128)S(1)}, u32[]{:S(2)}, u32[]{:S(2)}) collective-permute-start(f32[32,352]{0,1:T(8,128)S(1)} %copy.40), channel_id=1, source_target_pairs={{0,1},{1,0},{2,3},{3,2},{4,5},{5,4},{6,7},{7,6},{8,9},{9,8},{10,11... | collective-permute-start | bytes 135176 | tf_op jit(solution)/shard_map/ppermute | solution.py:33
  91.2 9.7 %collective-permute-start.14 = (f32[32,352]{0,1:T(8,128)S(1)}, f32[32,352]{0,1:T(8,128)}, u32[]{:S(2)}, u32[]{:S(2)}) collective-permute-start(f32[32,352]{0,1:T(8,128)S(1)} %copy.40), channel_id=1, source_target_pairs={{0,2},{1,3},{2,0},{3,1},{4,6},{5,7},{6,4},{7,5},{8,10},{9,11},{10,... | collective-permute-start | bytes 135176 | tf_op jit(solution)/shard_map/ppermute | solution.py:33
  93.7 8.0 %collective-permute-start.15 = (f32[32,352]{0,1:T(8,128)S(1)}, f32[32,352]{0,1:T(8,128)}, u32[]{:S(2)}, u32[]{:S(2)}) collective-permute-start(f32[32,352]{0,1:T(8,128)S(1)} %copy.40), channel_id=1, source_target_pairs={{0,3},{1,2},{2,1},{3,0},{4,7},{5,6},{6,5},{7,4},{8,11},{9,10},{10,... | collective-permute-start | bytes 135176 | tf_op jit(solution)/shard_map/ppermute | solution.py:33
  93.9 21.1 %collective-permute-start.26 = (f32[4,320]{1,0:T(4,128)S(1)}, f32[4,320]{1,0:T(4,128)}, u32[]{:S(2)}, u32[]{:S(2)}) collective-permute-start(f32[4,320]{1,0:T(4,128)S(1)} %bitcast.106), channel_id=1, source_target_pairs={{0,4},{4,0},{8,12},{12,8},{16,20},{20,16},{24,28},{28,24},{32,36},... | collective-permute-start | bytes 15368 | tf_op jit(solution)/shard_map/ppermute | solution.py:70
  111.0 7.3 %collective-permute-start.16 = (f32[32,352]{0,1:T(8,128)S(1)}, f32[32,352]{0,1:T(8,128)S(1)}, u32[]{:S(2)}, u32[]{:S(2)}) collective-permute-start(f32[32,352]{0,1:T(8,128)S(1)} %copy.45), channel_id=1, source_target_pairs={{0,8},{4,12},{8,0},{12,4},{16,24},{20,28},{24,16},{28,20},{32,40},... | collective-permute-start | bytes 135176 | tf_op jit(solution)/shard_map/ppermute | solution.py:25
  111.1 8.4 %collective-permute-start.17 = (f32[32,352]{0,1:T(8,128)S(1)}, f32[32,352]{0,1:T(8,128)S(1)}, u32[]{:S(2)}, u32[]{:S(2)}) collective-permute-start(f32[32,352]{0,1:T(8,128)S(1)} %copy.45), channel_id=1, source_target_pairs={{0,16},{4,20},{8,24},{12,28},{16,0},{20,4},{24,8},{28,12},{32,48},... | collective-permute-start | bytes 135176 | tf_op jit(solution)/shard_map/ppermute | solution.py:25
  115.7 16.8 %collective-permute-start.27 = (f32[4,320]{1,0:T(4,128)S(1)}, f32[4,320]{1,0:T(4,128)S(1)}, u32[]{:S(2)}, u32[]{:S(2)}) collective-permute-start(f32[4,320]{1,0:T(4,128)S(1)} %bitcast_add_fusion.4), channel_id=1, source_target_pairs={{0,8},{4,12},{8,0},{12,4},{16,24},{20,28},{24,16},{28,20},{32,40},... | collective-permute-start | bytes 15368 | tf_op jit(solution)/shard_map/ppermute | solution.py:25
  115.7 17.0 %collective-permute-start.28 = (f32[4,320]{1,0:T(4,128)S(1)}, f32[4,320]{1,0:T(4,128)}, u32[]{:S(2)}, u32[]{:S(2)}) collective-permute-start(f32[4,320]{1,0:T(4,128)S(1)} %bitcast_add_fusion.4), channel_id=1, source_target_pairs={{0,16},{4,20},{8,24},{12,28},{16,0},{20,4},{24,8},{28,12},{32,48},... | collective-permute-start | bytes 15368 | tf_op jit(solution)/shard_map/ppermute | solution.py:25
  118.4 14.3 %collective-permute-start.29 = (f32[4,320]{1,0:T(4,128)S(1)}, f32[4,320]{1,0:T(4,128)}, u32[]{:S(2)}, u32[]{:S(2)}) collective-permute-start(f32[4,320]{1,0:T(4,128)S(1)} %bitcast_add_fusion.4), channel_id=1, source_target_pairs={{0,24},{4,28},{8,16},{12,20},{16,8},{20,12},{24,0},{28,4},{32,56},... | collective-permute-start | bytes 15368 | tf_op jit(solution)/shard_map/ppermute | solution.py:25
  128.8 8.6 %collective-permute-start.20 = (f32[32,352]{0,1:T(8,128)S(1)}, f32[32,352]{0,1:T(8,128)S(1)}, u32[]{:S(2)}, u32[]{:S(2)}) collective-permute-start(f32[32,352]{0,1:T(8,128)S(1)} %copy.50), channel_id=1, source_target_pairs={{0,2},{1,3},{2,0},{3,1},{4,6},{5,7},{6,4},{7,5},{8,10},{9,11},{10,... | collective-permute-start | bytes 135176 | tf_op jit(solution)/shard_map/ppermute | solution.py:33
  133.4 28.5 %collective-permute-start.30 = (f32[4,320]{1,0:T(4,128)S(1)}, f32[4,320]{1,0:T(4,128)S(1)}, u32[]{:S(2)}, u32[]{:S(2)}) collective-permute-start(f32[4,320]{1,0:T(4,128)S(1)} %add_add_fusion.6), channel_id=1, source_target_pairs={{0,32},{4,36},{8,40},{12,44},{16,48},{20,52},{24,56},{28,60},{32,0... | collective-permute-start | bytes 15368 | tf_op jit(solution)/shard_map/ppermute | solution.py:29
  133.4 28.5 %collective-permute-start.31 = (f32[4,320]{1,0:T(4,128)S(1)}, f32[4,320]{1,0:T(4,128)S(1)}, u32[]{:S(2)}, u32[]{:S(2)}) collective-permute-start(f32[4,320]{1,0:T(4,128)S(1)} %add_add_fusion.6), channel_id=1, source_target_pairs={{0,64},{4,68},{8,72},{12,76},{16,80},{20,84},{24,88},{28,92},{32,9... | collective-permute-start | bytes 15368 | tf_op jit(solution)/shard_map/ppermute | solution.py:29
  150.7 11.2 %collective-permute-start.32 = (f32[4,320]{1,0:T(4,128)S(1)}, f32[4,320]{1,0:T(4,128)S(1)}, u32[]{:S(2)}, u32[]{:S(2)}) collective-permute-start(f32[4,320]{1,0:T(4,128)S(1)} %add_add_fusion.6), channel_id=1, source_target_pairs={{0,96},{4,100},{8,104},{12,108},{16,112},{20,116},{24,120},{28,124... | collective-permute-start | bytes 15368 | tf_op jit(solution)/shard_map/ppermute | solution.py:29
  153.3 9.7 %collective-permute-start.25 = (f32[32,1600]{1,0:T(8,128)S(1)}, f32[32,1600]{1,0:T(8,128)S(1)}, u32[]{:S(2)}, u32[]{:S(2)}) collective-permute-start(f32[32,1600]{1,0:T(8,128)S(1)} %concatenate.15), channel_id=1, source_target_pairs={{0,4},{4,0},{8,12},{12,8},{16,20},{20,16},{24,28},{28,24},{32,36},... | collective-permute-start | bytes 614408 | tf_op jit(solution)/shard_map/ppermute | solution.py:90
  (17 other events, 246.7 us)

commit v2 on v0

v2 whole, which is shorter than its diff:
```python
import math

import jax
import jax.numpy as jnp
from jax import lax
from jax.experimental import pallas as pl
from jax.experimental.pallas import tpu as pltpu
from jax.sharding import PartitionSpec as P

F32 = jnp.float32
BF16 = jnp.bfloat16
HIGH = lax.Precision.HIGHEST
NN = (((1,), (0,)), ((), ()))
NT = (((1,), (1,)), ((), ()))
TN = (((0,), (0,)), ((), ()))

CORE = [(r, r ^ 1) for r in range(32)]


def swap_core(value):
    return lax.ppermute(value, "replica", CORE)


def swap_y(value, k):
    return lax.ppermute(value, "replica", [(r, r ^ (k << 1)) for r in range(32)])


def swap_z(value, k):
    return lax.ppermute(value, "replica", [(r, r ^ (k << 3)) for r in range(32)])


def swap_x(value, k):
    return lax.ppermute(value, "shard", [(s, s ^ k) for s in range(4)])


def fan(value, swap):
    return [value] + [swap(value, k) for k in (1, 2, 3)]


def add4(parts):
    return (parts[0] + parts[1]) + (parts[2] + parts[3])


def dot(a, b, dims, precision=None):
    return lax.dot_general(a, b, dims, precision=precision, preferred_element_type=F32)


def split(value):
    high = value.astype(BF16)
    return high, (value - high.astype(F32)).astype(BF16)


def dot3(a, b_high, b_low, dims):
    high, low = split(a)
    rows = a.shape[0]
    top = dot(jnp.concatenate([high, low], axis=0), b_high, dims)
    return top[:rows] + (top[rows:] + dot(high, b_low, dims))


def lanes(shape):
    return lax.broadcasted_iota(jnp.int32, shape, 1)


def unpack(chunk):
    half = chunk[640:800]
    half = jnp.concatenate([half, pltpu.roll(half, 64, 1)], axis=0)
    half = jnp.where(lanes(half.shape) < 64, half, 0.0)
    return jnp.concatenate([chunk[:320], chunk[320:640], half], axis=1)


def grad_kernel(which, a_ref, c_ref, e_ref, out_ref, *, scale):
    out_ref[...] = dot(a_ref[0], c_ref[0], NN) * scale + e_ref[0]


def route_kernel(where, a_ref, b_ref, o0, o1, o2, o3, stage):
    left = lanes((160, 128)) < 64
    for i in range(2):
        def tile(t):
            at = 640 * i + 128 * t
            return a_ref[:, at:at + 128] + b_ref[:, at:at + 128]
        middle = tile(2)
        rolled = pltpu.roll(middle, 64, 1)
        stage[2 * i, 0:320] = tile(0)
        stage[2 * i, 320:640] = tile(1)
        stage[2 * i, 640:800] = jnp.where(left, middle[:160], rolled[160:])
        stage[2 * i + 1, 0:320] = tile(3)
        stage[2 * i + 1, 320:640] = tile(4)
        stage[2 * i + 1, 640:800] = jnp.where(left, rolled[:160], middle[160:])
    y = where[1]
    for k, out in enumerate((o0, o1, o2, o3)):
        out[...] = stage[y ^ k]


def first_kernel(where, c0, c1, c2, c3, q_ref, v_ref, out_ref, stage):
    core, y = where[0], where[1]
    q = q_ref[core]
    left = lanes((32, 128)) < 64
    for i in range(2):
        at = 640 * i
        middle = q[:, at + 256:at + 384]
        stage[2 * i, :, 0:256] = q[:, at:at + 256]
        stage[2 * i, :, 256:384] = jnp.where(left, middle, 0.0)
        stage[2 * i + 1, :, 0:256] = q[:, at + 384:at + 640]
        stage[2 * i + 1, :, 256:384] = jnp.where(left, pltpu.roll(middle, 64, 1), 0.0)
    total = jnp.zeros((32, 320), F32)
    for k, chunk in enumerate((c0, c1, c2, c3)):
        high, low = split(unpack(chunk[...]))
        total = total + dot3(stage[y ^ k], high, low, NT)
    out_ref[...] = jnp.zeros((40, 384), F32)
    out_ref[0:32, 0:320] = total
    out_ref[32:36, 0:320] = v_ref[...]


def eliminate(tile):
    lane = lanes((32, 128))
    row = lax.broadcasted_iota(jnp.int32, (32, 128), 0)
    work = jnp.where((lane >= 64) & (lane < 96), tile, jnp.where(lane == row + 96, 1.0, 0.0))
    for k in range(31):
        factor = work[:, 64 + k:65 + k] * (1.0 / work[k:k + 1, 64 + k:65 + k])
        work = work - jnp.where(row > k, factor * work[k:k + 1, :], 0.0)
    pivots = jnp.sum(jnp.where(lane == row + 64, work, 0.0), axis=1, keepdims=True)
    return jnp.where(lane >= 96, work, 0.0), pivots


def below(value):
    return jnp.concatenate([jnp.zeros((96, value.shape[1]), F32), value], axis=0)


def payload(value):
    return jnp.where(lanes(value.shape) < 320, value, 0.0)


def orth(packed):
    inverse, pivots = eliminate(packed[:, 256:384])
    return dot(inverse * lax.rsqrt(pivots), below(payload(packed)), NN, HIGH)


def to_right(left, w_high, w_low):
    out = dot3(left, w_high, w_low, NN)
    zero = jnp.zeros((64, left.shape[1]), F32)
    shifted = jnp.concatenate([zero, left, zero[:32]], axis=0)
    gram = dot(left, shifted, NT, HIGH)
    return jnp.concatenate([out[:, :256], out[:, 256:] + gram], axis=1)


def wide_kernel(m0, m1, m2, m3, p0, p1, p2, p3, high_ref, low_ref, out_ref):
    whole = unpack((m0[...] + m1[...]) + (m2[...] + m3[...]))
    high, low = split(whole)
    zero = jnp.zeros((64, 384), BF16)
    high_ref[...] = jnp.concatenate([high, zero], axis=0)
    low_ref[...] = jnp.concatenate([low, zero], axis=0)
    left = ((p0[...] + p1[...]) + (p2[...] + p3[...]))[:32]
    out_ref[...] = to_right(left, high_ref[...], low_ref[...])


def left_kernel(a0, a1, a2, a3, high_ref, low_ref, out_ref):
    right = orth((a0[...] + a1[...]) + (a2[...] + a3[...]))
    high, low = split(right)
    zero = jnp.zeros((32, 384), BF16)
    w_high = jnp.concatenate([high_ref[0:320], high, zero], axis=0)
    w_low = jnp.concatenate([low_ref[0:320], low, zero], axis=0)
    out_ref[...] = dot3(right, w_high, w_low, NT)


def right_kernel(a0, a1, a2, a3, high_ref, low_ref, left_ref, out_ref):
    left = orth((a0[...] + a1[...]) + (a2[...] + a3[...]))
    left_ref[...] = left
    out_ref[...] = to_right(left, high_ref[...], low_ref[...])


def solve_kernel(packed_ref, left_ref, out_ref, *, scale):
    inverse, pivots = eliminate(packed_ref[:, 256:384])
    once = dot(inverse, below(left_ref[...]), NN, HIGH) * (scale / pivots)
    out_ref[...] = dot(inverse, once, TN, HIGH)[96:128]


def final_kernel(where, own, other, g0, g1, g2, g3, l_own, l_other, w_ref, m_ref,
                 e_out, w_out, m_out, stage, approx):
    slot, block = pl.program_id(0), pl.program_id(1)
    y = where[1]

    def start(first, left_ref):
        for k, g in enumerate((g0, g1, g2, g3)):
            stage[y ^ k] = g[first:first + 32]
        side = lanes((32, 128)) < 64
        tiles = []
        for i in range(2):
            even, odd = stage[2 * i], stage[2 * i + 1]
            middle = jnp.where(side, even[:, 256:], pltpu.roll(odd[:, 256:], 64, 1))
            tiles += [even[:, :256], middle, odd[:, :256]]
        r_high, r_low = split(jnp.concatenate(tiles, axis=1))
        l_high, l_low = split(left_ref[...])
        rights = jnp.concatenate([r_high, r_low, r_high], axis=0)
        lefts = jnp.concatenate([l_high, l_high, l_low], axis=0)
        approx[...] = dot(lefts, rights, TN)[:320]

    @pl.when((slot == 0) & (block == 0))
    def _():
        start(0, l_own)

    @pl.when((slot == 1) & (block == 0))
    def _():
        start(32, l_other)

    size = w_ref.shape[1]
    at = pl.multiple_of(block * size, 8)
    part = approx[pl.ds(at, size), :]

    @pl.when(slot == 0)
    def _():
        e_out[0] = own[pl.ds(at, size), :] - part

    @pl.when(slot == 1)
    def _():
        e_out[0] = other[pl.ds(at, size), :] - part

    moved = 0.9 * m_ref[0] + part
    m_out[0] = moved
    w_out[0] = w_ref[0] - 0.1 * moved


VM = pl.BlockSpec(memory_space=pltpu.VMEM)
SM = pl.BlockSpec(memory_space=pltpu.SMEM)
LIMIT = pltpu.CompilerParams(vmem_limit_bytes=40 << 20)


def shaped(shape, dtype=F32):
    return jax.ShapeDtypeStruct(shape, dtype)


def call(kernel, args, outs, specs, scratch=(), name=None):
    many = isinstance(outs, (list, tuple))
    return pl.pallas_call(
        kernel,
        out_shape=outs,
        in_specs=specs,
        out_specs=[VM] * len(outs) if many else VM,
        scratch_shapes=list(scratch),
        compiler_params=LIMIT,
        name=name,
    )(*args)


def gradients(which, acts, cots, errors, scale, name):
    mats, rows, toks = acts.shape
    cols = cots.shape[2]
    step = 256
    return pl.pallas_call(
        lambda *refs: grad_kernel(*refs, scale=scale),
        out_shape=shaped((rows, cols)),
        grid_spec=pltpu.PrefetchScalarGridSpec(
            num_scalar_prefetch=1,
            grid=(cols // step,),
            in_specs=[
                pl.BlockSpec((1, rows, toks), lambda j, s: (s[0], 0, 0)),
                pl.BlockSpec((1, toks, step), lambda j, s: (s[0], 0, j)),
                pl.BlockSpec((1, rows, step), lambda j, s: (s[0], 0, j)),
            ],
            out_specs=pl.BlockSpec((rows, step), lambda j, s: (0, j)),
        ),
        compiler_params=LIMIT,
        name=name,
    )(which, acts, cots, errors)


def finish(where, own, other, rights, l_own, l_other, weights, momentum):
    mats, rows, cols = weights.shape
    blocks = 4
    size = rows // blocks
    block = pl.BlockSpec((1, size, cols), lambda s, i, w: (w[0] ^ s, i, 0))
    return pl.pallas_call(
        final_kernel,
        out_shape=[shaped(weights.shape)] * 3,
        grid_spec=pltpu.PrefetchScalarGridSpec(
            num_scalar_prefetch=1,
            grid=(mats, blocks),
            in_specs=[VM] * 8 + [block, block],
            out_specs=[block] * 3,
            scratch_shapes=[pltpu.VMEM((4, 32, 384), F32), pltpu.VMEM((rows, cols), F32)],
        ),
        compiler_params=LIMIT,
        name="finish",
    )(where, own, other, *rights, l_own, l_other, weights, momentum)


def body(acts, cots, errors, weights, momentum, start_q, vec_grads, vec_weights, vec_momentum):
    scale = 1.0 / math.sqrt(acts.shape[1])
    replicas = float(lax.axis_size("replica"))
    index = lax.axis_index("replica")
    core = index & 1
    y = (index >> 1) & 3
    where = jnp.stack([core, y]).astype(jnp.int32)
    acts = acts.swapaxes(1, 2)

    vec_core = vec_grads[0] + swap_core(vec_grads[0])
    other = gradients(1 - where[:1], acts, cots, errors[0], scale, "grad_other")
    own = gradients(where[:1], acts, cots, errors[0], scale, "grad_own")
    chunks = call(route_kernel, (where, own, swap_core(other)), [shaped((800, 128))] * 4, [SM, VM, VM],
                  [pltpu.VMEM((4, 800, 128), F32)], name="route")
    mine = add4([chunks[0]] + [swap_y(chunks[k], k) for k in (1, 2, 3)])
    first = call(first_kernel, (where, *chunks, start_q.swapaxes(1, 2), vec_core), shaped((40, 384)),
                 [SM] + [VM] * 6, [pltpu.VMEM((4, 32, 384), F32)], name="first_left")
    firsts = fan(add4(fan(first, swap_y)), swap_z)
    wides = fan(mine, swap_z)
    w_high, w_low, packed = call(wide_kernel, (*wides, *firsts),
                                 [shaped((384, 384), BF16), shaped((384, 384), BF16), shaped((32, 384))],
                                 [VM] * 8, name="first_right")
    packed = call(left_kernel, (*fan(packed, swap_x), w_high, w_low), shaped((32, 384)), [VM] * 6, name="second_left")
    left, packed = call(right_kernel, (*fan(packed, swap_y), w_high, w_low), [shaped((32, 384))] * 2, [VM] * 6,
                        name="second_right")
    packed = add4(fan(packed, swap_x))
    rights = fan(jnp.concatenate([packed, swap_core(packed)], axis=0), swap_y)
    l_own = call(lambda *refs: solve_kernel(*refs, scale=1.0 / replicas), (packed, left), shaped((32, 384)), [VM] * 2,
                 name="solve")
    new_errors, new_weights, new_momentum = finish(where, own, other, rights, l_own, swap_core(l_own), weights, momentum)
    vec_moved = 0.9 * vec_momentum + add4(firsts)[32:36, :320] / replicas
    return (new_errors[None], new_weights, new_momentum, vec_weights - 0.1 * vec_moved, vec_moved)


def solution(mesh):
    placed = (
        P(None, "replica", "shard"),
        P(None, "replica", None),
        P("replica", None, "shard", None),
        P(None, "shard", None),
        P(None, "shard", None),
        P(),
        P("replica", None, "shard"),
        P(None, "shard"),
        P(None, "shard"),
    )
    return jax.shard_map(
        body,
        mesh=mesh,
        in_specs=placed,
        out_specs=(
            P("replica", None, "shard", None),
            P(None, "shard", None),
            P(None, "shard", None),
            P(None, "shard"),
            P(None, "shard"),
        ),
        check_vma=False,
    )
```

time: 610 us -> 125 us (0.20)
  waiting for transfers between devices: 423 us -> 46.5 us
  blocking collectives: 89.2 us -> 0 us
  matrix products: 45.7 us -> 0 us
  starting transfers between devices: 0.34 us -> 38.4 us
  other arithmetic: 33.7 us -> 0.81 us
  Pallas kernels: 0 us -> 30 us
  between operations: 13.9 us -> 0.81 us
    psum x4 -> x0, waiting for transfers between devices: 423 us -> none  [the longest x2 289 us: reduce_right(): return lax.psum(terms, ('replica', 'shard'))]
    psum x3 -> x0, blocking collectives: 89.2 us -> none  [the longest x1 62.7 us: body(): vec_total = lax.psum(vec_grads[0], 'replica')]
    ppermute x0 -> x28, waiting for transfers between devices: none -> 46.5 us  [the longest x12 20.5 us: swap_y(): return lax.ppermute(value, 'replica', [(r, r ^ k << 1) for r in range(32)])]
    dot_general x9 -> x0, matrix products: 41.8 us -> none  [the longest x1 11.3 us: body(): approx = jnp.einsum('mdk,mek->mde', left, right, precision=HIGH) / replicas]
    ppermute x0 -> x28, starting transfers between devices: none -> 38.4 us  [the longest x12 15 us: swap_y(): return lax.ppermute(value, 'replica', [(r, r ^ k << 1) for r in range(32)])]
    another operation x17 -> x1, other arithmetic: 33 us -> 0.08 us  [body(): where = jnp.stack([core, y]).astype(jnp.int32)]
    pallas_call x0 -> x9, Pallas kernels: none -> 30 us  [the longest x6 12.8 us: call(): pl.pallas_call(kernel, out_shape=outs, in_specs=specs, out_specs=[VM] * l...]
  transfers between devices with their start and end apart: 4 -> 28, of which waited for: 4 -> 16; matrix products, arithmetic and copies ran while one was open for 0% -> 1% of each run, Pallas kernels for 0% -> 8%
where the time goes in v2:
time: 125 us; the launch traced here: 124 us
  waiting for transfers between devices  46.5 us (37%)
  starting transfers between devices  38.4 us (31%)
  Pallas kernels  30 us (24%)
  local copies, waits for them, and re-layouts  7.37 us (6%)
    ppermute x12, waiting for transfers between devices, swap_y(): return lax.ppermute(value, 'replica', [(r, r ^ k << 1) for r in range(32)])  20.5 us
    ppermute x6, waiting for transfers between devices, swap_z(): return lax.ppermute(value, 'replica', [(r, r ^ k << 3) for r in range(32)])  19.4 us
    ppermute x12, starting transfers between devices, swap_y(): return lax.ppermute(value, 'replica', [(r, r ^ k << 1) for r in range(32)])  15 us
    pallas_call x6, Pallas kernels, call(): pl.pallas_call(kernel, out_shape=outs, in_specs=specs, out_specs=[VM] * l...  12.8 us
    pallas_call x2, Pallas kernels, gradients(): pl.pallas_call(lambda *refs: grad_kernel(*refs, scale=scale), out_shape=s...  10.7 us
    ppermute x4, starting transfers between devices, swap_core(): return lax.ppermute(value, 'replica', CORE)  9.56 us
    unnamed x20, local copies, waits for them, and re-layouts  7.37 us
    ppermute x6, starting transfers between devices, swap_z(): return lax.ppermute(value, 'replica', [(r, r ^ k << 3) for r in range(32)])  7.17 us
  transfers between devices with their start and end apart: 28, of which 16 were waited for; matrix products, arithmetic and copies ran while one was open for 1% of the time, Pallas kernels for 8%

profile of v2, /device:TPU:1, one launch (start us, length us, event | category | flops | bytes accessed | tf_op | source)
XLA Modules:
  0.0 123.9 jit_solution(5621323000276973861)
XLA Ops:
  0.6 1.9 %copy-done = f32[1,2,320,1280]{3,2,1,0:T(8,128)S(1)} copy-done((f32[1,2,320,1280]{3,2,1,0:T(8,128)S(1)}, f32[1,2,320,1280]{3,2,1,0:T(8,128)}, u32[]{:S(2)}) %copy-start) | copy-done | bytes 3276824
  2.6 1.7 %copy-done.2 = bf16[2,2048,320]{1,2,0:T(8,128)(2,1)S(1)} copy-done((bf16[2,2048,320]{1,2,0:T(8,128)(2,1)S(1)}, bf16[2,2048,320]{1,2,0:T(8,128)(2,1)}, u32[]{:S(2)}) %copy-start.2) | copy-done | bytes 2621464
  4.3 5.3 %grad_other.1.other = f32[320,1280]{1,0:T(8,128)S(1)} custom-call(s32[1]{0:T(128)S(6)} %sub.6.refs_0_, bf16[2,320,2048]{2,1,0:T(8,128)(2,1)S(1)} %bitcast.10, bf16[2,2048,1280]{2,1,0:T(8,128)(2,1)} %refs_2_.3, f32[2,320,1280]{2,1,0:T(8,128)S(1)} %bitcast.8), custom_call_target="tpu_custom_call" | custom-call | tf_op jit(solution)/shard_map/grad_other/pallas_call | solution.py:248
  11.1 1.9 %copy-done.1 = f32[1,2,320,1280]{3,2,1,0:T(8,128)S(1)} copy-done((f32[1,2,320,1280]{3,2,1,0:T(8,128)S(1)}, f32[1,2,320,1280]{3,2,1,0:T(8,128)}, u32[]{:S(2)}) %copy-start.1) | copy-done | bytes 3276824
  14.8 5.4 %grad_own.1.a_ref.own = f32[320,1280]{1,0:T(8,128)S(1)} custom-call(s32[1]{0:T(128)} %bitcast.refs_0_, bf16[2,320,2048]{2,1,0:T(8,128)(2,1)S(1)} %bitcast.11, bf16[2,2048,1280]{2,1,0:T(8,128)(2,1)} %refs_2_.3, f32[2,320,1280]{2,1,0:T(8,128)S(1)} %bitcast.9), custom_call_target="tpu_custom_call" | custom-call | tf_op jit(solution)/shard_map/grad_own/pallas_call | solution.py:248
  20.3 1.8 %route.1 = (f32[800,128]{1,0:T(8,128)S(1)}, f32[800,128]{1,0:T(8,128)S(1)}, f32[800,128]{1,0:T(8,128)S(1)}, f32[800,128]{1,0:T(8,128)S(1)}) custom-call(s32[2]{0:T(128)S(1)} %pad_add_fusion.where, f32[320,1280]{1,0:T(8,128)S(1)} %grad_own.1.a_ref.own, f32[320,1280]{1,0:T(8,128)} %collective-permute-done.b_ref), custom_call_target="tpu_custom_call" | custom-call | tf_op jit(solution)/shard_map/route/pallas_call | solution.py:233
  23.6 2.6 %collective-permute-start.2 = (f32[800,128]{1,0:T(8,128)S(1)}, f32[800,128]{1,0:T(8,128)S(1)}, u32[]{:S(2)}, u32[]{:S(2)}) collective-permute-start(f32[800,128]{1,0:T(8,128)S(1)} %get-tuple-element.19.c2), channel_id=1, source_target_pairs={{0,16},{4,20},{8,24},{12,28},{16,0},{20,4},{24,8},{28,12},{32,48},... | collective-permute-start | bytes 1228808 | tf_op jit(solution)/shard_map/ppermute | solution.py:25
  29.1 2.9 %collective-permute-start.10 = (f32[40,384]{1,0:T(8,128)S(1)}, f32[40,384]{1,0:T(8,128)S(1)}, u32[]{:S(2)}, u32[]{:S(2)}) collective-permute-start(f32[40,384]{1,0:T(8,128)S(1)} %first_left.1), channel_id=1, source_target_pairs={{0,24},{4,28},{8,16},{12,20},{16,8},{20,12},{24,0},{28,4},{32,56},... | collective-permute-start | bytes 184328 | tf_op jit(solution)/shard_map/ppermute | solution.py:25
  34.6 10.0 %collective-permute-done.2 = f32[800,128]{1,0:T(8,128)S(1)} collective-permute-done((f32[800,128]{1,0:T(8,128)S(1)}, f32[800,128]{1,0:T(8,128)S(1)}, u32[]{:S(2)}, u32[]{:S(2)}) %collective-permute-start.2) | collective-permute-done | bytes 409632 | tf_op jit(solution)/shard_map/ppermute | solution.py:25
  44.6 3.3 %collective-permute-done.3 = f32[800,128]{1,0:T(8,128)S(1)} collective-permute-done((f32[800,128]{1,0:T(8,128)S(1)}, f32[800,128]{1,0:T(8,128)S(1)}, u32[]{:S(2)}, u32[]{:S(2)}) %collective-permute-start.3) | collective-permute-done | bytes 409632 | tf_op jit(solution)/shard_map/ppermute | solution.py:25
  48.0 3.8 %collective-permute-start.6 = (f32[800,128]{1,0:T(8,128)S(1)}, f32[800,128]{1,0:T(8,128)S(1)}, u32[]{:S(2)}, u32[]{:S(2)}) collective-permute-start(f32[800,128]{1,0:T(8,128)S(1)} %add_add_fusion.m0), channel_id=1, source_target_pairs={{0,96},{4,100},{8,104},{12,108},{16,112},{20,116},{24,120},{28,124... | collective-permute-start | bytes 1228808 | tf_op jit(solution)/shard_map/ppermute | solution.py:29
  52.5 2.7 %collective-permute-start.13 = (f32[40,384]{1,0:T(8,128)S(1)}, f32[40,384]{1,0:T(8,128)S(1)}, u32[]{:S(2)}, u32[]{:S(2)}) collective-permute-start(f32[40,384]{1,0:T(8,128)S(1)} %add_add_fusion.1.p0), channel_id=1, source_target_pairs={{0,96},{4,100},{8,104},{12,108},{16,112},{20,116},{24,120},{28,124... | collective-permute-start | bytes 184328 | tf_op jit(solution)/shard_map/ppermute | solution.py:29
  55.2 16.1 %collective-permute-done.13.p3 = f32[40,384]{1,0:T(8,128)S(1)} collective-permute-done((f32[40,384]{1,0:T(8,128)S(1)}, f32[40,384]{1,0:T(8,128)S(1)}, u32[]{:S(2)}, u32[]{:S(2)}) %collective-permute-start.13) | collective-permute-done | bytes 61472 | tf_op jit(solution)/shard_map/ppermute | solution.py:29
  71.8 2.8 %collective-permute-done.11.p1 = f32[40,384]{1,0:T(8,128)S(1)} collective-permute-done((f32[40,384]{1,0:T(8,128)S(1)}, f32[40,384]{1,0:T(8,128)S(1)}, u32[]{:S(2)}, u32[]{:S(2)}) %collective-permute-start.11) | collective-permute-done | bytes 61472 | tf_op jit(solution)/shard_map/ppermute | solution.py:29
  75.1 2.6 %collective-permute-start.16 = (f32[32,384]{1,0:T(8,128)S(1)}, f32[32,384]{1,0:T(8,128)S(1)}, u32[]{:S(2)}, u32[]{:S(2)}) collective-permute-start(f32[32,384]{1,0:T(8,128)S(1)} %get-tuple-element.21.a0), channel_id=1, source_target_pairs={{0,3},{1,2},{2,1},{3,0},{4,7},{5,6},{6,5},{7,4},{8,11},{9,10},{10,... | collective-permute-start | bytes 147464 | tf_op jit(solution)/shard_map/ppermute | solution.py:33
  79.4 2.8 %collective-permute-done.15.a2 = f32[32,384]{1,0:T(8,128)S(1)} collective-permute-done((f32[32,384]{1,0:T(8,128)S(1)}, f32[32,384]{1,0:T(8,128)S(1)}, u32[]{:S(2)}, u32[]{:S(2)}) %collective-permute-start.15) | collective-permute-done | bytes 49184 | tf_op jit(solution)/shard_map/ppermute | solution.py:33
  82.2 3.0 %second_left.1.a0 = f32[32,384]{1,0:T(8,128)S(1)} custom-call(f32[32,384]{1,0:T(8,128)S(1)} %get-tuple-element.21.a0, f32[32,384]{1,0:T(8,128)S(1)} %collective-permute-done.14.a1, f32[32,384]{1,0:T(8,128)S(1)} %collective-permute-done.15.a2, f32[32,384]{1,0:T(8,128)S(1)} %collective-permute-done.16.a3, bf16[384,384]{1,0:T(8,128)(2,1)S(1)} %get-tuple-element.22.high_ref, ...), custom_call_target="tpu_custom_call" | custom-call | tf_op jit(solution)/shard_map/second_left/pallas_call | solution.py:233
  85.7 2.9 %collective-permute-start.17 = (f32[32,384]{1,0:T(8,128)S(1)}, f32[32,384]{1,0:T(8,128)S(1)}, u32[]{:S(2)}, u32[]{:S(2)}) collective-permute-start(f32[32,384]{1,0:T(8,128)S(1)} %second_left.1.a0), channel_id=1, source_target_pairs={{0,8},{4,12},{8,0},{12,4},{16,24},{20,28},{24,16},{28,20},{32,40},... | collective-permute-start | bytes 147464 | tf_op jit(solution)/shard_map/ppermute | solution.py:25
  90.5 3.1 %second_right.1 = (f32[32,384]{1,0:T(8,128)S(1)}, f32[32,384]{1,0:T(8,128)S(1)}) custom-call(f32[32,384]{1,0:T(8,128)S(1)} %second_left.1.a0, f32[32,384]{1,0:T(8,128)S(1)} %collective-permute-done.17.a1, f32[32,384]{1,0:T(8,128)S(1)} %collective-permute-done.18.a2, f32[32,384]{1,0:T(8,128)S(1)} %collective-permute-done.19.a3, ...), custom_call_target="tpu_custom_call" | custom-call | tf_op jit(solution)/shard_map/second_right/pallas_call | solution.py:233
  99.0 7.3 %collective-permute-start.23 = (f32[32,384]{1,0:T(8,128)S(1)}, f32[32,384]{1,0:T(8,128)S(1)}, u32[]{:S(2)}, u32[]{:S(2)}) collective-permute-start(f32[32,384]{1,0:T(8,128)S(1)} %add_add_fusion.2.refs_0_), channel_id=1, source_target_pairs={{0,4},{4,0},{8,12},{12,8},{16,20},{20,16},{24,28},{28,24},{32,36},... | collective-permute-start | bytes 147464 | tf_op jit(solution)/shard_map/ppermute | solution.py:21
  106.3 3.0 %solve.1.l_own = f32[32,384]{1,0:T(8,128)S(1)} custom-call(f32[32,384]{1,0:T(8,128)S(1)} %add_add_fusion.2.refs_0_, f32[32,384]{1,0:T(8,128)S(1)} %get-tuple-element.25.refs_1_), custom_call_target="tpu_custom_call" | custom-call | tf_op jit(solution)/shard_map/solve/pallas_call | solution.py:233
  109.4 1.9 %collective-permute-start.26 = (f32[64,384]{1,0:T(8,128)S(1)}, f32[64,384]{1,0:T(8,128)S(1)}, u32[]{:S(2)}, u32[]{:S(2)}) collective-permute-start(f32[64,384]{1,0:T(8,128)S(1)} %pad_maximum_fusion.g0), channel_id=1, source_target_pairs={{0,24},{4,28},{8,16},{12,20},{16,8},{20,12},{24,0},{28,4},{32,56},... | collective-permute-start | bytes 294920 | tf_op jit(solution)/shard_map/ppermute | solution.py:25
  114.6 1.8 %collective-permute-done.25.g2 = f32[64,384]{1,0:T(8,128)S(1)} collective-permute-done((f32[64,384]{1,0:T(8,128)S(1)}, f32[64,384]{1,0:T(8,128)S(1)}, u32[]{:S(2)}, u32[]{:S(2)}) %collective-permute-start.25) | collective-permute-done | bytes 98336 | tf_op jit(solution)/shard_map/ppermute | solution.py:25
  117.3 6.6 %finish.1 = (f32[2,320,1280]{2,1,0:T(8,128)}, f32[2,320,1280]{2,1,0:T(8,128)}, f32[2,320,1280]{2,1,0:T(8,128)}) custom-call(s32[2]{0:T(128)S(1)} %pad_add_fusion.where, f32[320,1280]{1,0:T(8,128)S(1)} %grad_own.1.a_ref.own, f32[320,1280]{1,0:T(8,128)S(1)} %grad_other.1.other, f32[64,384]{1,0:T(8,128)S(1)} %pad_maximum_fusion.g0, ...), custom_call_target="tpu_custom_call" | custom-call | tf_op jit(solution)/shard_map/finish/pallas_call | solution.py:271
  (68 shorter events, 25.9 us)
Async XLA Ops:
  9.6 10.6 %collective-permute-start = (f32[320,1280]{1,0:T(8,128)S(1)}, f32[320,1280]{1,0:T(8,128)}, u32[]{:S(2)}, u32[]{:S(2)}) collective-permute-start(f32[320,1280]{1,0:T(8,128)S(1)} %grad_other.1.other), channel_id=1, source_target_pairs={{0,4},{4,0},{8,12},{12,8},{16,20},{20,16},{24,28},{28,24},{32,36},... | collective-permute-start | bytes 4915208 | tf_op jit(solution)/shard_map/ppermute | solution.py:21
  22.1 11.2 %collective-permute-start.1 = (f32[800,128]{1,0:T(8,128)S(1)}, f32[800,128]{1,0:T(8,128)S(1)}, u32[]{:S(2)}, u32[]{:S(2)}) collective-permute-start(f32[800,128]{1,0:T(8,128)S(1)} %get-tuple-element.18.c1), channel_id=1, source_target_pairs={{0,8},{4,12},{8,0},{12,4},{16,24},{20,28},{24,16},{28,20},{32,40},... | collective-permute-start | bytes 1228808 | tf_op jit(solution)/shard_map/ppermute | solution.py:25
  23.6 21.0 %collective-permute-start.2 = (f32[800,128]{1,0:T(8,128)S(1)}, f32[800,128]{1,0:T(8,128)S(1)}, u32[]{:S(2)}, u32[]{:S(2)}) collective-permute-start(f32[800,128]{1,0:T(8,128)S(1)} %get-tuple-element.19.c2), channel_id=1, source_target_pairs={{0,16},{4,20},{8,24},{12,28},{16,0},{20,4},{24,8},{28,12},{32,48},... | collective-permute-start | bytes 1228808 | tf_op jit(solution)/shard_map/ppermute | solution.py:25
  26.2 21.7 %collective-permute-start.3 = (f32[800,128]{1,0:T(8,128)S(1)}, f32[800,128]{1,0:T(8,128)S(1)}, u32[]{:S(2)}, u32[]{:S(2)}) collective-permute-start(f32[800,128]{1,0:T(8,128)S(1)} %get-tuple-element.20.c3), channel_id=1, source_target_pairs={{0,24},{4,28},{8,16},{12,20},{16,8},{20,12},{24,0},{28,4},{32,56},... | collective-permute-start | bytes 1228808 | tf_op jit(solution)/shard_map/ppermute | solution.py:25
  29.1 22.7 %collective-permute-start.10 = (f32[40,384]{1,0:T(8,128)S(1)}, f32[40,384]{1,0:T(8,128)S(1)}, u32[]{:S(2)}, u32[]{:S(2)}) collective-permute-start(f32[40,384]{1,0:T(8,128)S(1)} %first_left.1), channel_id=1, source_target_pairs={{0,24},{4,28},{8,16},{12,20},{16,8},{20,12},{24,0},{28,4},{32,56},... | collective-permute-start | bytes 184328 | tf_op jit(solution)/shard_map/ppermute | solution.py:25
  32.0 20.5 %collective-permute-start.9 = (f32[40,384]{1,0:T(8,128)S(1)}, f32[40,384]{1,0:T(8,128)S(1)}, u32[]{:S(2)}, u32[]{:S(2)}) collective-permute-start(f32[40,384]{1,0:T(8,128)S(1)} %first_left.1), channel_id=1, source_target_pairs={{0,16},{4,20},{8,24},{12,28},{16,0},{20,4},{24,8},{28,12},{32,48},... | collective-permute-start | bytes 184328 | tf_op jit(solution)/shard_map/ppermute | solution.py:25
  33.3 19.3 %collective-permute-start.8 = (f32[40,384]{1,0:T(8,128)S(1)}, f32[40,384]{1,0:T(8,128)S(1)}, u32[]{:S(2)}, u32[]{:S(2)}) collective-permute-start(f32[40,384]{1,0:T(8,128)S(1)} %first_left.1), channel_id=1, source_target_pairs={{0,8},{4,12},{8,0},{12,4},{16,24},{20,28},{24,16},{28,20},{32,40},... | collective-permute-start | bytes 184328 | tf_op jit(solution)/shard_map/ppermute | solution.py:25
  48.0 26.6 %collective-permute-start.6 = (f32[800,128]{1,0:T(8,128)S(1)}, f32[800,128]{1,0:T(8,128)S(1)}, u32[]{:S(2)}, u32[]{:S(2)}) collective-permute-start(f32[800,128]{1,0:T(8,128)S(1)} %add_add_fusion.m0), channel_id=1, source_target_pairs={{0,96},{4,100},{8,104},{12,108},{16,112},{20,116},{24,120},{28,124... | collective-permute-start | bytes 1228808 | tf_op jit(solution)/shard_map/ppermute | solution.py:29
  51.8 22.8 %collective-permute-start.5 = (f32[800,128]{1,0:T(8,128)S(1)}, f32[800,128]{1,0:T(8,128)S(1)}, u32[]{:S(2)}, u32[]{:S(2)}) collective-permute-start(f32[800,128]{1,0:T(8,128)S(1)} %add_add_fusion.m0), channel_id=1, source_target_pairs={{0,64},{4,68},{8,72},{12,76},{16,80},{20,84},{24,88},{28,92},{32,9... | collective-permute-start | bytes 1228808 | tf_op jit(solution)/shard_map/ppermute | solution.py:29
  51.9 22.8 %collective-permute-start.4 = (f32[800,128]{1,0:T(8,128)S(1)}, f32[800,128]{1,0:T(8,128)S(1)}, u32[]{:S(2)}, u32[]{:S(2)}) collective-permute-start(f32[800,128]{1,0:T(8,128)S(1)} %add_add_fusion.m0), channel_id=1, source_target_pairs={{0,32},{4,36},{8,40},{12,44},{16,48},{20,52},{24,56},{28,60},{32,0... | collective-permute-start | bytes 1228808 | tf_op jit(solution)/shard_map/ppermute | solution.py:29
  52.5 18.7 %collective-permute-start.13 = (f32[40,384]{1,0:T(8,128)S(1)}, f32[40,384]{1,0:T(8,128)S(1)}, u32[]{:S(2)}, u32[]{:S(2)}) collective-permute-start(f32[40,384]{1,0:T(8,128)S(1)} %add_add_fusion.1.p0), channel_id=1, source_target_pairs={{0,96},{4,100},{8,104},{12,108},{16,112},{20,116},{24,120},{28,124... | collective-permute-start | bytes 184328 | tf_op jit(solution)/shard_map/ppermute | solution.py:29
  55.2 16.6 %collective-permute-start.12 = (f32[40,384]{1,0:T(8,128)S(1)}, f32[40,384]{1,0:T(8,128)S(1)}, u32[]{:S(2)}, u32[]{:S(2)}) collective-permute-start(f32[40,384]{1,0:T(8,128)S(1)} %add_add_fusion.1.p0), channel_id=1, source_target_pairs={{0,64},{4,68},{8,72},{12,76},{16,80},{20,84},{24,88},{28,92},{32,9... | collective-permute-start | bytes 184328 | tf_op jit(solution)/shard_map/ppermute | solution.py:29
  75.1 4.2 %collective-permute-start.16 = (f32[32,384]{1,0:T(8,128)S(1)}, f32[32,384]{1,0:T(8,128)S(1)}, u32[]{:S(2)}, u32[]{:S(2)}) collective-permute-start(f32[32,384]{1,0:T(8,128)S(1)} %get-tuple-element.21.a0), channel_id=1, source_target_pairs={{0,3},{1,2},{2,1},{3,0},{4,7},{5,6},{6,5},{7,4},{8,11},{9,10},{10,... | collective-permute-start | bytes 147464 | tf_op jit(solution)/shard_map/ppermute | solution.py:33
  77.7 4.5 %collective-permute-start.15 = (f32[32,384]{1,0:T(8,128)S(1)}, f32[32,384]{1,0:T(8,128)S(1)}, u32[]{:S(2)}, u32[]{:S(2)}) collective-permute-start(f32[32,384]{1,0:T(8,128)S(1)} %get-tuple-element.21.a0), channel_id=1, source_target_pairs={{0,2},{1,3},{2,0},{3,1},{4,6},{5,7},{6,4},{7,5},{8,10},{9,11},{10,... | collective-permute-start | bytes 147464 | tf_op jit(solution)/shard_map/ppermute | solution.py:33
  85.2 4.8 %collective-permute-start.19 = (f32[32,384]{1,0:T(8,128)S(1)}, f32[32,384]{1,0:T(8,128)S(1)}, u32[]{:S(2)}, u32[]{:S(2)}) collective-permute-start(f32[32,384]{1,0:T(8,128)S(1)} %second_left.1.a0), channel_id=1, source_target_pairs={{0,24},{4,28},{8,16},{12,20},{16,8},{20,12},{24,0},{28,4},{32,56},... | collective-permute-start | bytes 147464 | tf_op jit(solution)/shard_map/ppermute | solution.py:25
  85.4 4.6 %collective-permute-start.18 = (f32[32,384]{1,0:T(8,128)S(1)}, f32[32,384]{1,0:T(8,128)S(1)}, u32[]{:S(2)}, u32[]{:S(2)}) collective-permute-start(f32[32,384]{1,0:T(8,128)S(1)} %second_left.1.a0), channel_id=1, source_target_pairs={{0,16},{4,20},{8,24},{12,28},{16,0},{20,4},{24,8},{28,12},{32,48},... | collective-permute-start | bytes 147464 | tf_op jit(solution)/shard_map/ppermute | solution.py:25
  85.7 4.9 %collective-permute-start.17 = (f32[32,384]{1,0:T(8,128)S(1)}, f32[32,384]{1,0:T(8,128)S(1)}, u32[]{:S(2)}, u32[]{:S(2)}) collective-permute-start(f32[32,384]{1,0:T(8,128)S(1)} %second_left.1.a0), channel_id=1, source_target_pairs={{0,8},{4,12},{8,0},{12,4},{16,24},{20,28},{24,16},{28,20},{32,40},... | collective-permute-start | bytes 147464 | tf_op jit(solution)/shard_map/ppermute | solution.py:25
  93.7 4.2 %collective-permute-start.22 = (f32[32,384]{1,0:T(8,128)S(1)}, f32[32,384]{1,0:T(8,128)S(1)}, u32[]{:S(2)}, u32[]{:S(2)}) collective-permute-start(f32[32,384]{1,0:T(8,128)S(1)} %get-tuple-element.24), channel_id=1, source_target_pairs={{0,3},{1,2},{2,1},{3,0},{4,7},{5,6},{6,5},{7,4},{8,11},{9,10},{10,... | collective-permute-start | bytes 147464 | tf_op jit(solution)/shard_map/ppermute | solution.py:33
  94.6 4.4 %collective-permute-start.21 = (f32[32,384]{1,0:T(8,128)S(1)}, f32[32,384]{1,0:T(8,128)S(1)}, u32[]{:S(2)}, u32[]{:S(2)}) collective-permute-start(f32[32,384]{1,0:T(8,128)S(1)} %get-tuple-element.24), channel_id=1, source_target_pairs={{0,2},{1,3},{2,0},{3,1},{4,6},{5,7},{6,4},{7,5},{8,10},{9,11},{10,... | collective-permute-start | bytes 147464 | tf_op jit(solution)/shard_map/ppermute | solution.py:33
  99.0 10.4 %collective-permute-start.23 = (f32[32,384]{1,0:T(8,128)S(1)}, f32[32,384]{1,0:T(8,128)S(1)}, u32[]{:S(2)}, u32[]{:S(2)}) collective-permute-start(f32[32,384]{1,0:T(8,128)S(1)} %add_add_fusion.2.refs_0_), channel_id=1, source_target_pairs={{0,4},{4,0},{8,12},{12,8},{16,20},{20,16},{24,28},{28,24},{32,36},... | collective-permute-start | bytes 147464 | tf_op jit(solution)/shard_map/ppermute | solution.py:21
  109.3 4.1 %collective-permute-start.27 = (f32[32,384]{1,0:T(8,128)S(1)}, f32[32,384]{1,0:T(8,128)S(1)}, u32[]{:S(2)}, u32[]{:S(2)}) collective-permute-start(f32[32,384]{1,0:T(8,128)S(1)} %solve.1.l_own), channel_id=1, source_target_pairs={{0,4},{4,0},{8,12},{12,8},{16,20},{20,16},{24,28},{28,24},{32,36},... | collective-permute-start | bytes 147464 | tf_op jit(solution)/shard_map/ppermute | solution.py:21
  109.4 5.2 %collective-permute-start.26 = (f32[64,384]{1,0:T(8,128)S(1)}, f32[64,384]{1,0:T(8,128)S(1)}, u32[]{:S(2)}, u32[]{:S(2)}) collective-permute-start(f32[64,384]{1,0:T(8,128)S(1)} %pad_maximum_fusion.g0), channel_id=1, source_target_pairs={{0,24},{4,28},{8,16},{12,20},{16,8},{20,12},{24,0},{28,4},{32,56},... | collective-permute-start | bytes 294920 | tf_op jit(solution)/shard_map/ppermute | solution.py:25
  111.4 5.0 %collective-permute-start.25 = (f32[64,384]{1,0:T(8,128)S(1)}, f32[64,384]{1,0:T(8,128)S(1)}, u32[]{:S(2)}, u32[]{:S(2)}) collective-permute-start(f32[64,384]{1,0:T(8,128)S(1)} %pad_maximum_fusion.g0), channel_id=1, source_target_pairs={{0,16},{4,20},{8,24},{12,28},{16,0},{20,4},{24,8},{28,12},{32,48},... | collective-permute-start | bytes 294920 | tf_op jit(solution)/shard_map/ppermute | solution.py:25
  112.5 4.8 %collective-permute-start.24 = (f32[64,384]{1,0:T(8,128)S(1)}, f32[64,384]{1,0:T(8,128)S(1)}, u32[]{:S(2)}, u32[]{:S(2)}) collective-permute-start(f32[64,384]{1,0:T(8,128)S(1)} %pad_maximum_fusion.g0), channel_id=1, source_target_pairs={{0,8},{4,12},{8,0},{12,4},{16,24},{20,28},{24,16},{28,20},{32,40},... | collective-permute-start | bytes 294920 | tf_op jit(solution)/shard_map/ppermute | solution.py:25
  (14 other events, 378.5 us)

commit v3 on v2

v3 whole, which is shorter than its diff:
```python
import math

import jax
import jax.numpy as jnp
from jax import lax
from jax.experimental import pallas as pl
from jax.experimental.pallas import tpu as pltpu
from jax.sharding import PartitionSpec as P

F32 = jnp.float32
BF16 = jnp.bfloat16
HIGH = lax.Precision.HIGHEST
NN = (((1,), (0,)), ((), ()))
NT = (((1,), (1,)), ((), ()))
TN = (((0,), (0,)), ((), ()))

CORE = [(r, r ^ 1) for r in range(32)]


def swap_core(value):
    return lax.ppermute(value, "replica", CORE)


def swap_y(value, k):
    return lax.ppermute(value, "replica", [(r, r ^ (k << 1)) for r in range(32)])


def swap_z(value, k):
    return lax.ppermute(value, "replica", [(r, r ^ (k << 3)) for r in range(32)])


def swap_x(value, k):
    return lax.ppermute(value, "shard", [(s, s ^ k) for s in range(4)])


def fan(value, swap):
    return [value] + [swap(value, k) for k in (1, 2, 3)]


def add4(parts):
    return (parts[0] + parts[1]) + (parts[2] + parts[3])


def dot(a, b, dims, precision=None):
    return lax.dot_general(a, b, dims, precision=precision, preferred_element_type=F32)


def split(value):
    high = value.astype(BF16)
    return high, (value - high.astype(F32)).astype(BF16)


def dot3(a, b_high, b_low, dims):
    high, low = split(a)
    rows = a.shape[0]
    top = dot(jnp.concatenate([high, low], axis=0), b_high, dims)
    return top[:rows] + (top[rows:] + dot(high, b_low, dims))


def lanes(shape):
    return lax.broadcasted_iota(jnp.int32, shape, 1)


def unpack(chunk):
    half = chunk[640:800]
    half = jnp.concatenate([half, pltpu.roll(half, 64, 1)], axis=0)
    half = jnp.where(lanes(half.shape) < 64, half, 0.0)
    return jnp.concatenate([chunk[:320], chunk[320:640], half], axis=1)


def grad_kernel(which, a_hbm, c_hbm, e_hbm, out_ref, a_buf, c_buf, e_buf, a_sem, c_sem, e_sem, *, scale, step, ahead):
    mat = which[0]
    blocks = [pl.ds(at, step) for at in range(0, c_buf.shape[0], step)]
    lhs = [pltpu.make_async_copy(a_hbm.at[mat, :, b], a_buf.at[:, b], a_sem.at[j]) for j, b in enumerate(blocks)]
    rhs = [pltpu.make_async_copy(c_hbm.at[mat, b], c_buf.at[b], c_sem.at[j]) for j, b in enumerate(blocks)]
    kept = pltpu.make_async_copy(e_hbm.at[mat], e_buf, e_sem)
    last = len(blocks) - 1

    def start(j):
        if j <= last:
            lhs[j].start()
            rhs[j].start()
        if j == last:
            kept.start()

    for j in range(ahead):
        start(j)
    for j, b in enumerate(blocks):
        lhs[j].wait()
        rhs[j].wait()
        start(j + ahead)
        value = dot(a_buf[:, b], c_buf[b], NN)
        if j == last:
            kept.wait()
            out_ref[...] = (out_ref[...] + value) * scale + e_buf[...]
        elif j > 0:
            out_ref[...] = out_ref[...] + value
        else:
            out_ref[...] = value


AHEAD = 448
REST = 800 - AHEAD


def route_kernel(where, a_ref, b_ref, q_hbm, v_ref, o0, o1, o2, o3, r0, r1, r2, r3, stage, both, q_buf, q_sem):
    core, y = where[0], where[1]
    fetch = pltpu.make_async_copy(q_hbm.at[core], q_buf, q_sem)
    fetch.start()
    left = lanes((160, 128)) < 64
    for i in range(2):
        tiles = []
        for t in range(5):
            at = 640 * i + 128 * t
            tiles.append(a_ref[:, at:at + 128] + b_ref[:, at:at + 128])
            both[0:320, at:at + 128] = tiles[-1]
        middle = tiles[2]
        rolled = pltpu.roll(middle, 64, 1)
        stage[2 * i, 0:320] = tiles[0]
        stage[2 * i, 320:640] = tiles[1]
        stage[2 * i, 640:800] = jnp.where(left, middle[:160], rolled[160:])
        stage[2 * i + 1, 0:320] = tiles[3]
        stage[2 * i + 1, 320:640] = tiles[4]
        stage[2 * i + 1, 640:800] = jnp.where(left, rolled[:160], middle[160:])
    both[320:384] = jnp.zeros((64, both.shape[1]), F32)
    for k, (out, rest) in enumerate(((o0, r0), (o1, r1), (o2, r2), (o3, r3))):
        out[...] = stage[y ^ k, 0:AHEAD]
        rest[0:REST] = stage[y ^ k, AHEAD:800]
    fetch.wait()
    high, low = split(both[...])
    total = dot3(q_buf[...], high, low, NT)
    for rest in (r0, r1, r2, r3):
        rest[REST:REST + 32] = total[:, 0:128]
        rest[REST + 32:REST + 64] = total[:, 128:256]
        rest[REST + 64:REST + 96] = total[:, 256:384] + v_ref[...]


def eliminate(tile):
    lane = lanes((32, 128))
    row = lax.broadcasted_iota(jnp.int32, (32, 128), 0)
    gram = jnp.where((lane >= 64) & (lane < 96), tile, 0.0)
    diagonal = jnp.where(lane == row + 64, gram, 0.0)
    down = lax.rsqrt(jnp.sum(diagonal, axis=1, keepdims=True))
    across = jnp.sum(diagonal, axis=0, keepdims=True)
    across = lax.rsqrt(jnp.where((lane[0:1] >= 64) & (lane[0:1] < 96), across, 1.0))
    work = gram * down * across + jnp.where(lane == row + 96, down, 0.0)
    for k in range(0, 32, 2):
        col0 = jnp.broadcast_to(work[:, 64 + k:65 + k], (32, 128))
        col1 = jnp.broadcast_to(work[:, 65 + k:66 + k], (32, 128))
        a, b, c = col0[k:k + 1], col0[k + 1:k + 2], col1[k + 1:k + 2]
        row0, row1 = work[k:k + 1], work[k + 1:k + 2]
        inverse = 1.0 / (a * c - b * b)
        step0 = (c * row0 - b * row1) * inverse
        step1 = (a * row1 - b * row0) * inverse
        second = jnp.where(row == k + 1, (b * (1.0 / a)) * row0, 0.0)
        work = work - jnp.where(row > k + 1, col0 * step0 + col1 * step1, second)
    pivots = jnp.sum(jnp.where(lane == row + 64, work, 0.0), axis=1, keepdims=True)
    return jnp.where(lane >= 96, work, 0.0), pivots


def below(value):
    return jnp.concatenate([jnp.zeros((96, value.shape[1]), F32), value], axis=0)


def payload(value):
    return jnp.where(lanes(value.shape) < 320, value, 0.0)


def orth(packed):
    inverse, pivots = eliminate(packed[:, 256:384])
    return dot(inverse * lax.rsqrt(pivots), below(payload(packed)), NN, HIGH)


def to_right(left, w_high, w_low):
    out = dot3(left, w_high, w_low, NN)
    zero = jnp.zeros((64, left.shape[1]), F32)
    shifted = jnp.concatenate([zero, left, zero[:32]], axis=0)
    gram = dot(left, shifted, NT, HIGH)
    return jnp.concatenate([out[:, :256], out[:, 256:] + gram], axis=1)


def wide_kernel(m0, m1, m2, m3, p0, p1, p2, p3, high_ref, low_ref, out_ref, vec_ref):
    tail = (p0[...] + p1[...]) + (p2[...] + p3[...])
    whole = unpack(jnp.concatenate([(m0[...] + m1[...]) + (m2[...] + m3[...]), tail[:REST]], axis=0))
    high, low = split(whole)
    zero = jnp.zeros((64, 384), BF16)
    high_ref[...] = jnp.concatenate([high, zero], axis=0)
    low_ref[...] = jnp.concatenate([low, zero], axis=0)
    vec_ref[...] = tail[REST + 64:REST + 96]
    left = payload(jnp.concatenate([tail[REST:REST + 32], tail[REST + 32:REST + 64], tail[REST + 64:REST + 96]], axis=1))
    out_ref[...] = to_right(left, high_ref[...], low_ref[...])


def left_kernel(a0, a1, a2, a3, high_ref, low_ref, out_ref):
    right = orth((a0[...] + a1[...]) + (a2[...] + a3[...]))
    high, low = split(right)
    zero = jnp.zeros((32, 384), BF16)
    w_high = jnp.concatenate([high_ref[0:320], high, zero], axis=0)
    w_low = jnp.concatenate([low_ref[0:320], low, zero], axis=0)
    out_ref[...] = dot3(right, w_high, w_low, NT)


def right_kernel(a0, a1, a2, a3, high_ref, low_ref, left_ref, out_ref):
    left = orth((a0[...] + a1[...]) + (a2[...] + a3[...]))
    left_ref[...] = left
    out_ref[...] = to_right(left, high_ref[...], low_ref[...])


def solve_kernel(packed_ref, left_ref, w_hbm, m_hbm, out_ref, w_out, m_out, sems, *, scale):
    one = pltpu.make_async_copy(w_hbm, w_out, sems.at[0])
    two = pltpu.make_async_copy(m_hbm, m_out, sems.at[1])
    one.start()
    two.start()
    inverse, pivots = eliminate(packed_ref[0:32, 256:384])
    once = dot(inverse, below(left_ref[...]), NN, HIGH) * (scale / pivots)
    out_ref[...] = dot(inverse, once, TN, HIGH)[96:128]
    one.wait()
    two.wait()


def final_kernel(where, own, other, g0, g1, g2, g3, l_own, l_other, w_ref, m_ref,
                 e_hbm, w_hbm, m_hbm, stage, e_buf, w_buf, m_buf, sems, *, blocks):
    core, y = where[0], where[1]
    size = own.shape[0] // blocks
    side = lanes((32, 128)) < 64
    copies = []
    for slot, (full, left_ref) in enumerate(((own, l_own), (other, l_other))):
        mat = core ^ slot
        for k, g in enumerate((g0, g1, g2, g3)):
            stage[y ^ k] = g[32 * slot:32 * slot + 32]
        tiles = []
        for i in range(2):
            even, odd = stage[2 * i], stage[2 * i + 1]
            middle = jnp.where(side, even[:, 256:], pltpu.roll(odd[:, 256:], 64, 1))
            tiles += [even[:, :256], middle, odd[:, :256]]
        r_high, r_low = split(jnp.concatenate(tiles, axis=1))
        l_high, l_low = split(left_ref[...])
        rights = jnp.concatenate([r_high, r_low, r_high], axis=0)
        lefts = jnp.concatenate([l_high, l_high, l_low], axis=0).T
        for block in range(blocks):
            rows = slice(block * size, block * size + size)
            part = dot(lefts[rows], rights, NN)
            e_buf[slot, rows] = full[rows] - part
            moved = 0.9 * m_ref[mat, rows] + part
            m_buf[slot, rows] = moved
            w_buf[slot, rows] = w_ref[mat, rows] - 0.1 * moved
            for j, (buf, hbm) in enumerate(((e_buf, e_hbm), (m_buf, m_hbm), (w_buf, w_hbm))):
                copies.append(pltpu.make_async_copy(buf.at[slot, rows], hbm.at[mat, rows], sems.at[slot, block, j]))
                copies[-1].start()
    for copy in copies:
        copy.wait()


VM = pl.BlockSpec(memory_space=pltpu.VMEM)
SM = pl.BlockSpec(memory_space=pltpu.SMEM)


def limit(mebi):
    return pltpu.CompilerParams(vmem_limit_bytes=mebi << 20)


def shaped(shape, dtype=F32):
    return jax.ShapeDtypeStruct(shape, dtype)


def call(kernel, args, outs, specs, scratch=(), name=None):
    many = isinstance(outs, (list, tuple))
    return pl.pallas_call(
        kernel,
        out_shape=outs,
        in_specs=specs,
        out_specs=[VM] * len(outs) if many else VM,
        scratch_shapes=list(scratch),
        compiler_params=limit(12),
        name=name,
    )(*args)


def gradients(which, acts, cots, errors, scale, name):
    mats, rows, toks = acts.shape
    cols = cots.shape[2]
    step = 512
    inputs = [pltpu.with_memory_space_constraint(value, pltpu.HBM) for value in (acts, cots, errors)]
    return pl.pallas_call(
        lambda *refs: grad_kernel(*refs, scale=scale, step=step, ahead=3),
        out_shape=shaped((rows, cols)),
        in_specs=[SM] + [pl.BlockSpec(memory_space=pltpu.HBM)] * 3,
        out_specs=VM,
        scratch_shapes=[
            pltpu.VMEM((rows, toks), BF16),
            pltpu.VMEM((toks, cols), BF16),
            pltpu.VMEM((rows, cols), F32),
            pltpu.SemaphoreType.DMA((toks // step,)),
            pltpu.SemaphoreType.DMA((toks // step,)),
            pltpu.SemaphoreType.DMA(()),
        ],
        compiler_params=limit(16),
        name=name,
    )(which, *inputs)


def finish(where, own, other, rights, l_own, l_other, weights, momentum):
    blocks = 4
    hbm = pl.BlockSpec(memory_space=pltpu.HBM)
    return pl.pallas_call(
        lambda *refs: final_kernel(*refs, blocks=blocks),
        out_shape=[shaped(weights.shape)] * 3,
        in_specs=[SM] + [VM] * 10,
        out_specs=[hbm] * 3,
        scratch_shapes=[pltpu.VMEM((4, 32, 384), F32)] + [pltpu.VMEM(weights.shape, F32)] * 3
        + [pltpu.SemaphoreType.DMA((2, blocks, 3))],
        compiler_params=limit(24),
        name="finish",
    )(where, own, other, *rights, l_own, l_other, weights, momentum)


def body(acts, cots, errors, weights, momentum, start_q, vec_grads, vec_weights, vec_momentum):
    scale = 1.0 / math.sqrt(acts.shape[1])
    replicas = float(lax.axis_size("replica"))
    index = lax.axis_index("replica")
    core = index & 1
    y = (index >> 1) & 3
    where = jnp.stack([core, y]).astype(jnp.int32)
    acts = acts.swapaxes(1, 2)

    vec_core = vec_grads[0] + swap_core(vec_grads[0])
    other = gradients(1 - where[:1], acts, cots, errors[0], scale, "grad_other")
    own = gradients(where[:1], acts, cots, errors[0], scale, "grad_own")
    vec_core = jnp.pad(vec_core.reshape(20, 64), ((0, 12), (64, 0)))
    hbm = pl.BlockSpec(memory_space=pltpu.HBM)
    in_hbm = lambda value: pltpu.with_memory_space_constraint(value, pltpu.HBM)
    sends = call(route_kernel, (where, own, swap_core(other), in_hbm(start_q.swapaxes(1, 2)), vec_core),
                 [shaped((AHEAD, 128))] * 4 + [shaped((REST + 96, 128))] * 4, [SM, VM, VM, hbm, VM],
                 [pltpu.VMEM((4, 800, 128), F32), pltpu.VMEM((384, 1280), F32), pltpu.VMEM((32, 1280), F32),
                  pltpu.SemaphoreType.DMA(())], name="route")
    ahead = add4([sends[0]] + [swap_y(sends[k], k) for k in (1, 2, 3)])
    behind = add4([sends[4]] + [swap_y(sends[4 + k], k) for k in (1, 2, 3)])
    w_high, w_low, packed, vec_sum = call(
        wide_kernel, (*fan(ahead, swap_z), *fan(behind, swap_z)),
        [shaped((384, 384), BF16), shaped((384, 384), BF16), shaped((32, 384)), shaped((32, 128))],
        [VM] * 8, name="first_right")
    packed = call(left_kernel, (*fan(packed, swap_x), w_high, w_low), shaped((32, 384)), [VM] * 6, name="second_left")
    left, packed = call(right_kernel, (*fan(packed, swap_y), w_high, w_low), [shaped((32, 384))] * 2, [VM] * 6,
                        name="second_right")
    packed = add4(fan(packed, swap_x))
    rights = fan(jnp.concatenate([packed, swap_core(packed)], axis=0), swap_y)
    held = pltpu.VMEM(weights.shape, F32)
    l_own, weights, momentum = call(
        lambda *refs: solve_kernel(*refs, scale=1.0 / replicas), (rights[0], left, in_hbm(weights), in_hbm(momentum)),
        [shaped((32, 384)), held, held], [VM, VM, hbm, hbm], [pltpu.SemaphoreType.DMA((2,))], name="solve")
    new_errors, new_weights, new_momentum = finish(where, own, other, rights, l_own, swap_core(l_own), weights, momentum)
    vec_moved = 0.9 * vec_momentum + vec_sum[:20, 64:].reshape(4, 320) / replicas
    return (new_errors[None], new_weights, new_momentum, vec_weights - 0.1 * vec_moved, vec_moved)


def solution(mesh):
    placed = (
        P(None, "replica", "shard"),
        P(None, "replica", None),
        P("replica", None, "shard", None),
        P(None, "shard", None),
        P(None, "shard", None),
        P(),
        P("replica", None, "shard"),
        P(None, "shard"),
        P(None, "shard"),
    )
    return jax.shard_map(
        body,
        mesh=mesh,
        in_specs=placed,
        out_specs=(
            P("replica", None, "shard", None),
            P(None, "shard", None),
            P(None, "shard", None),
            P(None, "shard"),
            P(None, "shard"),
        ),
        check_vma=False,
    )
```

time: 125 us -> 98 us (0.78)
  waiting for transfers between devices: 46.5 us -> 29.7 us
  local copies, waits for them, and re-layouts: 7.37 us -> 0.25 us
  Pallas kernels: 30 us -> 24 us
  starting transfers between devices: 38.4 us -> 42.1 us
    ppermute x6, waiting for transfers between devices: 19.4 us -> 9.03 us  [swap_z(): return lax.ppermute(value, 'replica', [(r, r ^ k << 3) for r in range(32)])]
    unnamed x20 -> x6, local copies, waits for them, and re-layouts: 7.37 us -> 0.01 us
    ppermute x12, waiting for transfers between devices: 20.5 us -> 14 us  [swap_y(): return lax.ppermute(value, 'replica', [(r, r ^ k << 1) for r in range(32)])]
    pallas_call x3, Pallas kernels: 17.2 us -> 13.2 us  [the longest x2 8.38 us: gradients(): pl.pallas_call(lambda *refs: grad_kernel(*refs, scale=scale, step=step, a...]
    pallas_call x6 -> x5, Pallas kernels: 12.8 us -> 10.9 us  [call(): pl.pallas_call(kernel, out_shape=outs, in_specs=specs, out_specs=[VM] * l...]
    ppermute x6, starting transfers between devices: 7.17 us -> 9.01 us  [swap_z(): return lax.ppermute(value, 'replica', [(r, r ^ k << 3) for r in range(32)])]
    ppermute x12, starting transfers between devices: 15 us -> 16.3 us  [swap_y(): return lax.ppermute(value, 'replica', [(r, r ^ k << 1) for r in range(32)])]
  transfers between devices with their start and end apart: 28 -> 28, of which waited for: 16 -> 13; matrix products, arithmetic and copies ran while one was open for 1% -> 1% of each run, Pallas kernels for 8% -> 7%
where the time goes in v3:
time: 98 us; the launch traced here: 97.9 us
  starting transfers between devices  42.1 us (43%)
  waiting for transfers between devices  29.7 us (30%)
  Pallas kernels  24 us (24%)
    ppermute x12, starting transfers between devices, swap_y(): return lax.ppermute(value, 'replica', [(r, r ^ k << 1) for r in range(32)])  16.3 us
    ppermute x12, waiting for transfers between devices, swap_y(): return lax.ppermute(value, 'replica', [(r, r ^ k << 1) for r in range(32)])  14 us
    pallas_call x5, Pallas kernels, call(): pl.pallas_call(kernel, out_shape=outs, in_specs=specs, out_specs=[VM] * l...  10.9 us
    ppermute x4, starting transfers between devices, swap_core(): return lax.ppermute(value, 'replica', CORE)  10.1 us
    ppermute x6, waiting for transfers between devices, swap_z(): return lax.ppermute(value, 'replica', [(r, r ^ k << 3) for r in range(32)])  9.03 us
    ppermute x6, starting transfers between devices, swap_z(): return lax.ppermute(value, 'replica', [(r, r ^ k << 3) for r in range(32)])  9.01 us
    pallas_call x2, Pallas kernels, gradients(): pl.pallas_call(lambda *refs: grad_kernel(*refs, scale=scale, step=step, a...  8.38 us
    ppermute x6, starting transfers between devices, swap_x(): return lax.ppermute(value, 'shard', [(s, s ^ k) for s in range(4)])  6.67 us
  transfers between devices with their start and end apart: 28, of which 13 were waited for; matrix products, arithmetic and copies ran while one was open for 1% of the time, Pallas kernels for 7%

profile of v3, /device:TPU:1, one launch (start us, length us, event | category | flops | bytes accessed | tf_op | source)
XLA Modules:
  0.0 97.9 jit_solution(11699189509740896463)
XLA Ops:
  0.6 4.2 %grad_other.1.refs_2_ = f32[320,1280]{1,0:T(8,128)S(1)} custom-call(s32[1]{0:T(128)S(6)} %sub.6.refs_0_, bf16[2,320,2048]{2,1,0:T(8,128)(2,1)} %bitcast.10, bf16[2,2048,1280]{2,1,0:T(8,128)(2,1)} %refs_2_.4, f32[2,320,1280]{2,1,0:T(8,128)} %bitcast.8), custom_call_target="tpu_custom_call" | custom-call | tf_op jit(solution)/shard_map/grad_other/pallas_call | solution.py:284
  4.8 1.5 %collective-permute-start = (f32[320,1280]{1,0:T(8,128)S(1)}, f32[320,1280]{1,0:T(8,128)}, u32[]{:S(2)}, u32[]{:S(2)}) collective-permute-start(f32[320,1280]{1,0:T(8,128)S(1)} %grad_other.1.refs_2_), channel_id=1, source_target_pairs={{0,4},{4,0},{8,12},{12,8},{16,20},{20,16},{24,28},{28,24},{32,36},... | collective-permute-start | bytes 4915208 | tf_op jit(solution)/shard_map/ppermute | solution.py:21
  6.5 4.2 %grad_own.1.a_ref.refs_1_ = f32[320,1280]{1,0:T(8,128)S(1)} custom-call(s32[1]{0:T(128)} %bitcast.refs_0_, bf16[2,320,2048]{2,1,0:T(8,128)(2,1)} %bitcast.11, bf16[2,2048,1280]{2,1,0:T(8,128)(2,1)} %refs_2_.4, f32[2,320,1280]{2,1,0:T(8,128)} %bitcast.9), custom_call_target="tpu_custom_call" | custom-call | tf_op jit(solution)/shard_map/grad_own/pallas_call | solution.py:284
  10.9 3.1 %route.1 = (f32[448,128]{1,0:T(8,128)S(1)}, f32[448,128]{1,0:T(8,128)S(1)}, f32[448,128]{1,0:T(8,128)S(1)}, f32[448,128]{1,0:T(8,128)S(1)}, f32[448,128]{1,0:T(8...) custom-call(s32[2]{0:T(128)S(1)} %pad_add_fusion.where.refs_0_, ...), custom_call_target="tpu_custom_call" | custom-call | tf_op jit(solution)/shard_map/route/pallas_call | solution.py:268
  14.0 1.5 %collective-permute-start.2 = (f32[448,128]{1,0:T(8,128)S(1)}, f32[448,128]{1,0:T(8,128)S(1)}, u32[]{:S(2)}, u32[]{:S(2)}) collective-permute-start(f32[448,128]{1,0:T(8,128)S(1)} %get-tuple-element.26), channel_id=1, source_target_pairs={{0,8},{4,12},{8,0},{12,4},{16,24},{20,28},{24,16},{28,20},{32,40},... | collective-permute-start | bytes 688136 | tf_op jit(solution)/shard_map/ppermute | solution.py:25
  15.5 2.6 %collective-permute-start.3 = (f32[448,128]{1,0:T(8,128)S(1)}, f32[448,128]{1,0:T(8,128)S(1)}, u32[]{:S(2)}, u32[]{:S(2)}) collective-permute-start(f32[448,128]{1,0:T(8,128)S(1)} %get-tuple-element.27), channel_id=1, source_target_pairs={{0,16},{4,20},{8,24},{12,28},{16,0},{20,4},{24,8},{28,12},{32,48},... | collective-permute-start | bytes 688136 | tf_op jit(solution)/shard_map/ppermute | solution.py:25
  18.1 3.8 %collective-permute-start.9 = (f32[448,128]{1,0:T(8,128)S(1)}, f32[448,128]{1,0:T(8,128)S(1)}, u32[]{:S(2)}, u32[]{:S(2)}) collective-permute-start(f32[448,128]{1,0:T(8,128)S(1)} %get-tuple-element.31), channel_id=1, source_target_pairs={{0,16},{4,20},{8,24},{12,28},{16,0},{20,4},{24,8},{28,12},{32,48},... | collective-permute-start | bytes 688136 | tf_op jit(solution)/shard_map/ppermute | solution.py:25
  21.9 1.7 %collective-permute-start.10 = (f32[448,128]{1,0:T(8,128)S(1)}, f32[448,128]{1,0:T(8,128)S(1)}, u32[]{:S(2)}, u32[]{:S(2)}) collective-permute-start(f32[448,128]{1,0:T(8,128)S(1)} %get-tuple-element.32), channel_id=1, source_target_pairs={{0,24},{4,28},{8,16},{12,20},{16,8},{20,12},{24,0},{28,4},{32,56},... | collective-permute-start | bytes 688136 | tf_op jit(solution)/shard_map/ppermute | solution.py:25
  23.7 4.7 %collective-permute-done.3 = f32[448,128]{1,0:T(8,128)S(1)} collective-permute-done((f32[448,128]{1,0:T(8,128)S(1)}, f32[448,128]{1,0:T(8,128)S(1)}, u32[]{:S(2)}, u32[]{:S(2)}) %collective-permute-start.3) | collective-permute-done | bytes 229408 | tf_op jit(solution)/shard_map/ppermute | solution.py:25
  28.3 2.0 %collective-permute-done.4 = f32[448,128]{1,0:T(8,128)S(1)} collective-permute-done((f32[448,128]{1,0:T(8,128)S(1)}, f32[448,128]{1,0:T(8,128)S(1)}, u32[]{:S(2)}, u32[]{:S(2)}) %collective-permute-start.4) | collective-permute-done | bytes 229408 | tf_op jit(solution)/shard_map/ppermute | solution.py:25
  30.4 3.8 %collective-permute-start.7 = (f32[448,128]{1,0:T(8,128)S(1)}, f32[448,128]{1,0:T(8,128)S(1)}, u32[]{:S(2)}, u32[]{:S(2)}) collective-permute-start(f32[448,128]{1,0:T(8,128)S(1)} %add_add_fusion.1.m0), channel_id=1, source_target_pairs={{0,96},{4,100},{8,104},{12,108},{16,112},{20,116},{24,120},{28,124... | collective-permute-start | bytes 688136 | tf_op jit(solution)/shard_map/ppermute | solution.py:29
  34.9 3.3 %collective-permute-done.9 = f32[448,128]{1,0:T(8,128)S(1)} collective-permute-done((f32[448,128]{1,0:T(8,128)S(1)}, f32[448,128]{1,0:T(8,128)S(1)}, u32[]{:S(2)}, u32[]{:S(2)}) %collective-permute-start.9) | collective-permute-done | bytes 229408 | tf_op jit(solution)/shard_map/ppermute | solution.py:25
  38.2 2.0 %collective-permute-done.10 = f32[448,128]{1,0:T(8,128)S(1)} collective-permute-done((f32[448,128]{1,0:T(8,128)S(1)}, f32[448,128]{1,0:T(8,128)S(1)}, u32[]{:S(2)}, u32[]{:S(2)}) %collective-permute-start.10) | collective-permute-done | bytes 229408 | tf_op jit(solution)/shard_map/ppermute | solution.py:25
  40.2 3.8 %collective-permute-start.13 = (f32[448,128]{1,0:T(8,128)S(1)}, f32[448,128]{1,0:T(8,128)S(1)}, u32[]{:S(2)}, u32[]{:S(2)}) collective-permute-start(f32[448,128]{1,0:T(8,128)S(1)} %add_add_fusion.p0), channel_id=1, source_target_pairs={{0,96},{4,100},{8,104},{12,108},{16,112},{20,116},{24,120},{28,124... | collective-permute-start | bytes 688136 | tf_op jit(solution)/shard_map/ppermute | solution.py:29
  44.8 9.0 %collective-permute-done.13.p3 = f32[448,128]{1,0:T(8,128)S(1)} collective-permute-done((f32[448,128]{1,0:T(8,128)S(1)}, f32[448,128]{1,0:T(8,128)S(1)}, u32[]{:S(2)}, u32[]{:S(2)}) %collective-permute-start.13) | collective-permute-done | bytes 229408 | tf_op jit(solution)/shard_map/ppermute | solution.py:29
  54.3 2.6 %collective-permute-start.16 = (f32[32,384]{1,0:T(8,128)S(1)}, f32[32,384]{1,0:T(8,128)S(1)}, u32[]{:S(2)}, u32[]{:S(2)}) collective-permute-start(f32[32,384]{1,0:T(8,128)S(1)} %get-tuple-element.33.a0), channel_id=1, source_target_pairs={{0,3},{1,2},{2,1},{3,0},{4,7},{5,6},{6,5},{7,4},{8,11},{9,10},{10,... | collective-permute-start | bytes 147464 | tf_op jit(solution)/shard_map/ppermute | solution.py:33
  58.5 2.8 %collective-permute-done.15.a2 = f32[32,384]{1,0:T(8,128)S(1)} collective-permute-done((f32[32,384]{1,0:T(8,128)S(1)}, f32[32,384]{1,0:T(8,128)S(1)}, u32[]{:S(2)}, u32[]{:S(2)}) %collective-permute-start.15) | collective-permute-done | bytes 49184 | tf_op jit(solution)/shard_map/ppermute | solution.py:33
  61.3 2.1 %second_left.1.a0 = f32[32,384]{1,0:T(8,128)S(1)} custom-call(f32[32,384]{1,0:T(8,128)S(1)} %get-tuple-element.33.a0, f32[32,384]{1,0:T(8,128)S(1)} %collective-permute-done.14.a1, f32[32,384]{1,0:T(8,128)S(1)} %collective-permute-done.15.a2, f32[32,384]{1,0:T(8,128)S(1)} %collective-permute-done.16.a3, bf16[384,384]{1,0:T(8,128)(2,1)S(1)} %get-tuple-element.34.high_ref, ...), custom_call_target="tpu_custom_call" | custom-call | tf_op jit(solution)/shard_map/second_left/pallas_call | solution.py:268
  63.6 3.1 %collective-permute-start.17 = (f32[32,384]{1,0:T(8,128)S(1)}, f32[32,384]{1,0:T(8,128)S(1)}, u32[]{:S(2)}, u32[]{:S(2)}) collective-permute-start(f32[32,384]{1,0:T(8,128)S(1)} %second_left.1.a0), channel_id=1, source_target_pairs={{0,8},{4,12},{8,0},{12,4},{16,24},{20,28},{24,16},{28,20},{32,40},... | collective-permute-start | bytes 147464 | tf_op jit(solution)/shard_map/ppermute | solution.py:25
  68.8 2.2 %second_right.1 = (f32[32,384]{1,0:T(8,128)S(1)}, f32[32,384]{1,0:T(8,128)S(1)}) custom-call(f32[32,384]{1,0:T(8,128)S(1)} %second_left.1.a0, f32[32,384]{1,0:T(8,128)S(1)} %collective-permute-done.17.a1, f32[32,384]{1,0:T(8,128)S(1)} %collective-permute-done.18.a2, f32[32,384]{1,0:T(8,128)S(1)} %collective-permute-done.19.a3, ...), custom_call_target="tpu_custom_call" | custom-call | tf_op jit(solution)/shard_map/second_right/pallas_call | solution.py:268
  76.3 7.2 %collective-permute-start.23 = (f32[32,384]{1,0:T(8,128)S(1)}, f32[32,384]{1,0:T(8,128)S(1)}, u32[]{:S(2)}, u32[]{:S(2)}) collective-permute-start(f32[32,384]{1,0:T(8,128)S(1)} %add_add_fusion.2), channel_id=1, source_target_pairs={{0,4},{4,0},{8,12},{12,8},{16,20},{20,16},{24,28},{28,24},{32,36},... | collective-permute-start | bytes 147464 | tf_op jit(solution)/shard_map/ppermute | solution.py:21
  84.4 1.9 %collective-permute-start.26 = (f32[64,384]{1,0:T(8,128)S(1)}, f32[64,384]{1,0:T(8,128)S(1)}, u32[]{:S(2)}, u32[]{:S(2)}) collective-permute-start(f32[64,384]{1,0:T(8,128)S(1)} %pad_maximum_fusion.refs_0_.refs_3_), channel_id=1, source_target_pairs={{0,24},{4,28},{8,16},{12,20},{16,8},{20,12},{24,0},{28,4},{32,56},... | collective-permute-start | bytes 294920 | tf_op jit(solution)/shard_map/ppermute | solution.py:25
  87.7 3.0 %solve.1 = (f32[32,384]{1,0:T(8,128)S(1)}, f32[2,320,1280]{2,1,0:T(8,128)S(1)}, f32[2,320,1280]{2,1,0:T(8,128)S(1)}) custom-call(f32[64,384]{1,0:T(8,128)S(1)} %pad_maximum_fusion.refs_0_.refs_3_, f32[32,384]{1,0:T(8,128)S(1)} %get-tuple-element.37.refs_1_, f32[2,320,1280]{2,1,0:T(8,128)} %refs_2_.5, f32[2,320,1280]{2,1,0:T(8,128)} %refs_3_.1), custom_call_target="tpu_custom_call" | custom-call | tf_op jit(solution)/shard_map/solve/pallas_call | solution.py:268
  92.9 4.8 %finish.1 = (f32[2,320,1280]{2,1,0:T(8,128)}, f32[2,320,1280]{2,1,0:T(8,128)}, f32[2,320,1280]{2,1,0:T(8,128)}) custom-call(s32[2]{0:T(128)S(1)} %pad_add_fusion.where.refs_0_, f32[320,1280]{1,0:T(8,128)S(1)} %grad_own.1.a_ref.refs_1_, f32[320,1280]{1,0:T(8,128)S(1)} %grad_other.1.refs_2_, f32[64,384]{1,0:T(8,128)S(1)} %pad_maximum_fusion.refs_0_.refs_3_, ...), custom_call_target="tpu_custom_call" | custom-call | tf_op jit(solution)/shard_map/finish/pallas_call | solution.py:305
  (57 shorter events, 16.0 us)
Async XLA Ops:
  4.8 6.1 %collective-permute-start = (f32[320,1280]{1,0:T(8,128)S(1)}, f32[320,1280]{1,0:T(8,128)}, u32[]{:S(2)}, u32[]{:S(2)}) collective-permute-start(f32[320,1280]{1,0:T(8,128)S(1)} %grad_other.1.refs_2_), channel_id=1, source_target_pairs={{0,4},{4,0},{8,12},{12,8},{16,20},{20,16},{24,28},{28,24},{32,36},... | collective-permute-start | bytes 4915208 | tf_op jit(solution)/shard_map/ppermute | solution.py:21
  6.4 4.4 %collective-permute-start.1 = (f32[4,320]{1,0:T(4,128)S(1)}, f32[4,320]{1,0:T(4,128)S(1)}, u32[]{:S(2)}, u32[]{:S(2)}) collective-permute-start(f32[4,320]{1,0:T(4,128)S(1)} %bitcast.13), channel_id=1, source_target_pairs={{0,4},{4,0},{8,12},{12,8},{16,20},{20,16},{24,28},{28,24},{32,36},... | collective-permute-start | bytes 15368 | tf_op jit(solution)/shard_map/ppermute | solution.py:21
  14.0 7.9 %collective-permute-start.2 = (f32[448,128]{1,0:T(8,128)S(1)}, f32[448,128]{1,0:T(8,128)S(1)}, u32[]{:S(2)}, u32[]{:S(2)}) collective-permute-start(f32[448,128]{1,0:T(8,128)S(1)} %get-tuple-element.26), channel_id=1, source_target_pairs={{0,8},{4,12},{8,0},{12,4},{16,24},{20,28},{24,16},{28,20},{32,40},... | collective-permute-start | bytes 688136 | tf_op jit(solution)/shard_map/ppermute | solution.py:25
  15.5 12.9 %collective-permute-start.3 = (f32[448,128]{1,0:T(8,128)S(1)}, f32[448,128]{1,0:T(8,128)S(1)}, u32[]{:S(2)}, u32[]{:S(2)}) collective-permute-start(f32[448,128]{1,0:T(8,128)S(1)} %get-tuple-element.27), channel_id=1, source_target_pairs={{0,16},{4,20},{8,24},{12,28},{16,0},{20,4},{24,8},{28,12},{32,48},... | collective-permute-start | bytes 688136 | tf_op jit(solution)/shard_map/ppermute | solution.py:25
  18.1 12.3 %collective-permute-start.4 = (f32[448,128]{1,0:T(8,128)S(1)}, f32[448,128]{1,0:T(8,128)S(1)}, u32[]{:S(2)}, u32[]{:S(2)}) collective-permute-start(f32[448,128]{1,0:T(8,128)S(1)} %get-tuple-element.28), channel_id=1, source_target_pairs={{0,24},{4,28},{8,16},{12,20},{16,8},{20,12},{24,0},{28,4},{32,56},... | collective-permute-start | bytes 688136 | tf_op jit(solution)/shard_map/ppermute | solution.py:25
  18.1 16.2 %collective-permute-start.8 = (f32[448,128]{1,0:T(8,128)S(1)}, f32[448,128]{1,0:T(8,128)S(1)}, u32[]{:S(2)}, u32[]{:S(2)}) collective-permute-start(f32[448,128]{1,0:T(8,128)S(1)} %get-tuple-element.30), channel_id=1, source_target_pairs={{0,8},{4,12},{8,0},{12,4},{16,24},{20,28},{24,16},{28,20},{32,40},... | collective-permute-start | bytes 688136 | tf_op jit(solution)/shard_map/ppermute | solution.py:25
  18.1 20.1 %collective-permute-start.9 = (f32[448,128]{1,0:T(8,128)S(1)}, f32[448,128]{1,0:T(8,128)S(1)}, u32[]{:S(2)}, u32[]{:S(2)}) collective-permute-start(f32[448,128]{1,0:T(8,128)S(1)} %get-tuple-element.31), channel_id=1, source_target_pairs={{0,16},{4,20},{8,24},{12,28},{16,0},{20,4},{24,8},{28,12},{32,48},... | collective-permute-start | bytes 688136 | tf_op jit(solution)/shard_map/ppermute | solution.py:25
  21.9 18.3 %collective-permute-start.10 = (f32[448,128]{1,0:T(8,128)S(1)}, f32[448,128]{1,0:T(8,128)S(1)}, u32[]{:S(2)}, u32[]{:S(2)}) collective-permute-start(f32[448,128]{1,0:T(8,128)S(1)} %get-tuple-element.32), channel_id=1, source_target_pairs={{0,24},{4,28},{8,16},{12,20},{16,8},{20,12},{24,0},{28,4},{32,56},... | collective-permute-start | bytes 688136 | tf_op jit(solution)/shard_map/ppermute | solution.py:25
  30.4 13.7 %collective-permute-start.7 = (f32[448,128]{1,0:T(8,128)S(1)}, f32[448,128]{1,0:T(8,128)S(1)}, u32[]{:S(2)}, u32[]{:S(2)}) collective-permute-start(f32[448,128]{1,0:T(8,128)S(1)} %add_add_fusion.1.m0), channel_id=1, source_target_pairs={{0,96},{4,100},{8,104},{12,108},{16,112},{20,116},{24,120},{28,124... | collective-permute-start | bytes 688136 | tf_op jit(solution)/shard_map/ppermute | solution.py:29
  34.2 10.5 %collective-permute-start.6 = (f32[448,128]{1,0:T(8,128)S(1)}, f32[448,128]{1,0:T(8,128)S(1)}, u32[]{:S(2)}, u32[]{:S(2)}) collective-permute-start(f32[448,128]{1,0:T(8,128)S(1)} %add_add_fusion.1.m0), channel_id=1, source_target_pairs={{0,64},{4,68},{8,72},{12,76},{16,80},{20,84},{24,88},{28,92},{32,9... | collective-permute-start | bytes 688136 | tf_op jit(solution)/shard_map/ppermute | solution.py:29
  34.3 10.5 %collective-permute-start.5 = (f32[448,128]{1,0:T(8,128)S(1)}, f32[448,128]{1,0:T(8,128)S(1)}, u32[]{:S(2)}, u32[]{:S(2)}) collective-permute-start(f32[448,128]{1,0:T(8,128)S(1)} %add_add_fusion.1.m0), channel_id=1, source_target_pairs={{0,32},{4,36},{8,40},{12,44},{16,48},{20,52},{24,56},{28,60},{32,0... | collective-permute-start | bytes 688136 | tf_op jit(solution)/shard_map/ppermute | solution.py:29
  40.2 13.5 %collective-permute-start.13 = (f32[448,128]{1,0:T(8,128)S(1)}, f32[448,128]{1,0:T(8,128)S(1)}, u32[]{:S(2)}, u32[]{:S(2)}) collective-permute-start(f32[448,128]{1,0:T(8,128)S(1)} %add_add_fusion.p0), channel_id=1, source_target_pairs={{0,96},{4,100},{8,104},{12,108},{16,112},{20,116},{24,120},{28,124... | collective-permute-start | bytes 688136 | tf_op jit(solution)/shard_map/ppermute | solution.py:29
  44.1 9.7 %collective-permute-start.12 = (f32[448,128]{1,0:T(8,128)S(1)}, f32[448,128]{1,0:T(8,128)S(1)}, u32[]{:S(2)}, u32[]{:S(2)}) collective-permute-start(f32[448,128]{1,0:T(8,128)S(1)} %add_add_fusion.p0), channel_id=1, source_target_pairs={{0,64},{4,68},{8,72},{12,76},{16,80},{20,84},{24,88},{28,92},{32,9... | collective-permute-start | bytes 688136 | tf_op jit(solution)/shard_map/ppermute | solution.py:29
  44.1 9.7 %collective-permute-start.11 = (f32[448,128]{1,0:T(8,128)S(1)}, f32[448,128]{1,0:T(8,128)S(1)}, u32[]{:S(2)}, u32[]{:S(2)}) collective-permute-start(f32[448,128]{1,0:T(8,128)S(1)} %add_add_fusion.p0), channel_id=1, source_target_pairs={{0,32},{4,36},{8,40},{12,44},{16,48},{20,52},{24,56},{28,60},{32,0... | collective-permute-start | bytes 688136 | tf_op jit(solution)/shard_map/ppermute | solution.py:29
  54.3 4.2 %collective-permute-start.16 = (f32[32,384]{1,0:T(8,128)S(1)}, f32[32,384]{1,0:T(8,128)S(1)}, u32[]{:S(2)}, u32[]{:S(2)}) collective-permute-start(f32[32,384]{1,0:T(8,128)S(1)} %get-tuple-element.33.a0), channel_id=1, source_target_pairs={{0,3},{1,2},{2,1},{3,0},{4,7},{5,6},{6,5},{7,4},{8,11},{9,10},{10,... | collective-permute-start | bytes 147464 | tf_op jit(solution)/shard_map/ppermute | solution.py:33
  56.8 4.5 %collective-permute-start.15 = (f32[32,384]{1,0:T(8,128)S(1)}, f32[32,384]{1,0:T(8,128)S(1)}, u32[]{:S(2)}, u32[]{:S(2)}) collective-permute-start(f32[32,384]{1,0:T(8,128)S(1)} %get-tuple-element.33.a0), channel_id=1, source_target_pairs={{0,2},{1,3},{2,0},{3,1},{4,6},{5,7},{6,4},{7,5},{8,10},{9,11},{10,... | collective-permute-start | bytes 147464 | tf_op jit(solution)/shard_map/ppermute | solution.py:33
  63.4 4.8 %collective-permute-start.19 = (f32[32,384]{1,0:T(8,128)S(1)}, f32[32,384]{1,0:T(8,128)S(1)}, u32[]{:S(2)}, u32[]{:S(2)}) collective-permute-start(f32[32,384]{1,0:T(8,128)S(1)} %second_left.1.a0), channel_id=1, source_target_pairs={{0,24},{4,28},{8,16},{12,20},{16,8},{20,12},{24,0},{28,4},{32,56},... | collective-permute-start | bytes 147464 | tf_op jit(solution)/shard_map/ppermute | solution.py:25
  63.6 4.6 %collective-permute-start.18 = (f32[32,384]{1,0:T(8,128)S(1)}, f32[32,384]{1,0:T(8,128)S(1)}, u32[]{:S(2)}, u32[]{:S(2)}) collective-permute-start(f32[32,384]{1,0:T(8,128)S(1)} %second_left.1.a0), channel_id=1, source_target_pairs={{0,16},{4,20},{8,24},{12,28},{16,0},{20,4},{24,8},{28,12},{32,48},... | collective-permute-start | bytes 147464 | tf_op jit(solution)/shard_map/ppermute | solution.py:25
  63.6 5.1 %collective-permute-start.17 = (f32[32,384]{1,0:T(8,128)S(1)}, f32[32,384]{1,0:T(8,128)S(1)}, u32[]{:S(2)}, u32[]{:S(2)}) collective-permute-start(f32[32,384]{1,0:T(8,128)S(1)} %second_left.1.a0), channel_id=1, source_target_pairs={{0,8},{4,12},{8,0},{12,4},{16,24},{20,28},{24,16},{28,20},{32,40},... | collective-permute-start | bytes 147464 | tf_op jit(solution)/shard_map/ppermute | solution.py:25
  71.9 4.4 %collective-permute-start.21 = (f32[32,384]{1,0:T(8,128)S(1)}, f32[32,384]{1,0:T(8,128)S(1)}, u32[]{:S(2)}, u32[]{:S(2)}) collective-permute-start(f32[32,384]{1,0:T(8,128)S(1)} %get-tuple-element.36), channel_id=1, source_target_pairs={{0,2},{1,3},{2,0},{3,1},{4,6},{5,7},{6,4},{7,5},{8,10},{9,11},{10,... | collective-permute-start | bytes 147464 | tf_op jit(solution)/shard_map/ppermute | solution.py:33
  76.3 8.1 %collective-permute-start.23 = (f32[32,384]{1,0:T(8,128)S(1)}, f32[32,384]{1,0:T(8,128)S(1)}, u32[]{:S(2)}, u32[]{:S(2)}) collective-permute-start(f32[32,384]{1,0:T(8,128)S(1)} %add_add_fusion.2), channel_id=1, source_target_pairs={{0,4},{4,0},{8,12},{12,8},{16,20},{20,16},{24,28},{28,24},{32,36},... | collective-permute-start | bytes 147464 | tf_op jit(solution)/shard_map/ppermute | solution.py:21
  84.4 8.5 %collective-permute-start.26 = (f32[64,384]{1,0:T(8,128)S(1)}, f32[64,384]{1,0:T(8,128)S(1)}, u32[]{:S(2)}, u32[]{:S(2)}) collective-permute-start(f32[64,384]{1,0:T(8,128)S(1)} %pad_maximum_fusion.refs_0_.refs_3_), channel_id=1, source_target_pairs={{0,24},{4,28},{8,16},{12,20},{16,8},{20,12},{24,0},{28,4},{32,56},... | collective-permute-start | bytes 294920 | tf_op jit(solution)/shard_map/ppermute | solution.py:25
  86.3 6.6 %collective-permute-start.25 = (f32[64,384]{1,0:T(8,128)S(1)}, f32[64,384]{1,0:T(8,128)S(1)}, u32[]{:S(2)}, u32[]{:S(2)}) collective-permute-start(f32[64,384]{1,0:T(8,128)S(1)} %pad_maximum_fusion.refs_0_.refs_3_), channel_id=1, source_target_pairs={{0,16},{4,20},{8,24},{12,28},{16,0},{20,4},{24,8},{28,12},{32,48},... | collective-permute-start | bytes 294920 | tf_op jit(solution)/shard_map/ppermute | solution.py:25
  87.5 5.4 %collective-permute-start.24 = (f32[64,384]{1,0:T(8,128)S(1)}, f32[64,384]{1,0:T(8,128)S(1)}, u32[]{:S(2)}, u32[]{:S(2)}) collective-permute-start(f32[64,384]{1,0:T(8,128)S(1)} %pad_maximum_fusion.refs_0_.refs_3_), channel_id=1, source_target_pairs={{0,8},{4,12},{8,0},{12,4},{16,24},{20,28},{24,16},{28,20},{32,40},... | collective-permute-start | bytes 294920 | tf_op jit(solution)/shard_map/ppermute | solution.py:25
  (7 other events, 28.1 us)

commit v4 on v3

--- a/solution.py
+++ b/solution.py
@@ -103,12 +103,17 @@
 REST = 800 - AHEAD
 
 
-def route_kernel(where, a_ref, b_ref, q_hbm, v_ref, o0, o1, o2, o3, r0, r1, r2, r3, stage, both, q_buf, q_sem):
+def route_kernel(where, a_ref, b_hbm, q_hbm, v_ref, o0, o1, o2, o3, r0, r1, r2, r3, stage, both, b_ref, q_buf, b_sem, q_sem):
     core, y = where[0], where[1]
     fetch = pltpu.make_async_copy(q_hbm.at[core], q_buf, q_sem)
+    halves = [pltpu.make_async_copy(b_hbm.at[:, at:at + 640], b_ref.at[:, at:at + 640], b_sem.at[i])
+              for i, at in enumerate((0, 640))]
+    halves[0].start()
+    halves[1].start()
     fetch.start()
     left = lanes((160, 128)) < 64
     for i in range(2):
+        halves[i].wait()
         tiles = []
         for t in range(5):
             at = 640 * i + 128 * t
@@ -168,15 +173,16 @@
 
 def orth(packed):
     inverse, pivots = eliminate(packed[:, 256:384])
-    return dot(inverse * lax.rsqrt(pivots), below(payload(packed)), NN, HIGH)
+    i_high, i_low = split(inverse * lax.rsqrt(pivots))
+    b_high, b_low = split(below(payload(packed)))
+    return dot(jnp.concatenate([i_high, i_low, i_high], axis=1), jnp.concatenate([b_high, b_high, b_low], axis=0), NN)
 
 
 def to_right(left, w_high, w_low):
     out = dot3(left, w_high, w_low, NN)
-    zero = jnp.zeros((64, left.shape[1]), F32)
-    shifted = jnp.concatenate([zero, left, zero[:32]], axis=0)
-    gram = dot(left, shifted, NT, HIGH)
-    return jnp.concatenate([out[:, :256], out[:, 256:] + gram], axis=1)
+    zero = jnp.zeros((64, left.shape[1]), BF16)
+    high, low = (jnp.concatenate([zero, part, zero[:32]], axis=0) for part in split(left))
+    return jnp.concatenate([out[:, :256], out[:, 256:] + dot3(left, high, low, NT)], axis=1)
 
 
 def wide_kernel(m0, m1, m2, m3, p0, p1, p2, p3, high_ref, low_ref, out_ref, vec_ref):
@@ -211,23 +217,24 @@
     two = pltpu.make_async_copy(m_hbm, m_out, sems.at[1])
     one.start()
     two.start()
-    inverse, pivots = eliminate(packed_ref[0:32, 256:384])
+    inverse, pivots = eliminate(packed_ref[:, 256:384])
     once = dot(inverse, below(left_ref[...]), NN, HIGH) * (scale / pivots)
     out_ref[...] = dot(inverse, once, TN, HIGH)[96:128]
     one.wait()
     two.wait()
 
 
-def final_kernel(where, own, other, g0, g1, g2, g3, l_own, l_other, w_ref, m_ref,
+def final_kernel(where, own, other, g0, g1, g2, g3, h0, h1, h2, h3, l_own, l_other, w_ref, m_ref,
                  e_hbm, w_hbm, m_hbm, stage, e_buf, w_buf, m_buf, sems, *, blocks):
     core, y = where[0], where[1]
     size = own.shape[0] // blocks
     side = lanes((32, 128)) < 64
     copies = []
-    for slot, (full, left_ref) in enumerate(((own, l_own), (other, l_other))):
+    for slot, (full, left_ref, quarters) in enumerate(
+            ((own, l_own, (g0, g1, g2, g3)), (other, l_other, (h0, h1, h2, h3)))):
         mat = core ^ slot
-        for k, g in enumerate((g0, g1, g2, g3)):
-            stage[y ^ k] = g[32 * slot:32 * slot + 32]
+        for k, quarter in enumerate(quarters):
+            stage[y ^ k] = quarter[...]
         tiles = []
         for i in range(2):
             even, odd = stage[2 * i], stage[2 * i + 1]
@@ -305,7 +312,7 @@
     return pl.pallas_call(
         lambda *refs: final_kernel(*refs, blocks=blocks),
         out_shape=[shaped(weights.shape)] * 3,
-        in_specs=[SM] + [VM] * 10,
+        in_specs=[SM] + [VM] * 14,
         out_specs=[hbm] * 3,
         scratch_shapes=[pltpu.VMEM((4, 32, 384), F32)] + [pltpu.VMEM(weights.shape, F32)] * 3
         + [pltpu.SemaphoreType.DMA((2, blocks, 3))],
@@ -330,9 +337,9 @@
     hbm = pl.BlockSpec(memory_space=pltpu.HBM)
     in_hbm = lambda value: pltpu.with_memory_space_constraint(value, pltpu.HBM)
     sends = call(route_kernel, (where, own, swap_core(other), in_hbm(start_q.swapaxes(1, 2)), vec_core),
-                 [shaped((AHEAD, 128))] * 4 + [shaped((REST + 96, 128))] * 4, [SM, VM, VM, hbm, VM],
-                 [pltpu.VMEM((4, 800, 128), F32), pltpu.VMEM((384, 1280), F32), pltpu.VMEM((32, 1280), F32),
-                  pltpu.SemaphoreType.DMA(())], name="route")
+                 [shaped((AHEAD, 128))] * 4 + [shaped((REST + 96, 128))] * 4, [SM, VM, hbm, hbm, VM],
+                 [pltpu.VMEM((4, 800, 128), F32), pltpu.VMEM((384, 1280), F32), pltpu.VMEM((320, 1280), F32),
+                  pltpu.VMEM((32, 1280), F32), pltpu.SemaphoreType.DMA((2,)), pltpu.SemaphoreType.DMA(())], name="route")
     ahead = add4([sends[0]] + [swap_y(sends[k], k) for k in (1, 2, 3)])
     behind = add4([sends[4]] + [swap_y(sends[4 + k], k) for k in (1, 2, 3)])
     w_high, w_low, packed, vec_sum = call(
@@ -343,7 +350,8 @@
     left, packed = call(right_kernel, (*fan(packed, swap_y), w_high, w_low), [shaped((32, 384))] * 2, [VM] * 6,
                         name="second_right")
     packed = add4(fan(packed, swap_x))
-    rights = fan(jnp.concatenate([packed, swap_core(packed)], axis=0), swap_y)
+    rights = fan(packed, swap_y)
+    rights += [swap_core(right) for right in rights]
     held = pltpu.VMEM(weights.shape, F32)
     l_own, weights, momentum = call(
         lambda *refs: solve_kernel(*refs, scale=1.0 / replicas), (rights[0], left, in_hbm(weights), in_hbm(momentum)),

time: 98 us -> 97.5 us (level)
    ppermute x4 -> x7, starting transfers between devices: 10.1 us -> 10.7 us  [swap_core(): return lax.ppermute(value, 'replica', CORE)]
  transfers between devices with their start and end apart: 28 -> 31, of which waited for: 13 -> 13; matrix products, arithmetic and copies ran while one was open for 1% -> 1% of each run, Pallas kernels for 7% -> 7%
where the time goes in v4:
time: 97.5 us; the launch traced here: 97.4 us
  starting transfers between devices  42.9 us (44%)
  waiting for transfers between devices  29 us (30%)
  Pallas kernels  23.5 us (24%)
    ppermute x12, starting transfers between devices, swap_y(): return lax.ppermute(value, 'replica', [(r, r ^ k << 1) for r in range(32)])  16.3 us
    ppermute x12, waiting for transfers between devices, swap_y(): return lax.ppermute(value, 'replica', [(r, r ^ k << 1) for r in range(32)])  14 us
    ppermute x7, starting transfers between devices, swap_core(): return lax.ppermute(value, 'replica', CORE)  10.7 us
    pallas_call x5, Pallas kernels, call(): pl.pallas_call(kernel, out_shape=outs, in_specs=specs, out_specs=[VM] * l...  10.3 us
    ppermute x6, waiting for transfers between devices, swap_z(): return lax.ppermute(value, 'replica', [(r, r ^ k << 3) for r in range(32)])  9.03 us
    ppermute x6, starting transfers between devices, swap_z(): return lax.ppermute(value, 'replica', [(r, r ^ k << 3) for r in range(32)])  9.03 us
    pallas_call x2, Pallas kernels, gradients(): pl.pallas_call(lambda *refs: grad_kernel(*refs, scale=scale, step=step, a...  8.38 us
    ppermute x6, starting transfers between devices, swap_x(): return lax.ppermute(value, 'shard', [(s, s ^ k) for s in range(4)])  6.85 us
  transfers between devices with their start and end apart: 31, of which 13 were waited for; matrix products, arithmetic and copies ran while one was open for 1% of the time, Pallas kernels for 7%

profile of v4, /device:TPU:1, one launch (start us, length us, event | category | flops | bytes accessed | tf_op | source)
XLA Modules:
  0.0 97.4 jit_solution(3718120013926457990)
XLA Ops:
  0.6 4.2 %grad_other.1.refs_2_ = f32[320,1280]{1,0:T(8,128)S(1)} custom-call(s32[1]{0:T(128)S(6)} %sub.6.refs_0_, bf16[2,320,2048]{2,1,0:T(8,128)(2,1)} %bitcast.10, bf16[2,2048,1280]{2,1,0:T(8,128)(2,1)} %refs_2_.4, f32[2,320,1280]{2,1,0:T(8,128)} %bitcast.8), custom_call_target="tpu_custom_call" | custom-call | tf_op jit(solution)/shard_map/grad_other/pallas_call | solution.py:291
  4.8 1.5 %collective-permute-start = (f32[320,1280]{1,0:T(8,128)S(1)}, f32[320,1280]{1,0:T(8,128)}, u32[]{:S(2)}, u32[]{:S(2)}) collective-permute-start(f32[320,1280]{1,0:T(8,128)S(1)} %grad_other.1.refs_2_), channel_id=1, source_target_pairs={{0,4},{4,0},{8,12},{12,8},{16,20},{20,16},{24,28},{28,24},{32,36},... | collective-permute-start | bytes 4915208 | tf_op jit(solution)/shard_map/ppermute | solution.py:21
  6.5 4.2 %grad_own.1.a_ref.refs_1_ = f32[320,1280]{1,0:T(8,128)S(1)} custom-call(s32[1]{0:T(128)} %bitcast.refs_0_, bf16[2,320,2048]{2,1,0:T(8,128)(2,1)} %bitcast.11, bf16[2,2048,1280]{2,1,0:T(8,128)(2,1)} %refs_2_.4, f32[2,320,1280]{2,1,0:T(8,128)} %bitcast.9), custom_call_target="tpu_custom_call" | custom-call | tf_op jit(solution)/shard_map/grad_own/pallas_call | solution.py:291
  10.9 2.9 %route.1 = (f32[448,128]{1,0:T(8,128)S(1)}, f32[448,128]{1,0:T(8,128)S(1)}, f32[448,128]{1,0:T(8,128)S(1)}, f32[448,128]{1,0:T(8,128)S(1)}, f32[448,128]{1,0:T(8...) custom-call(s32[2]{0:T(128)S(1)} %pad_add_fusion.where.refs_0_, ...), custom_call_target="tpu_custom_call" | custom-call | tf_op jit(solution)/shard_map/route/pallas_call | solution.py:275
  13.8 1.5 %collective-permute-start.2 = (f32[448,128]{1,0:T(8,128)S(1)}, f32[448,128]{1,0:T(8,128)S(1)}, u32[]{:S(2)}, u32[]{:S(2)}) collective-permute-start(f32[448,128]{1,0:T(8,128)S(1)} %get-tuple-element.26), channel_id=1, source_target_pairs={{0,8},{4,12},{8,0},{12,4},{16,24},{20,28},{24,16},{28,20},{32,40},... | collective-permute-start | bytes 688136 | tf_op jit(solution)/shard_map/ppermute | solution.py:25
  15.3 2.6 %collective-permute-start.3 = (f32[448,128]{1,0:T(8,128)S(1)}, f32[448,128]{1,0:T(8,128)S(1)}, u32[]{:S(2)}, u32[]{:S(2)}) collective-permute-start(f32[448,128]{1,0:T(8,128)S(1)} %get-tuple-element.27), channel_id=1, source_target_pairs={{0,16},{4,20},{8,24},{12,28},{16,0},{20,4},{24,8},{28,12},{32,48},... | collective-permute-start | bytes 688136 | tf_op jit(solution)/shard_map/ppermute | solution.py:25
  17.9 3.8 %collective-permute-start.9 = (f32[448,128]{1,0:T(8,128)S(1)}, f32[448,128]{1,0:T(8,128)S(1)}, u32[]{:S(2)}, u32[]{:S(2)}) collective-permute-start(f32[448,128]{1,0:T(8,128)S(1)} %get-tuple-element.31), channel_id=1, source_target_pairs={{0,16},{4,20},{8,24},{12,28},{16,0},{20,4},{24,8},{28,12},{32,48},... | collective-permute-start | bytes 688136 | tf_op jit(solution)/shard_map/ppermute | solution.py:25
  21.8 1.7 %collective-permute-start.10 = (f32[448,128]{1,0:T(8,128)S(1)}, f32[448,128]{1,0:T(8,128)S(1)}, u32[]{:S(2)}, u32[]{:S(2)}) collective-permute-start(f32[448,128]{1,0:T(8,128)S(1)} %get-tuple-element.32), channel_id=1, source_target_pairs={{0,24},{4,28},{8,16},{12,20},{16,8},{20,12},{24,0},{28,4},{32,56},... | collective-permute-start | bytes 688136 | tf_op jit(solution)/shard_map/ppermute | solution.py:25
  23.5 4.7 %collective-permute-done.3 = f32[448,128]{1,0:T(8,128)S(1)} collective-permute-done((f32[448,128]{1,0:T(8,128)S(1)}, f32[448,128]{1,0:T(8,128)S(1)}, u32[]{:S(2)}, u32[]{:S(2)}) %collective-permute-start.3) | collective-permute-done | bytes 229408 | tf_op jit(solution)/shard_map/ppermute | solution.py:25
  28.2 2.0 %collective-permute-done.4 = f32[448,128]{1,0:T(8,128)S(1)} collective-permute-done((f32[448,128]{1,0:T(8,128)S(1)}, f32[448,128]{1,0:T(8,128)S(1)}, u32[]{:S(2)}, u32[]{:S(2)}) %collective-permute-start.4) | collective-permute-done | bytes 229408 | tf_op jit(solution)/shard_map/ppermute | solution.py:25
  30.2 3.8 %collective-permute-start.7 = (f32[448,128]{1,0:T(8,128)S(1)}, f32[448,128]{1,0:T(8,128)S(1)}, u32[]{:S(2)}, u32[]{:S(2)}) collective-permute-start(f32[448,128]{1,0:T(8,128)S(1)} %add_add_fusion.1.m0), channel_id=1, source_target_pairs={{0,96},{4,100},{8,104},{12,108},{16,112},{20,116},{24,120},{28,124... | collective-permute-start | bytes 688136 | tf_op jit(solution)/shard_map/ppermute | solution.py:29
  34.7 3.3 %collective-permute-done.9 = f32[448,128]{1,0:T(8,128)S(1)} collective-permute-done((f32[448,128]{1,0:T(8,128)S(1)}, f32[448,128]{1,0:T(8,128)S(1)}, u32[]{:S(2)}, u32[]{:S(2)}) %collective-permute-start.9) | collective-permute-done | bytes 229408 | tf_op jit(solution)/shard_map/ppermute | solution.py:25
  38.0 2.0 %collective-permute-done.10 = f32[448,128]{1,0:T(8,128)S(1)} collective-permute-done((f32[448,128]{1,0:T(8,128)S(1)}, f32[448,128]{1,0:T(8,128)S(1)}, u32[]{:S(2)}, u32[]{:S(2)}) %collective-permute-start.10) | collective-permute-done | bytes 229408 | tf_op jit(solution)/shard_map/ppermute | solution.py:25
  40.1 3.8 %collective-permute-start.13 = (f32[448,128]{1,0:T(8,128)S(1)}, f32[448,128]{1,0:T(8,128)S(1)}, u32[]{:S(2)}, u32[]{:S(2)}) collective-permute-start(f32[448,128]{1,0:T(8,128)S(1)} %add_add_fusion.p0), channel_id=1, source_target_pairs={{0,96},{4,100},{8,104},{12,108},{16,112},{20,116},{24,120},{28,124... | collective-permute-start | bytes 688136 | tf_op jit(solution)/shard_map/ppermute | solution.py:29
  44.6 9.0 %collective-permute-done.13.p3 = f32[448,128]{1,0:T(8,128)S(1)} collective-permute-done((f32[448,128]{1,0:T(8,128)S(1)}, f32[448,128]{1,0:T(8,128)S(1)}, u32[]{:S(2)}, u32[]{:S(2)}) %collective-permute-start.13) | collective-permute-done | bytes 229408 | tf_op jit(solution)/shard_map/ppermute | solution.py:29
  54.0 2.6 %collective-permute-start.16 = (f32[32,384]{1,0:T(8,128)S(1)}, f32[32,384]{1,0:T(8,128)S(1)}, u32[]{:S(2)}, u32[]{:S(2)}) collective-permute-start(f32[32,384]{1,0:T(8,128)S(1)} %get-tuple-element.33.a0), channel_id=1, source_target_pairs={{0,3},{1,2},{2,1},{3,0},{4,7},{5,6},{6,5},{7,4},{8,11},{9,10},{10,... | collective-permute-start | bytes 147464 | tf_op jit(solution)/shard_map/ppermute | solution.py:33
  58.2 2.8 %collective-permute-done.15.a2 = f32[32,384]{1,0:T(8,128)S(1)} collective-permute-done((f32[32,384]{1,0:T(8,128)S(1)}, f32[32,384]{1,0:T(8,128)S(1)}, u32[]{:S(2)}, u32[]{:S(2)}) %collective-permute-start.15) | collective-permute-done | bytes 49184 | tf_op jit(solution)/shard_map/ppermute | solution.py:33
  61.0 2.1 %second_left.1.a0 = f32[32,384]{1,0:T(8,128)S(1)} custom-call(f32[32,384]{1,0:T(8,128)S(1)} %get-tuple-element.33.a0, f32[32,384]{1,0:T(8,128)S(1)} %collective-permute-done.14.a1, f32[32,384]{1,0:T(8,128)S(1)} %collective-permute-done.15.a2, f32[32,384]{1,0:T(8,128)S(1)} %collective-permute-done.16.a3, bf16[384,384]{1,0:T(8,128)(2,1)S(1)} %get-tuple-element.34.high_ref, ...), custom_call_target="tpu_custom_call" | custom-call | tf_op jit(solution)/shard_map/second_left/pallas_call | solution.py:275
  63.2 3.1 %collective-permute-start.17 = (f32[32,384]{1,0:T(8,128)S(1)}, f32[32,384]{1,0:T(8,128)S(1)}, u32[]{:S(2)}, u32[]{:S(2)}) collective-permute-start(f32[32,384]{1,0:T(8,128)S(1)} %second_left.1.a0), channel_id=1, source_target_pairs={{0,8},{4,12},{8,0},{12,4},{16,24},{20,28},{24,16},{28,20},{32,40},... | collective-permute-start | bytes 147464 | tf_op jit(solution)/shard_map/ppermute | solution.py:25
  68.4 2.1 %second_right.1 = (f32[32,384]{1,0:T(8,128)S(1)}, f32[32,384]{1,0:T(8,128)S(1)}) custom-call(f32[32,384]{1,0:T(8,128)S(1)} %second_left.1.a0, f32[32,384]{1,0:T(8,128)S(1)} %collective-permute-done.17.a1, f32[32,384]{1,0:T(8,128)S(1)} %collective-permute-done.18.a2, f32[32,384]{1,0:T(8,128)S(1)} %collective-permute-done.19.a3, ...), custom_call_target="tpu_custom_call" | custom-call | tf_op jit(solution)/shard_map/second_right/pallas_call | solution.py:275
  76.0 2.0 %collective-permute-start.25 = (f32[32,384]{1,0:T(8,128)S(1)}, f32[32,384]{1,0:T(8,128)S(1)}, u32[]{:S(2)}, u32[]{:S(2)}) collective-permute-start(f32[32,384]{1,0:T(8,128)S(1)} %add_add_fusion.2.refs_0_.refs_3_), channel_id=1, source_target_pairs={{0,24},{4,28},{8,16},{12,20},{16,8},{20,12},{24,0},{28,4},{32,56},... | collective-permute-start | bytes 147464 | tf_op jit(solution)/shard_map/ppermute | solution.py:25
  79.5 8.0 %collective-permute-start.26 = (f32[32,384]{1,0:T(8,128)S(1)}, f32[32,384]{1,0:T(8,128)S(1)}, u32[]{:S(2)}, u32[]{:S(2)}) collective-permute-start(f32[32,384]{1,0:T(8,128)S(1)} %add_add_fusion.2.refs_0_.refs_3_), channel_id=1, source_target_pairs={{0,4},{4,0},{8,12},{12,8},{16,20},{20,16},{24,28},{28,24},{32,36},... | collective-permute-start | bytes 147464 | tf_op jit(solution)/shard_map/ppermute | solution.py:21
  87.5 3.0 %solve.1 = (f32[32,384]{1,0:T(8,128)S(1)}, f32[2,320,1280]{2,1,0:T(8,128)S(1)}, f32[2,320,1280]{2,1,0:T(8,128)S(1)}) custom-call(f32[32,384]{1,0:T(8,128)S(1)} %add_add_fusion.2.refs_0_.refs_3_, f32[32,384]{1,0:T(8,128)S(1)} %get-tuple-element.37.refs_1_, f32[2,320,1280]{2,1,0:T(8,128)} %refs_2_.5, f32[2,320,1280]{2,1,0:T(8,128)} %refs_3_.1), custom_call_target="tpu_custom_call" | custom-call | tf_op jit(solution)/shard_map/solve/pallas_call | solution.py:275
  92.4 4.8 %finish.1 = (f32[2,320,1280]{2,1,0:T(8,128)}, f32[2,320,1280]{2,1,0:T(8,128)}, f32[2,320,1280]{2,1,0:T(8,128)}) custom-call(s32[2]{0:T(128)S(1)} %pad_add_fusion.where.refs_0_, f32[320,1280]{1,0:T(8,128)S(1)} %grad_own.1.a_ref.refs_1_, f32[320,1280]{1,0:T(8,128)S(1)} %grad_other.1.refs_2_, f32[32,384]{1,0:T(8,128)S(1)} %add_add_fusion.2.refs_0_.refs_3_, ...), custom_call_target="tpu_custom_call" | custom-call | tf_op jit(solution)/shard_map/finish/pallas_call | solution.py:312
  (62 shorter events, 15.1 us)
Async XLA Ops:
  4.8 6.1 %collective-permute-start = (f32[320,1280]{1,0:T(8,128)S(1)}, f32[320,1280]{1,0:T(8,128)}, u32[]{:S(2)}, u32[]{:S(2)}) collective-permute-start(f32[320,1280]{1,0:T(8,128)S(1)} %grad_other.1.refs_2_), channel_id=1, source_target_pairs={{0,4},{4,0},{8,12},{12,8},{16,20},{20,16},{24,28},{28,24},{32,36},... | collective-permute-start | bytes 4915208 | tf_op jit(solution)/shard_map/ppermute | solution.py:21
  6.4 4.4 %collective-permute-start.1 = (f32[4,320]{1,0:T(4,128)S(1)}, f32[4,320]{1,0:T(4,128)S(1)}, u32[]{:S(2)}, u32[]{:S(2)}) collective-permute-start(f32[4,320]{1,0:T(4,128)S(1)} %bitcast.13), channel_id=1, source_target_pairs={{0,4},{4,0},{8,12},{12,8},{16,20},{20,16},{24,28},{28,24},{32,36},... | collective-permute-start | bytes 15368 | tf_op jit(solution)/shard_map/ppermute | solution.py:21
  13.8 7.9 %collective-permute-start.2 = (f32[448,128]{1,0:T(8,128)S(1)}, f32[448,128]{1,0:T(8,128)S(1)}, u32[]{:S(2)}, u32[]{:S(2)}) collective-permute-start(f32[448,128]{1,0:T(8,128)S(1)} %get-tuple-element.26), channel_id=1, source_target_pairs={{0,8},{4,12},{8,0},{12,4},{16,24},{20,28},{24,16},{28,20},{32,40},... | collective-permute-start | bytes 688136 | tf_op jit(solution)/shard_map/ppermute | solution.py:25
  15.3 12.9 %collective-permute-start.3 = (f32[448,128]{1,0:T(8,128)S(1)}, f32[448,128]{1,0:T(8,128)S(1)}, u32[]{:S(2)}, u32[]{:S(2)}) collective-permute-start(f32[448,128]{1,0:T(8,128)S(1)} %get-tuple-element.27), channel_id=1, source_target_pairs={{0,16},{4,20},{8,24},{12,28},{16,0},{20,4},{24,8},{28,12},{32,48},... | collective-permute-start | bytes 688136 | tf_op jit(solution)/shard_map/ppermute | solution.py:25
  17.9 12.3 %collective-permute-start.4 = (f32[448,128]{1,0:T(8,128)S(1)}, f32[448,128]{1,0:T(8,128)S(1)}, u32[]{:S(2)}, u32[]{:S(2)}) collective-permute-start(f32[448,128]{1,0:T(8,128)S(1)} %get-tuple-element.28), channel_id=1, source_target_pairs={{0,24},{4,28},{8,16},{12,20},{16,8},{20,12},{24,0},{28,4},{32,56},... | collective-permute-start | bytes 688136 | tf_op jit(solution)/shard_map/ppermute | solution.py:25
  17.9 16.2 %collective-permute-start.8 = (f32[448,128]{1,0:T(8,128)S(1)}, f32[448,128]{1,0:T(8,128)S(1)}, u32[]{:S(2)}, u32[]{:S(2)}) collective-permute-start(f32[448,128]{1,0:T(8,128)S(1)} %get-tuple-element.30), channel_id=1, source_target_pairs={{0,8},{4,12},{8,0},{12,4},{16,24},{20,28},{24,16},{28,20},{32,40},... | collective-permute-start | bytes 688136 | tf_op jit(solution)/shard_map/ppermute | solution.py:25
  17.9 20.1 %collective-permute-start.9 = (f32[448,128]{1,0:T(8,128)S(1)}, f32[448,128]{1,0:T(8,128)S(1)}, u32[]{:S(2)}, u32[]{:S(2)}) collective-permute-start(f32[448,128]{1,0:T(8,128)S(1)} %get-tuple-element.31), channel_id=1, source_target_pairs={{0,16},{4,20},{8,24},{12,28},{16,0},{20,4},{24,8},{28,12},{32,48},... | collective-permute-start | bytes 688136 | tf_op jit(solution)/shard_map/ppermute | solution.py:25
  21.8 18.2 %collective-permute-start.10 = (f32[448,128]{1,0:T(8,128)S(1)}, f32[448,128]{1,0:T(8,128)S(1)}, u32[]{:S(2)}, u32[]{:S(2)}) collective-permute-start(f32[448,128]{1,0:T(8,128)S(1)} %get-tuple-element.32), channel_id=1, source_target_pairs={{0,24},{4,28},{8,16},{12,20},{16,8},{20,12},{24,0},{28,4},{32,56},... | collective-permute-start | bytes 688136 | tf_op jit(solution)/shard_map/ppermute | solution.py:25
  30.2 13.7 %collective-permute-start.7 = (f32[448,128]{1,0:T(8,128)S(1)}, f32[448,128]{1,0:T(8,128)S(1)}, u32[]{:S(2)}, u32[]{:S(2)}) collective-permute-start(f32[448,128]{1,0:T(8,128)S(1)} %add_add_fusion.1.m0), channel_id=1, source_target_pairs={{0,96},{4,100},{8,104},{12,108},{16,112},{20,116},{24,120},{28,124... | collective-permute-start | bytes 688136 | tf_op jit(solution)/shard_map/ppermute | solution.py:29
  34.1 10.5 %collective-permute-start.6 = (f32[448,128]{1,0:T(8,128)S(1)}, f32[448,128]{1,0:T(8,128)S(1)}, u32[]{:S(2)}, u32[]{:S(2)}) collective-permute-start(f32[448,128]{1,0:T(8,128)S(1)} %add_add_fusion.1.m0), channel_id=1, source_target_pairs={{0,64},{4,68},{8,72},{12,76},{16,80},{20,84},{24,88},{28,92},{32,9... | collective-permute-start | bytes 688136 | tf_op jit(solution)/shard_map/ppermute | solution.py:29
  34.1 10.5 %collective-permute-start.5 = (f32[448,128]{1,0:T(8,128)S(1)}, f32[448,128]{1,0:T(8,128)S(1)}, u32[]{:S(2)}, u32[]{:S(2)}) collective-permute-start(f32[448,128]{1,0:T(8,128)S(1)} %add_add_fusion.1.m0), channel_id=1, source_target_pairs={{0,32},{4,36},{8,40},{12,44},{16,48},{20,52},{24,56},{28,60},{32,0... | collective-permute-start | bytes 688136 | tf_op jit(solution)/shard_map/ppermute | solution.py:29
  40.1 13.5 %collective-permute-start.13 = (f32[448,128]{1,0:T(8,128)S(1)}, f32[448,128]{1,0:T(8,128)S(1)}, u32[]{:S(2)}, u32[]{:S(2)}) collective-permute-start(f32[448,128]{1,0:T(8,128)S(1)} %add_add_fusion.p0), channel_id=1, source_target_pairs={{0,96},{4,100},{8,104},{12,108},{16,112},{20,116},{24,120},{28,124... | collective-permute-start | bytes 688136 | tf_op jit(solution)/shard_map/ppermute | solution.py:29
  43.9 9.7 %collective-permute-start.12 = (f32[448,128]{1,0:T(8,128)S(1)}, f32[448,128]{1,0:T(8,128)S(1)}, u32[]{:S(2)}, u32[]{:S(2)}) collective-permute-start(f32[448,128]{1,0:T(8,128)S(1)} %add_add_fusion.p0), channel_id=1, source_target_pairs={{0,64},{4,68},{8,72},{12,76},{16,80},{20,84},{24,88},{28,92},{32,9... | collective-permute-start | bytes 688136 | tf_op jit(solution)/shard_map/ppermute | solution.py:29
  43.9 9.7 %collective-permute-start.11 = (f32[448,128]{1,0:T(8,128)S(1)}, f32[448,128]{1,0:T(8,128)S(1)}, u32[]{:S(2)}, u32[]{:S(2)}) collective-permute-start(f32[448,128]{1,0:T(8,128)S(1)} %add_add_fusion.p0), channel_id=1, source_target_pairs={{0,32},{4,36},{8,40},{12,44},{16,48},{20,52},{24,56},{28,60},{32,0... | collective-permute-start | bytes 688136 | tf_op jit(solution)/shard_map/ppermute | solution.py:29
  56.5 4.5 %collective-permute-start.15 = (f32[32,384]{1,0:T(8,128)S(1)}, f32[32,384]{1,0:T(8,128)S(1)}, u32[]{:S(2)}, u32[]{:S(2)}) collective-permute-start(f32[32,384]{1,0:T(8,128)S(1)} %get-tuple-element.33.a0), channel_id=1, source_target_pairs={{0,2},{1,3},{2,0},{3,1},{4,6},{5,7},{6,4},{7,5},{8,10},{9,11},{10,... | collective-permute-start | bytes 147464 | tf_op jit(solution)/shard_map/ppermute | solution.py:33
  63.1 4.8 %collective-permute-start.19 = (f32[32,384]{1,0:T(8,128)S(1)}, f32[32,384]{1,0:T(8,128)S(1)}, u32[]{:S(2)}, u32[]{:S(2)}) collective-permute-start(f32[32,384]{1,0:T(8,128)S(1)} %second_left.1.a0), channel_id=1, source_target_pairs={{0,24},{4,28},{8,16},{12,20},{16,8},{20,12},{24,0},{28,4},{32,56},... | collective-permute-start | bytes 147464 | tf_op jit(solution)/shard_map/ppermute | solution.py:25
  63.2 4.6 %collective-permute-start.18 = (f32[32,384]{1,0:T(8,128)S(1)}, f32[32,384]{1,0:T(8,128)S(1)}, u32[]{:S(2)}, u32[]{:S(2)}) collective-permute-start(f32[32,384]{1,0:T(8,128)S(1)} %second_left.1.a0), channel_id=1, source_target_pairs={{0,16},{4,20},{8,24},{12,28},{16,0},{20,4},{24,8},{28,12},{32,48},... | collective-permute-start | bytes 147464 | tf_op jit(solution)/shard_map/ppermute | solution.py:25
  63.2 5.1 %collective-permute-start.17 = (f32[32,384]{1,0:T(8,128)S(1)}, f32[32,384]{1,0:T(8,128)S(1)}, u32[]{:S(2)}, u32[]{:S(2)}) collective-permute-start(f32[32,384]{1,0:T(8,128)S(1)} %second_left.1.a0), channel_id=1, source_target_pairs={{0,8},{4,12},{8,0},{12,4},{16,24},{20,28},{24,16},{28,20},{32,40},... | collective-permute-start | bytes 147464 | tf_op jit(solution)/shard_map/ppermute | solution.py:25
  70.5 4.4 %collective-permute-start.22 = (f32[32,384]{1,0:T(8,128)S(1)}, f32[32,384]{1,0:T(8,128)S(1)}, u32[]{:S(2)}, u32[]{:S(2)}) collective-permute-start(f32[32,384]{1,0:T(8,128)S(1)} %get-tuple-element.36), channel_id=1, source_target_pairs={{0,3},{1,2},{2,1},{3,0},{4,7},{5,6},{6,5},{7,4},{8,11},{9,10},{10,... | collective-permute-start | bytes 147464 | tf_op jit(solution)/shard_map/ppermute | solution.py:33
  71.5 4.4 %collective-permute-start.21 = (f32[32,384]{1,0:T(8,128)S(1)}, f32[32,384]{1,0:T(8,128)S(1)}, u32[]{:S(2)}, u32[]{:S(2)}) collective-permute-start(f32[32,384]{1,0:T(8,128)S(1)} %get-tuple-element.36), channel_id=1, source_target_pairs={{0,2},{1,3},{2,0},{3,1},{4,6},{5,7},{6,4},{7,5},{8,10},{9,11},{10,... | collective-permute-start | bytes 147464 | tf_op jit(solution)/shard_map/ppermute | solution.py:33
  76.0 14.5 %collective-permute-start.25 = (f32[32,384]{1,0:T(8,128)S(1)}, f32[32,384]{1,0:T(8,128)S(1)}, u32[]{:S(2)}, u32[]{:S(2)}) collective-permute-start(f32[32,384]{1,0:T(8,128)S(1)} %add_add_fusion.2.refs_0_.refs_3_), channel_id=1, source_target_pairs={{0,24},{4,28},{8,16},{12,20},{16,8},{20,12},{24,0},{28,4},{32,56},... | collective-permute-start | bytes 147464 | tf_op jit(solution)/shard_map/ppermute | solution.py:25
  77.9 13.1 %collective-permute-start.24 = (f32[32,384]{1,0:T(8,128)S(1)}, f32[32,384]{1,0:T(8,128)S(1)}, u32[]{:S(2)}, u32[]{:S(2)}) collective-permute-start(f32[32,384]{1,0:T(8,128)S(1)} %add_add_fusion.2.refs_0_.refs_3_), channel_id=1, source_target_pairs={{0,16},{4,20},{8,24},{12,28},{16,0},{20,4},{24,8},{28,12},{32,48},... | collective-permute-start | bytes 147464 | tf_op jit(solution)/shard_map/ppermute | solution.py:25
  78.8 12.3 %collective-permute-start.23 = (f32[32,384]{1,0:T(8,128)S(1)}, f32[32,384]{1,0:T(8,128)S(1)}, u32[]{:S(2)}, u32[]{:S(2)}) collective-permute-start(f32[32,384]{1,0:T(8,128)S(1)} %add_add_fusion.2.refs_0_.refs_3_), channel_id=1, source_target_pairs={{0,8},{4,12},{8,0},{12,4},{16,24},{20,28},{24,16},{28,20},{32,40},... | collective-permute-start | bytes 147464 | tf_op jit(solution)/shard_map/ppermute | solution.py:25
  79.5 12.7 %collective-permute-start.26 = (f32[32,384]{1,0:T(8,128)S(1)}, f32[32,384]{1,0:T(8,128)S(1)}, u32[]{:S(2)}, u32[]{:S(2)}) collective-permute-start(f32[32,384]{1,0:T(8,128)S(1)} %add_add_fusion.2.refs_0_.refs_3_), channel_id=1, source_target_pairs={{0,4},{4,0},{8,12},{12,8},{16,20},{20,16},{24,28},{28,24},{32,36},... | collective-permute-start | bytes 147464 | tf_op jit(solution)/shard_map/ppermute | solution.py:21
  (10 other events, 31.4 us)

commit v5 on v4

--- a/solution.py
+++ b/solution.py
@@ -212,8 +212,8 @@
     out_ref[...] = to_right(left, high_ref[...], low_ref[...])
 
 
-def solve_kernel(packed_ref, left_ref, w_hbm, m_hbm, out_ref, w_out, m_out, sems, *, scale):
-    one = pltpu.make_async_copy(w_hbm, w_out, sems.at[0])
+def solve_kernel(where, packed_ref, left_ref, w_hbm, m_hbm, out_ref, w_out, m_out, sems, *, scale):
+    one = pltpu.make_async_copy(w_hbm.at[where[0]], w_out, sems.at[0])
     two = pltpu.make_async_copy(m_hbm, m_out, sems.at[1])
     one.start()
     two.start()
@@ -224,15 +224,20 @@
     two.wait()
 
 
-def final_kernel(where, own, other, g0, g1, g2, g3, h0, h1, h2, h3, l_own, l_other, w_ref, m_ref,
-                 e_hbm, w_hbm, m_hbm, stage, e_buf, w_buf, m_buf, sems, *, blocks):
+def final_kernel(where, own, other, g0, g1, g2, g3, h0, h1, h2, h3, l_own, l_other, w_ref, m_ref, w_in,
+                 e_hbm, w_hbm, m_hbm, stage, e_buf, w_buf, m_buf, w_rest, sems, w_sem, *, blocks):
     core, y = where[0], where[1]
     size = own.shape[0] // blocks
     side = lanes((32, 128)) < 64
+    fetch = pltpu.make_async_copy(w_in.at[1 - core], w_rest, w_sem)
+    fetch.start()
     copies = []
     for slot, (full, left_ref, quarters) in enumerate(
             ((own, l_own, (g0, g1, g2, g3)), (other, l_other, (h0, h1, h2, h3)))):
         mat = core ^ slot
+        held = (w_ref, w_rest)[slot]
+        if slot == 1:
+            fetch.wait()
         for k, quarter in enumerate(quarters):
             stage[y ^ k] = quarter[...]
         tiles = []
@@ -250,7 +255,7 @@
             e_buf[slot, rows] = full[rows] - part
             moved = 0.9 * m_ref[mat, rows] + part
             m_buf[slot, rows] = moved
-            w_buf[slot, rows] = w_ref[mat, rows] - 0.1 * moved
+            w_buf[slot, rows] = held[rows] - 0.1 * moved
             for j, (buf, hbm) in enumerate(((e_buf, e_hbm), (m_buf, m_hbm), (w_buf, w_hbm))):
                 copies.append(pltpu.make_async_copy(buf.at[slot, rows], hbm.at[mat, rows], sems.at[slot, block, j]))
                 copies[-1].start()
@@ -306,19 +311,19 @@
     )(which, *inputs)
 
 
-def finish(where, own, other, rights, l_own, l_other, weights, momentum):
+def finish(where, own, other, rights, l_own, l_other, own_weights, momentum, weights):
     blocks = 4
     hbm = pl.BlockSpec(memory_space=pltpu.HBM)
     return pl.pallas_call(
         lambda *refs: final_kernel(*refs, blocks=blocks),
         out_shape=[shaped(weights.shape)] * 3,
-        in_specs=[SM] + [VM] * 14,
+        in_specs=[SM] + [VM] * 14 + [hbm],
         out_specs=[hbm] * 3,
         scratch_shapes=[pltpu.VMEM((4, 32, 384), F32)] + [pltpu.VMEM(weights.shape, F32)] * 3
-        + [pltpu.SemaphoreType.DMA((2, blocks, 3))],
+        + [pltpu.VMEM(weights.shape[1:], F32), pltpu.SemaphoreType.DMA((2, blocks, 3)), pltpu.SemaphoreType.DMA(())],
         compiler_params=limit(24),
         name="finish",
-    )(where, own, other, *rights, l_own, l_other, weights, momentum)
+    )(where, own, other, *rights, l_own, l_other, own_weights, momentum, weights)
 
 
 def body(acts, cots, errors, weights, momentum, start_q, vec_grads, vec_weights, vec_momentum):
@@ -352,11 +357,13 @@
     packed = add4(fan(packed, swap_x))
     rights = fan(packed, swap_y)
     rights += [swap_core(right) for right in rights]
-    held = pltpu.VMEM(weights.shape, F32)
-    l_own, weights, momentum = call(
-        lambda *refs: solve_kernel(*refs, scale=1.0 / replicas), (rights[0], left, in_hbm(weights), in_hbm(momentum)),
-        [shaped((32, 384)), held, held], [VM, VM, hbm, hbm], [pltpu.SemaphoreType.DMA((2,))], name="solve")
-    new_errors, new_weights, new_momentum = finish(where, own, other, rights, l_own, swap_core(l_own), weights, momentum)
+    weights = in_hbm(weights)
+    l_own, own_weights, momentum = call(
+        lambda *refs: solve_kernel(*refs, scale=1.0 / replicas), (where, rights[0], left, weights, in_hbm(momentum)),
+        [shaped((32, 384)), pltpu.VMEM(weights.shape[1:], F32), pltpu.VMEM(weights.shape, F32)], [SM, VM, VM, hbm, hbm],
+        [pltpu.SemaphoreType.DMA((2,))], name="solve")
+    new_errors, new_weights, new_momentum = finish(where, own, other, rights, l_own, swap_core(l_own), own_weights, momentum,
+                                                   weights)
     vec_moved = 0.9 * vec_momentum + vec_sum[:20, 64:].reshape(4, 320) / replicas
     return (new_errors[None], new_weights, new_momentum, vec_weights - 0.1 * vec_moved, vec_moved)
 

time: 97.5 us -> 100 us (1.026)
  Pallas kernels: 23.5 us -> 26.2 us
    pallas_call x1, Pallas kernels: 4.81 us -> 6.63 us  [finish(): pl.pallas_call(lambda *refs: final_kernel(*refs, blocks=blocks), out_shap...]
  transfers between devices with their start and end apart: 31 -> 31, of which waited for: 13 -> 13; matrix products, arithmetic and copies ran while one was open for 1% -> 1% of each run, Pallas kernels for 7% -> 8%
where the time goes in v5:
time: 100 us
  starting transfers between devices  42.9 us (43%)
  waiting for transfers between devices  29 us (29%)
  Pallas kernels  26.2 us (26%)
    ppermute x12, starting transfers between devices, swap_y(): return lax.ppermute(value, 'replica', [(r, r ^ k << 1) for r in range(32)])  16.3 us
    ppermute x12, waiting for transfers between devices, swap_y(): return lax.ppermute(value, 'replica', [(r, r ^ k << 1) for r in range(32)])  14 us
    pallas_call x5, Pallas kernels, call(): pl.pallas_call(kernel, out_shape=outs, in_specs=specs, out_specs=[VM] * l...  11.2 us
    ppermute x7, starting transfers between devices, swap_core(): return lax.ppermute(value, 'replica', CORE)  10.7 us
    ppermute x6, waiting for transfers between devices, swap_z(): return lax.ppermute(value, 'replica', [(r, r ^ k << 3) for r in range(32)])  9.03 us
    ppermute x6, starting transfers between devices, swap_z(): return lax.ppermute(value, 'replica', [(r, r ^ k << 3) for r in range(32)])  9.03 us
    pallas_call x2, Pallas kernels, gradients(): pl.pallas_call(lambda *refs: grad_kernel(*refs, scale=scale, step=step, a...  8.38 us
    ppermute x6, starting transfers between devices, swap_x(): return lax.ppermute(value, 'shard', [(s, s ^ k) for s in range(4)])  6.85 us
  transfers between devices with their start and end apart: 31, of which 13 were waited for; matrix products, arithmetic and copies ran while one was open for 1% of the time, Pallas kernels for 8%

profile of v5, /device:TPU:1, one launch (start us, length us, event | category | flops | bytes accessed | tf_op | source)
XLA Modules:
  0.0 100.0 jit_solution(7432688125837602860)
XLA Ops:
  0.6 4.2 %grad_other.1.refs_2_ = f32[320,1280]{1,0:T(8,128)S(1)} custom-call(s32[1]{0:T(128)S(6)} %sub.6.refs_0_, bf16[2,320,2048]{2,1,0:T(8,128)(2,1)} %bitcast.10, bf16[2,2048,1280]{2,1,0:T(8,128)(2,1)} %refs_2_.3, f32[2,320,1280]{2,1,0:T(8,128)} %bitcast.8), custom_call_target="tpu_custom_call" | custom-call | tf_op jit(solution)/shard_map/grad_other/pallas_call | solution.py:296
  4.8 1.5 %collective-permute-start = (f32[320,1280]{1,0:T(8,128)S(1)}, f32[320,1280]{1,0:T(8,128)}, u32[]{:S(2)}, u32[]{:S(2)}) collective-permute-start(f32[320,1280]{1,0:T(8,128)S(1)} %grad_other.1.refs_2_), channel_id=1, source_target_pairs={{0,4},{4,0},{8,12},{12,8},{16,20},{20,16},{24,28},{28,24},{32,36},... | collective-permute-start | bytes 4915208 | tf_op jit(solution)/shard_map/ppermute | solution.py:21
  6.5 4.2 %grad_own.1.a_ref.refs_1_ = f32[320,1280]{1,0:T(8,128)S(1)} custom-call(s32[1]{0:T(128)} %bitcast.refs_0_, bf16[2,320,2048]{2,1,0:T(8,128)(2,1)} %bitcast.11, bf16[2,2048,1280]{2,1,0:T(8,128)(2,1)} %refs_2_.3, f32[2,320,1280]{2,1,0:T(8,128)} %bitcast.9), custom_call_target="tpu_custom_call" | custom-call | tf_op jit(solution)/shard_map/grad_own/pallas_call | solution.py:296
  10.9 2.9 %route.1 = (f32[448,128]{1,0:T(8,128)S(1)}, f32[448,128]{1,0:T(8,128)S(1)}, f32[448,128]{1,0:T(8,128)S(1)}, f32[448,128]{1,0:T(8,128)S(1)}, f32[448,128]{1,0:T(8...) custom-call(s32[2]{0:T(128)S(1)} %pad_add_fusion.where.refs_0_, ...), custom_call_target="tpu_custom_call" | custom-call | tf_op jit(solution)/shard_map/route/pallas_call | solution.py:280
  13.8 1.5 %collective-permute-start.2 = (f32[448,128]{1,0:T(8,128)S(1)}, f32[448,128]{1,0:T(8,128)S(1)}, u32[]{:S(2)}, u32[]{:S(2)}) collective-permute-start(f32[448,128]{1,0:T(8,128)S(1)} %get-tuple-element.26), channel_id=1, source_target_pairs={{0,8},{4,12},{8,0},{12,4},{16,24},{20,28},{24,16},{28,20},{32,40},... | collective-permute-start | bytes 688136 | tf_op jit(solution)/shard_map/ppermute | solution.py:25
  15.3 2.6 %collective-permute-start.3 = (f32[448,128]{1,0:T(8,128)S(1)}, f32[448,128]{1,0:T(8,128)S(1)}, u32[]{:S(2)}, u32[]{:S(2)}) collective-permute-start(f32[448,128]{1,0:T(8,128)S(1)} %get-tuple-element.27), channel_id=1, source_target_pairs={{0,16},{4,20},{8,24},{12,28},{16,0},{20,4},{24,8},{28,12},{32,48},... | collective-permute-start | bytes 688136 | tf_op jit(solution)/shard_map/ppermute | solution.py:25
  17.9 3.8 %collective-permute-start.9 = (f32[448,128]{1,0:T(8,128)S(1)}, f32[448,128]{1,0:T(8,128)S(1)}, u32[]{:S(2)}, u32[]{:S(2)}) collective-permute-start(f32[448,128]{1,0:T(8,128)S(1)} %get-tuple-element.31), channel_id=1, source_target_pairs={{0,16},{4,20},{8,24},{12,28},{16,0},{20,4},{24,8},{28,12},{32,48},... | collective-permute-start | bytes 688136 | tf_op jit(solution)/shard_map/ppermute | solution.py:25
  21.8 1.7 %collective-permute-start.10 = (f32[448,128]{1,0:T(8,128)S(1)}, f32[448,128]{1,0:T(8,128)S(1)}, u32[]{:S(2)}, u32[]{:S(2)}) collective-permute-start(f32[448,128]{1,0:T(8,128)S(1)} %get-tuple-element.32), channel_id=1, source_target_pairs={{0,24},{4,28},{8,16},{12,20},{16,8},{20,12},{24,0},{28,4},{32,56},... | collective-permute-start | bytes 688136 | tf_op jit(solution)/shard_map/ppermute | solution.py:25
  23.5 4.7 %collective-permute-done.3 = f32[448,128]{1,0:T(8,128)S(1)} collective-permute-done((f32[448,128]{1,0:T(8,128)S(1)}, f32[448,128]{1,0:T(8,128)S(1)}, u32[]{:S(2)}, u32[]{:S(2)}) %collective-permute-start.3) | collective-permute-done | bytes 229408 | tf_op jit(solution)/shard_map/ppermute | solution.py:25
  28.2 2.0 %collective-permute-done.4 = f32[448,128]{1,0:T(8,128)S(1)} collective-permute-done((f32[448,128]{1,0:T(8,128)S(1)}, f32[448,128]{1,0:T(8,128)S(1)}, u32[]{:S(2)}, u32[]{:S(2)}) %collective-permute-start.4) | collective-permute-done | bytes 229408 | tf_op jit(solution)/shard_map/ppermute | solution.py:25
  30.2 3.8 %collective-permute-start.7 = (f32[448,128]{1,0:T(8,128)S(1)}, f32[448,128]{1,0:T(8,128)S(1)}, u32[]{:S(2)}, u32[]{:S(2)}) collective-permute-start(f32[448,128]{1,0:T(8,128)S(1)} %add_add_fusion.1.m0), channel_id=1, source_target_pairs={{0,96},{4,100},{8,104},{12,108},{16,112},{20,116},{24,120},{28,124... | collective-permute-start | bytes 688136 | tf_op jit(solution)/shard_map/ppermute | solution.py:29
  34.7 3.3 %collective-permute-done.9 = f32[448,128]{1,0:T(8,128)S(1)} collective-permute-done((f32[448,128]{1,0:T(8,128)S(1)}, f32[448,128]{1,0:T(8,128)S(1)}, u32[]{:S(2)}, u32[]{:S(2)}) %collective-permute-start.9) | collective-permute-done | bytes 229408 | tf_op jit(solution)/shard_map/ppermute | solution.py:25
  38.0 2.0 %collective-permute-done.10 = f32[448,128]{1,0:T(8,128)S(1)} collective-permute-done((f32[448,128]{1,0:T(8,128)S(1)}, f32[448,128]{1,0:T(8,128)S(1)}, u32[]{:S(2)}, u32[]{:S(2)}) %collective-permute-start.10) | collective-permute-done | bytes 229408 | tf_op jit(solution)/shard_map/ppermute | solution.py:25
  40.1 3.8 %collective-permute-start.13 = (f32[448,128]{1,0:T(8,128)S(1)}, f32[448,128]{1,0:T(8,128)S(1)}, u32[]{:S(2)}, u32[]{:S(2)}) collective-permute-start(f32[448,128]{1,0:T(8,128)S(1)} %add_add_fusion.p0), channel_id=1, source_target_pairs={{0,96},{4,100},{8,104},{12,108},{16,112},{20,116},{24,120},{28,124... | collective-permute-start | bytes 688136 | tf_op jit(solution)/shard_map/ppermute | solution.py:29
  44.6 9.0 %collective-permute-done.13.p3 = f32[448,128]{1,0:T(8,128)S(1)} collective-permute-done((f32[448,128]{1,0:T(8,128)S(1)}, f32[448,128]{1,0:T(8,128)S(1)}, u32[]{:S(2)}, u32[]{:S(2)}) %collective-permute-start.13) | collective-permute-done | bytes 229408 | tf_op jit(solution)/shard_map/ppermute | solution.py:29
  54.0 2.6 %collective-permute-start.16 = (f32[32,384]{1,0:T(8,128)S(1)}, f32[32,384]{1,0:T(8,128)S(1)}, u32[]{:S(2)}, u32[]{:S(2)}) collective-permute-start(f32[32,384]{1,0:T(8,128)S(1)} %get-tuple-element.33.a0), channel_id=1, source_target_pairs={{0,3},{1,2},{2,1},{3,0},{4,7},{5,6},{6,5},{7,4},{8,11},{9,10},{10,... | collective-permute-start | bytes 147464 | tf_op jit(solution)/shard_map/ppermute | solution.py:33
  58.2 2.8 %collective-permute-done.15.a2 = f32[32,384]{1,0:T(8,128)S(1)} collective-permute-done((f32[32,384]{1,0:T(8,128)S(1)}, f32[32,384]{1,0:T(8,128)S(1)}, u32[]{:S(2)}, u32[]{:S(2)}) %collective-permute-start.15) | collective-permute-done | bytes 49184 | tf_op jit(solution)/shard_map/ppermute | solution.py:33
  61.0 2.1 %second_left.1.a0 = f32[32,384]{1,0:T(8,128)S(1)} custom-call(f32[32,384]{1,0:T(8,128)S(1)} %get-tuple-element.33.a0, f32[32,384]{1,0:T(8,128)S(1)} %collective-permute-done.14.a1, f32[32,384]{1,0:T(8,128)S(1)} %collective-permute-done.15.a2, f32[32,384]{1,0:T(8,128)S(1)} %collective-permute-done.16.a3, bf16[384,384]{1,0:T(8,128)(2,1)S(1)} %get-tuple-element.34.high_ref, ...), custom_call_target="tpu_custom_call" | custom-call | tf_op jit(solution)/shard_map/second_left/pallas_call | solution.py:280
  63.2 3.1 %collective-permute-start.17 = (f32[32,384]{1,0:T(8,128)S(1)}, f32[32,384]{1,0:T(8,128)S(1)}, u32[]{:S(2)}, u32[]{:S(2)}) collective-permute-start(f32[32,384]{1,0:T(8,128)S(1)} %second_left.1.a0), channel_id=1, source_target_pairs={{0,8},{4,12},{8,0},{12,4},{16,24},{20,28},{24,16},{28,20},{32,40},... | collective-permute-start | bytes 147464 | tf_op jit(solution)/shard_map/ppermute | solution.py:25
  68.4 2.1 %second_right.1 = (f32[32,384]{1,0:T(8,128)S(1)}, f32[32,384]{1,0:T(8,128)S(1)}) custom-call(f32[32,384]{1,0:T(8,128)S(1)} %second_left.1.a0, f32[32,384]{1,0:T(8,128)S(1)} %collective-permute-done.17.a1, f32[32,384]{1,0:T(8,128)S(1)} %collective-permute-done.18.a2, f32[32,384]{1,0:T(8,128)S(1)} %collective-permute-done.19.a3, ...), custom_call_target="tpu_custom_call" | custom-call | tf_op jit(solution)/shard_map/second_right/pallas_call | solution.py:280
  76.0 2.0 %collective-permute-start.25 = (f32[32,384]{1,0:T(8,128)S(1)}, f32[32,384]{1,0:T(8,128)S(1)}, u32[]{:S(2)}, u32[]{:S(2)}) collective-permute-start(f32[32,384]{1,0:T(8,128)S(1)} %add_add_fusion.2.refs_1_.refs_3_), channel_id=1, source_target_pairs={{0,24},{4,28},{8,16},{12,20},{16,8},{20,12},{24,0},{28,4},{32,56},... | collective-permute-start | bytes 147464 | tf_op jit(solution)/shard_map/ppermute | solution.py:25
  79.5 8.0 %collective-permute-start.26 = (f32[32,384]{1,0:T(8,128)S(1)}, f32[32,384]{1,0:T(8,128)S(1)}, u32[]{:S(2)}, u32[]{:S(2)}) collective-permute-start(f32[32,384]{1,0:T(8,128)S(1)} %add_add_fusion.2.refs_1_.refs_3_), channel_id=1, source_target_pairs={{0,4},{4,0},{8,12},{12,8},{16,20},{20,16},{24,28},{28,24},{32,36},... | collective-permute-start | bytes 147464 | tf_op jit(solution)/shard_map/ppermute | solution.py:21
  87.5 3.8 %solve.1 = (f32[32,384]{1,0:T(8,128)S(1)}, f32[320,1280]{1,0:T(8,128)S(1)}, f32[2,320,1280]{2,1,0:T(8,128)S(1)}) custom-call(s32[2]{0:T(128)S(1)} %pad_add_fusion.where.refs_0_, f32[32,384]{1,0:T(8,128)S(1)} %add_add_fusion.2.refs_1_.refs_3_, f32[32,384]{1,0:T(8,128)S(1)} %get-tuple-element.37.refs_2_, f32[2,320,1280]{2,1,0:T(8,128)} %refs_15_.1, ...), custom_call_target="tpu_custom_call" | custom-call | tf_op jit(solution)/shard_map/solve/pallas_call | solution.py:280
  93.2 6.6 %finish.1 = (f32[2,320,1280]{2,1,0:T(8,128)}, f32[2,320,1280]{2,1,0:T(8,128)}, f32[2,320,1280]{2,1,0:T(8,128)}) custom-call(s32[2]{0:T(128)S(1)} %pad_add_fusion.where.refs_0_, f32[320,1280]{1,0:T(8,128)S(1)} %grad_own.1.a_ref.refs_1_, f32[320,1280]{1,0:T(8,128)S(1)} %grad_other.1.refs_2_, f32[32,384]{1,0:T(8,128)S(1)} %add_add_fusion.2.refs_1_.refs_3_, ...), custom_call_target="tpu_custom_call" | custom-call | tf_op jit(solution)/shard_map/finish/pallas_call | solution.py:317
  (62 shorter events, 15.1 us)
Async XLA Ops:
  4.8 6.1 %collective-permute-start = (f32[320,1280]{1,0:T(8,128)S(1)}, f32[320,1280]{1,0:T(8,128)}, u32[]{:S(2)}, u32[]{:S(2)}) collective-permute-start(f32[320,1280]{1,0:T(8,128)S(1)} %grad_other.1.refs_2_), channel_id=1, source_target_pairs={{0,4},{4,0},{8,12},{12,8},{16,20},{20,16},{24,28},{28,24},{32,36},... | collective-permute-start | bytes 4915208 | tf_op jit(solution)/shard_map/ppermute | solution.py:21
  6.4 4.4 %collective-permute-start.1 = (f32[4,320]{1,0:T(4,128)S(1)}, f32[4,320]{1,0:T(4,128)S(1)}, u32[]{:S(2)}, u32[]{:S(2)}) collective-permute-start(f32[4,320]{1,0:T(4,128)S(1)} %bitcast.13), channel_id=1, source_target_pairs={{0,4},{4,0},{8,12},{12,8},{16,20},{20,16},{24,28},{28,24},{32,36},... | collective-permute-start | bytes 15368 | tf_op jit(solution)/shard_map/ppermute | solution.py:21
  13.8 7.9 %collective-permute-start.2 = (f32[448,128]{1,0:T(8,128)S(1)}, f32[448,128]{1,0:T(8,128)S(1)}, u32[]{:S(2)}, u32[]{:S(2)}) collective-permute-start(f32[448,128]{1,0:T(8,128)S(1)} %get-tuple-element.26), channel_id=1, source_target_pairs={{0,8},{4,12},{8,0},{12,4},{16,24},{20,28},{24,16},{28,20},{32,40},... | collective-permute-start | bytes 688136 | tf_op jit(solution)/shard_map/ppermute | solution.py:25
  15.3 12.9 %collective-permute-start.3 = (f32[448,128]{1,0:T(8,128)S(1)}, f32[448,128]{1,0:T(8,128)S(1)}, u32[]{:S(2)}, u32[]{:S(2)}) collective-permute-start(f32[448,128]{1,0:T(8,128)S(1)} %get-tuple-element.27), channel_id=1, source_target_pairs={{0,16},{4,20},{8,24},{12,28},{16,0},{20,4},{24,8},{28,12},{32,48},... | collective-permute-start | bytes 688136 | tf_op jit(solution)/shard_map/ppermute | solution.py:25
  17.9 12.3 %collective-permute-start.4 = (f32[448,128]{1,0:T(8,128)S(1)}, f32[448,128]{1,0:T(8,128)S(1)}, u32[]{:S(2)}, u32[]{:S(2)}) collective-permute-start(f32[448,128]{1,0:T(8,128)S(1)} %get-tuple-element.28), channel_id=1, source_target_pairs={{0,24},{4,28},{8,16},{12,20},{16,8},{20,12},{24,0},{28,4},{32,56},... | collective-permute-start | bytes 688136 | tf_op jit(solution)/shard_map/ppermute | solution.py:25
  17.9 16.2 %collective-permute-start.8 = (f32[448,128]{1,0:T(8,128)S(1)}, f32[448,128]{1,0:T(8,128)S(1)}, u32[]{:S(2)}, u32[]{:S(2)}) collective-permute-start(f32[448,128]{1,0:T(8,128)S(1)} %get-tuple-element.30), channel_id=1, source_target_pairs={{0,8},{4,12},{8,0},{12,4},{16,24},{20,28},{24,16},{28,20},{32,40},... | collective-permute-start | bytes 688136 | tf_op jit(solution)/shard_map/ppermute | solution.py:25
  17.9 20.1 %collective-permute-start.9 = (f32[448,128]{1,0:T(8,128)S(1)}, f32[448,128]{1,0:T(8,128)S(1)}, u32[]{:S(2)}, u32[]{:S(2)}) collective-permute-start(f32[448,128]{1,0:T(8,128)S(1)} %get-tuple-element.31), channel_id=1, source_target_pairs={{0,16},{4,20},{8,24},{12,28},{16,0},{20,4},{24,8},{28,12},{32,48},... | collective-permute-start | bytes 688136 | tf_op jit(solution)/shard_map/ppermute | solution.py:25
  21.8 18.2 %collective-permute-start.10 = (f32[448,128]{1,0:T(8,128)S(1)}, f32[448,128]{1,0:T(8,128)S(1)}, u32[]{:S(2)}, u32[]{:S(2)}) collective-permute-start(f32[448,128]{1,0:T(8,128)S(1)} %get-tuple-element.32), channel_id=1, source_target_pairs={{0,24},{4,28},{8,16},{12,20},{16,8},{20,12},{24,0},{28,4},{32,56},... | collective-permute-start | bytes 688136 | tf_op jit(solution)/shard_map/ppermute | solution.py:25
  30.2 13.7 %collective-permute-start.7 = (f32[448,128]{1,0:T(8,128)S(1)}, f32[448,128]{1,0:T(8,128)S(1)}, u32[]{:S(2)}, u32[]{:S(2)}) collective-permute-start(f32[448,128]{1,0:T(8,128)S(1)} %add_add_fusion.1.m0), channel_id=1, source_target_pairs={{0,96},{4,100},{8,104},{12,108},{16,112},{20,116},{24,120},{28,124... | collective-permute-start | bytes 688136 | tf_op jit(solution)/shard_map/ppermute | solution.py:29
  34.1 10.5 %collective-permute-start.6 = (f32[448,128]{1,0:T(8,128)S(1)}, f32[448,128]{1,0:T(8,128)S(1)}, u32[]{:S(2)}, u32[]{:S(2)}) collective-permute-start(f32[448,128]{1,0:T(8,128)S(1)} %add_add_fusion.1.m0), channel_id=1, source_target_pairs={{0,64},{4,68},{8,72},{12,76},{16,80},{20,84},{24,88},{28,92},{32,9... | collective-permute-start | bytes 688136 | tf_op jit(solution)/shard_map/ppermute | solution.py:29
  34.1 10.5 %collective-permute-start.5 = (f32[448,128]{1,0:T(8,128)S(1)}, f32[448,128]{1,0:T(8,128)S(1)}, u32[]{:S(2)}, u32[]{:S(2)}) collective-permute-start(f32[448,128]{1,0:T(8,128)S(1)} %add_add_fusion.1.m0), channel_id=1, source_target_pairs={{0,32},{4,36},{8,40},{12,44},{16,48},{20,52},{24,56},{28,60},{32,0... | collective-permute-start | bytes 688136 | tf_op jit(solution)/shard_map/ppermute | solution.py:29
  40.1 13.5 %collective-permute-start.13 = (f32[448,128]{1,0:T(8,128)S(1)}, f32[448,128]{1,0:T(8,128)S(1)}, u32[]{:S(2)}, u32[]{:S(2)}) collective-permute-start(f32[448,128]{1,0:T(8,128)S(1)} %add_add_fusion.p0), channel_id=1, source_target_pairs={{0,96},{4,100},{8,104},{12,108},{16,112},{20,116},{24,120},{28,124... | collective-permute-start | bytes 688136 | tf_op jit(solution)/shard_map/ppermute | solution.py:29
  43.9 9.7 %collective-permute-start.12 = (f32[448,128]{1,0:T(8,128)S(1)}, f32[448,128]{1,0:T(8,128)S(1)}, u32[]{:S(2)}, u32[]{:S(2)}) collective-permute-start(f32[448,128]{1,0:T(8,128)S(1)} %add_add_fusion.p0), channel_id=1, source_target_pairs={{0,64},{4,68},{8,72},{12,76},{16,80},{20,84},{24,88},{28,92},{32,9... | collective-permute-start | bytes 688136 | tf_op jit(solution)/shard_map/ppermute | solution.py:29
  43.9 9.7 %collective-permute-start.11 = (f32[448,128]{1,0:T(8,128)S(1)}, f32[448,128]{1,0:T(8,128)S(1)}, u32[]{:S(2)}, u32[]{:S(2)}) collective-permute-start(f32[448,128]{1,0:T(8,128)S(1)} %add_add_fusion.p0), channel_id=1, source_target_pairs={{0,32},{4,36},{8,40},{12,44},{16,48},{20,52},{24,56},{28,60},{32,0... | collective-permute-start | bytes 688136 | tf_op jit(solution)/shard_map/ppermute | solution.py:29
  56.5 4.5 %collective-permute-start.15 = (f32[32,384]{1,0:T(8,128)S(1)}, f32[32,384]{1,0:T(8,128)S(1)}, u32[]{:S(2)}, u32[]{:S(2)}) collective-permute-start(f32[32,384]{1,0:T(8,128)S(1)} %get-tuple-element.33.a0), channel_id=1, source_target_pairs={{0,2},{1,3},{2,0},{3,1},{4,6},{5,7},{6,4},{7,5},{8,10},{9,11},{10,... | collective-permute-start | bytes 147464 | tf_op jit(solution)/shard_map/ppermute | solution.py:33
  63.1 4.8 %collective-permute-start.19 = (f32[32,384]{1,0:T(8,128)S(1)}, f32[32,384]{1,0:T(8,128)S(1)}, u32[]{:S(2)}, u32[]{:S(2)}) collective-permute-start(f32[32,384]{1,0:T(8,128)S(1)} %second_left.1.a0), channel_id=1, source_target_pairs={{0,24},{4,28},{8,16},{12,20},{16,8},{20,12},{24,0},{28,4},{32,56},... | collective-permute-start | bytes 147464 | tf_op jit(solution)/shard_map/ppermute | solution.py:25
  63.2 4.6 %collective-permute-start.18 = (f32[32,384]{1,0:T(8,128)S(1)}, f32[32,384]{1,0:T(8,128)S(1)}, u32[]{:S(2)}, u32[]{:S(2)}) collective-permute-start(f32[32,384]{1,0:T(8,128)S(1)} %second_left.1.a0), channel_id=1, source_target_pairs={{0,16},{4,20},{8,24},{12,28},{16,0},{20,4},{24,8},{28,12},{32,48},... | collective-permute-start | bytes 147464 | tf_op jit(solution)/shard_map/ppermute | solution.py:25
  63.2 5.1 %collective-permute-start.17 = (f32[32,384]{1,0:T(8,128)S(1)}, f32[32,384]{1,0:T(8,128)S(1)}, u32[]{:S(2)}, u32[]{:S(2)}) collective-permute-start(f32[32,384]{1,0:T(8,128)S(1)} %second_left.1.a0), channel_id=1, source_target_pairs={{0,8},{4,12},{8,0},{12,4},{16,24},{20,28},{24,16},{28,20},{32,40},... | collective-permute-start | bytes 147464 | tf_op jit(solution)/shard_map/ppermute | solution.py:25
  70.5 4.4 %collective-permute-start.22 = (f32[32,384]{1,0:T(8,128)S(1)}, f32[32,384]{1,0:T(8,128)S(1)}, u32[]{:S(2)}, u32[]{:S(2)}) collective-permute-start(f32[32,384]{1,0:T(8,128)S(1)} %get-tuple-element.36), channel_id=1, source_target_pairs={{0,3},{1,2},{2,1},{3,0},{4,7},{5,6},{6,5},{7,4},{8,11},{9,10},{10,... | collective-permute-start | bytes 147464 | tf_op jit(solution)/shard_map/ppermute | solution.py:33
  71.5 4.4 %collective-permute-start.21 = (f32[32,384]{1,0:T(8,128)S(1)}, f32[32,384]{1,0:T(8,128)S(1)}, u32[]{:S(2)}, u32[]{:S(2)}) collective-permute-start(f32[32,384]{1,0:T(8,128)S(1)} %get-tuple-element.36), channel_id=1, source_target_pairs={{0,2},{1,3},{2,0},{3,1},{4,6},{5,7},{6,4},{7,5},{8,10},{9,11},{10,... | collective-permute-start | bytes 147464 | tf_op jit(solution)/shard_map/ppermute | solution.py:33
  76.0 15.4 %collective-permute-start.25 = (f32[32,384]{1,0:T(8,128)S(1)}, f32[32,384]{1,0:T(8,128)S(1)}, u32[]{:S(2)}, u32[]{:S(2)}) collective-permute-start(f32[32,384]{1,0:T(8,128)S(1)} %add_add_fusion.2.refs_1_.refs_3_), channel_id=1, source_target_pairs={{0,24},{4,28},{8,16},{12,20},{16,8},{20,12},{24,0},{28,4},{32,56},... | collective-permute-start | bytes 147464 | tf_op jit(solution)/shard_map/ppermute | solution.py:25
  77.9 13.9 %collective-permute-start.24 = (f32[32,384]{1,0:T(8,128)S(1)}, f32[32,384]{1,0:T(8,128)S(1)}, u32[]{:S(2)}, u32[]{:S(2)}) collective-permute-start(f32[32,384]{1,0:T(8,128)S(1)} %add_add_fusion.2.refs_1_.refs_3_), channel_id=1, source_target_pairs={{0,16},{4,20},{8,24},{12,28},{16,0},{20,4},{24,8},{28,12},{32,48},... | collective-permute-start | bytes 147464 | tf_op jit(solution)/shard_map/ppermute | solution.py:25
  78.8 13.1 %collective-permute-start.23 = (f32[32,384]{1,0:T(8,128)S(1)}, f32[32,384]{1,0:T(8,128)S(1)}, u32[]{:S(2)}, u32[]{:S(2)}) collective-permute-start(f32[32,384]{1,0:T(8,128)S(1)} %add_add_fusion.2.refs_1_.refs_3_), channel_id=1, source_target_pairs={{0,8},{4,12},{8,0},{12,4},{16,24},{20,28},{24,16},{28,20},{32,40},... | collective-permute-start | bytes 147464 | tf_op jit(solution)/shard_map/ppermute | solution.py:25
  79.5 13.5 %collective-permute-start.26 = (f32[32,384]{1,0:T(8,128)S(1)}, f32[32,384]{1,0:T(8,128)S(1)}, u32[]{:S(2)}, u32[]{:S(2)}) collective-permute-start(f32[32,384]{1,0:T(8,128)S(1)} %add_add_fusion.2.refs_1_.refs_3_), channel_id=1, source_target_pairs={{0,4},{4,0},{8,12},{12,8},{16,20},{20,16},{24,28},{28,24},{32,36},... | collective-permute-start | bytes 147464 | tf_op jit(solution)/shard_map/ppermute | solution.py:21
  (10 other events, 33.0 us)
